TPU v7x, 256 devices: a whole 4x4x8 slice. The times are simulated.
256 devices in a mesh: row: 16 (over y, x), col: 16 (over z, core).
Axes of the slice: x: 4, y: 4, z: 8, core: 2. Of those that a mesh axis runs over, the one named last changes fastest.
Arguments:
- excitation: float32 [16, 16, 2, 32, 1024], P('row', 'col'), may hold values from -6 to 6
- shift_real: float32 [16, 16, 1024], P('row', 'col'), may hold values from 6 to 10
- shift_imag: float32 [16, 16, 1024], P('row', 'col'), may hold values from 1.5 to 4
- local_tiles: bfloat16 [16, 16, 8, 4, 128, 128], P('row', 'col'), may hold values from -0.25 to 0.25
- tile_columns: int32 [16, 16, 8, 4], P('row', 'col'), may hold values from 0 to 7
- coupling: bfloat16 [16, 16, 4, 128, 128], P('row', 'col'), may hold values from -0.5 to 0.5
- send_edges: int32 [16, 16, 4, 128], P('row', 'col'), may hold values from 0 to 1023
- receive_edges: int32 [16, 16, 4, 128], P('row', 'col'), may hold values from 0 to 1023
- local_modes: bfloat16 [16, 16, 96, 1024], P('row', 'col'), may hold values from -0.1875 to 0.1875
- coarse_inverse: bfloat16 [24576, 24576], P('row', 'col'), may hold values from -0.0546875 to 0.0546875
Outputs:
- solution: float32 [16, 16, 2, 32, 1024], P('row', 'col')
- residual: float32 [16, 16, 2, 32, 1024], P('row', 'col')
Inputs may be any that keep to these rules, and one draw needn't show every extreme that they name: `tile_columns`: tile column numbers of one subdomain's operator. `send_edges`: edge numbers within the sending subdomain; an edge may repeat. `receive_edges`: edge numbers within the receiving subdomain; an edge may repeat.
All inputs are finite; a program needn't handle non-finite values.
Results may differ from a plain program's by a relative error of at most 0.0003.
Values sent between devices are 32-bit elements; how exact they have to be, the bound alone decides.
No kernel may reach another device: no remote copies, remote signals or barrier semaphores. Data moves between devices by JAX's collectives and lax.ppermute only.
A program may use at most 64 MiB of HBM per device.

v0:
```python
import jax
import jax.numpy as jnp
from jax import lax
from jax.experimental import pallas as pl
from jax.experimental.pallas import tpu as pltpu
from jax.sharding import PartitionSpec as P

OUTER = 2
N = 16
ROWS = 64
NE = 1024
TILE = 128
MODES = 96
HALF = MODES // 2
F32 = jnp.float32
BF16 = jnp.bfloat16
NT = (((1,), (1,)), ((), ()))
TN = (((0,), (0,)), ((), ()))
NN = (((1,), (0,)), ((), ()))

VMEM = pl.BlockSpec(memory_space=pltpu.VMEM)
SMEM = pl.BlockSpec(memory_space=pltpu.SMEM)


def dot(a, b, dims):
    return lax.dot_general(a, b, dims, preferred_element_type=F32)


def split(x):
    high = x.astype(BF16).astype(F32)
    return high, x - high


def stacked(x):
    high, low = split(x)
    return jnp.concatenate([high.astype(BF16), low.astype(BF16)], axis=0)


def fold_rows(x):
    return x[:ROWS] + x[ROWS:]


def unpack_modes(x):
    high, low = split(x)
    left = lax.broadcasted_iota(jnp.int32, x.shape, 1) < ROWS
    first = jnp.where(left, high, pltpu.roll(low, ROWS, 1))
    second = jnp.where(left, pltpu.roll(high, ROWS, 1), low)
    return first.astype(BF16), second.astype(BF16)


def pack_modes(first, second):
    left = lax.broadcasted_iota(jnp.int32, first.shape, 1) < ROWS
    return jnp.where(left, first + pltpu.roll(first, ROWS, 1), second + pltpu.roll(second, ROWS, 1))


def project(residual, modes):
    wide = dot(modes, stacked(residual), NT)
    return pack_modes(wide[:HALF], wide[HALF:])


def relax(field, real_shift, imag_shift):
    modulus = real_shift * real_shift + imag_shift * imag_shift
    a, b = real_shift / modulus, imag_shift / modulus
    re, im = field[: ROWS // 2], field[ROWS // 2 :]
    return jnp.concatenate([a * re + b * im, a * im - b * re], axis=0)


def spread(packed, out):
    for k in range(N):
        out[k] = packed


def project_kernel(residual, modes, out):
    spread(project(residual[...], modes[...]), out)


def rim_kernel(order, send, modes, pick, rim_modes):
    edge = lax.broadcasted_iota(jnp.int32, (NE, TILE), 0)
    for slot in range(4):
        lanes = slice(slot * TILE, (slot + 1) * TILE)
        chosen = send[pl.ds(order[slot], 1), :]
        pick[:, lanes] = jnp.where(edge == chosen, 1.0, 0.0).astype(BF16)
    rim_modes[...] = dot(modes[...], pick[...], NN).astype(BF16)


def link_kernel(order, receive, coupling, link_high, link_low):
    edge = lax.broadcasted_iota(jnp.int32, (NE, TILE), 0)
    for slot in range(4):
        lanes = slice(slot * TILE, (slot + 1) * TILE)
        target = receive[pl.ds(order[slot], 1), :]
        place = jnp.where(edge == target, 1.0, 0.0).astype(BF16)
        link = dot(place, coupling[order[slot]], NN)
        high, low = split(link)
        link_high[:, lanes] = high.astype(BF16)
        link_low[:, lanes] = low.astype(BF16)


def coarse_kernel(gathered, inverse, out, column):
    for k in range(N):
        first, second = unpack_modes(gathered[k])
        column[k * MODES : k * MODES + HALF, :] = first
        column[k * MODES + HALF : (k + 1) * MODES, :] = second
    step = 4
    for k in range(0, N, step):
        wide = dot(inverse[k * MODES : (k + step) * MODES, :], column[...], NN)
        for m in range(step):
            out[k + m] = pack_modes(wide[m * MODES : m * MODES + HALF], wide[m * MODES + HALF : (m + 1) * MODES])


def start_kernel(parts, rim_modes, field, *rims):
    total = parts[0]
    for k in range(1, N):
        total = total + parts[k]
    first, second = unpack_modes(total)
    both = jnp.concatenate([first, second], axis=0)
    field[...] = both
    rim = fold_rows(dot(both, rim_modes[...], TN))
    for slot in range(4):
        rims[slot][...] = rim[:, slot * TILE : (slot + 1) * TILE]


def tile_product(columns, terms, tiles, scratch, out):
    for k in range(NE // TILE):
        scratch[k] = terms[:, k * TILE : (k + 1) * TILE]
    for t in range(NE // TILE):
        total = None
        for k in range(4):
            part = dot(scratch[columns[t, k]], tiles[t, k], NT)
            total = part if total is None else total + part
        out[:, t * TILE : (t + 1) * TILE] = fold_rows(total)


def first_tiles_kernel(columns, field, modes, tiles, out, scratch):
    update = fold_rows(dot(field[...], modes[...], TN))
    tile_product(columns, stacked(update), tiles, scratch, out)


def tiles_kernel(columns, update, tiles, out, scratch):
    tile_product(columns, stacked(update[...]), tiles, scratch, out)


def applied(inside, local, links, link_high, link_low):
    pieces = [jnp.where(inside[slot] > 0, links[slot][...], 0.0) for slot in range(4)]
    terms = stacked(jnp.concatenate(pieces, axis=1))
    image = local[...] + fold_rows(dot(terms, link_high[...], NT))
    return image + dot(terms[:ROWS], link_low[...], NT)


def sweep_kernel(inside, local, l0, l1, l2, l3, link_high, link_low, pick, residual, real_shift, imag_shift, image, update, *rims):
    value = applied(inside, local, (l0, l1, l2, l3), link_high, link_low)
    image[...] = value
    fresh = relax(residual[...] - value, real_shift[...], imag_shift[...])
    update[...] = fresh
    rim = fold_rows(dot(stacked(fresh), pick[...], NN))
    for slot in range(4):
        rims[slot][...] = rim[:, slot * TILE : (slot + 1) * TILE]


def close_kernel(inside, local, l0, l1, l2, l3, link_high, link_low, image, modes, residual, out):
    value = image[...] - applied(inside, local, (l0, l1, l2, l3), link_high, link_low)
    residual[...] = value
    spread(project(value, modes[...]), out)


def last_kernel(inside, local, l0, l1, l2, l3, link_high, link_low, image, update, before, residual, solution):
    residual[...] = image[...] - applied(inside, local, (l0, l1, l2, l3), link_high, link_low)
    solution[...] = before[...] + update[...]


def shape(dims, dtype=F32):
    return jax.ShapeDtypeStruct(dims, dtype)


def call(kernel, out_shape, in_specs, args, scratch=(), flops=0, name=None):
    outs = out_shape if isinstance(out_shape, (tuple, list)) else (out_shape,)
    moved = sum(a.size * a.dtype.itemsize for a in args) + sum(o.size * jnp.dtype(o.dtype).itemsize for o in outs)
    out_specs = [VMEM] * len(outs)
    return pl.pallas_call(
        kernel,
        out_shape=list(outs),
        in_specs=in_specs,
        out_specs=out_specs,
        scratch_shapes=list(scratch),
        compiler_params=pltpu.CompilerParams(vmem_limit_bytes=16 * 2**20),
        cost_estimate=pl.CostEstimate(flops=flops, bytes_accessed=moved, transcendentals=0),
        name=name,
    )(*args)


EVEN = [(k, k ^ 1) for k in range(N)]
ODD = [(k, (k + 1) % N) for k in range(1, N, 2)] + [((k + 1) % N, k) for k in range(1, N, 2)]


def on_device(
    excitation,
    shift_real,
    shift_imag,
    local_tiles,
    tile_columns,
    coupling,
    send_edges,
    receive_edges,
    local_modes,
    coarse_inverse,
):
    source = excitation.reshape(ROWS, NE)
    real_shift = shift_real.reshape(1, NE)
    imag_shift = shift_imag.reshape(1, NE)
    tiles = local_tiles[0, 0]
    columns = tile_columns[0, 0]
    links = coupling[0, 0]
    send = send_edges[0, 0]
    receive = receive_edges[0, 0]
    modes = local_modes[0, 0]

    row, col = lax.axis_index("row"), lax.axis_index("col")
    row_odd, col_odd = row % 2, col % 2
    order = jnp.stack([1 - row_odd, row_odd, 3 - col_odd, 2 + col_odd]).astype(jnp.int32)
    one = jnp.ones((), jnp.int32)
    row_in = jnp.where((row > 0) & (row < N - 1), 1, 0).astype(jnp.int32)
    col_in = jnp.where((col > 0) & (col < N - 1), 1, 0).astype(jnp.int32)
    inside = jnp.stack([one, row_in, one, col_in])

    rim_shapes = [shape((ROWS, TILE))] * 4
    field_shape = shape((ROWS, NE))
    spread_shape = shape((N, HALF, TILE))

    def exchange(rims):
        return [
            lax.ppermute(rims[0], "row", EVEN),
            lax.ppermute(rims[1], "row", ODD),
            lax.ppermute(rims[2], "col", EVEN),
            lax.ppermute(rims[3], "col", ODD),
        ]

    tile_scratch = [pltpu.VMEM((NE // TILE, 2 * ROWS, TILE), BF16)]
    tile_flops = 2 * 128 * NE * 512
    link_flops = 2 * 192 * 512 * NE

    (packed,) = call(project_kernel, spread_shape, [VMEM] * 2, [source, modes], name="project")
    pick, rim_modes = call(
        rim_kernel, [shape((NE, 4 * TILE), BF16), shape((MODES, 4 * TILE), BF16)], [SMEM, VMEM, VMEM], [order, send, modes], name="rim"
    )
    link_high, link_low = call(
        link_kernel, [shape((NE, 4 * TILE), BF16)] * 2, [SMEM, VMEM, VMEM], [order, receive, links], name="link"
    )

    residual = source
    solution = None
    for repeat in range(OUTER):
        gathered = lax.all_to_all(packed, "row", 0, 0)
        (partial_sums,) = call(
            coarse_kernel, spread_shape, [VMEM] * 2, [gathered, coarse_inverse],
            scratch=[pltpu.VMEM((N * MODES, TILE), BF16)], flops=2 * 1536 * 1536 * 128, name="coarse",
        )
        parts = lax.all_to_all(partial_sums, "col", 0, 0)
        field, *rims = call(
            start_kernel, [shape((MODES, TILE), BF16)] + rim_shapes, [VMEM] * 2, [parts, rim_modes], name="start"
        )
        arrived = exchange(rims)
        (local,) = call(
            first_tiles_kernel, field_shape, [SMEM] + [VMEM] * 3, [columns, field, modes, tiles],
            scratch=tile_scratch, flops=tile_flops, name="tiles0",
        )
        for sweep in range(2):
            image, update, *rims = call(
                sweep_kernel, [field_shape, field_shape] + rim_shapes, [SMEM] + [VMEM] * 11,
                [inside, local, *arrived, link_high, link_low, pick, residual, real_shift, imag_shift],
                flops=link_flops, name="sweep",
            )
            arrived = exchange(rims)
            (local,) = call(
                tiles_kernel, field_shape, [SMEM] + [VMEM] * 2, [columns, update, tiles],
                scratch=tile_scratch, flops=tile_flops, name="tiles",
            )
        common = [inside, local, *arrived, link_high, link_low, image]
        if repeat + 1 < OUTER:
            solution = update
            residual, packed = call(
                close_kernel, [field_shape, spread_shape], [SMEM] + [VMEM] * 9, common + [modes], flops=link_flops, name="close"
            )
        else:
            residual, solution = call(
                last_kernel, [field_shape, field_shape], [SMEM] + [VMEM] * 10, common + [update, solution], flops=link_flops, name="last"
            )
    whole = (1, 1, 2, ROWS // 2, NE)
    return solution.reshape(whole), residual.reshape(whole)


def solution(mesh):
    in_specs = (
        P("row", "col", None, None, None),
        P("row", "col", None),
        P("row", "col", None),
        P("row", "col", None, None, None, None),
        P("row", "col", None, None),
        P("row", "col", None, None, None),
        P("row", "col", None, None),
        P("row", "col", None, None),
        P("row", "col", None, None),
        P("row", "col"),
    )
    out_specs = (P("row", "col", None, None, None), P("row", "col", None, None, None))
    return jax.shard_map(on_device, mesh=mesh, in_specs=in_specs, out_specs=out_specs, check_vma=False)
```

profile of v0, /device:TPU:1, one launch (start us, length us, event | category | flops | bytes accessed | tf_op | source)
XLA Modules:
  0.0 138.6 jit_solution(17614381931065304337)
XLA Ops:
  2.9 16.7 %all_to_all.20.gathered = f32[16,48,128]{2,1,0:T(8,128)S(1)} all-to-all(f32[16,48,128]{2,1,0:T(8,128)S(1)} %project.1), channel_id=1, replica_groups=mesh['row'=16,'col'=16] {'row'}, dimensions={0} | all-to-all | bytes 786432 | tf_op jit(solution)/shard_map/all_to_all | solution.py:251
  19.7 2.3 %copy-done.1 = bf16[1536,1536]{1,0:T(8,128)(2,1)S(1)} copy-done((bf16[1536,1536]{1,0:T(8,128)(2,1)S(1)}, bf16[1536,1536]{1,0:T(8,128)(2,1)}, u32[]{:S(2)}) %copy-start.1) | copy-done | bytes 4718616
  22.0 2.3 %coarse.2 = f32[16,48,128]{2,1,0:T(8,128)} custom-call(f32[16,48,128]{2,1,0:T(8,128)S(1)} %all_to_all.20.gathered, bf16[1536,1536]{1,0:T(8,128)(2,1)S(1)} %copy-done.1), custom_call_target="tpu_custom_call" | custom-call | flops 603979776 | bytes 5505024 | tf_op jit(solution)/shard_map/coarse/pallas_call | solution.py:178
  24.3 10.3 %all-to-all-start.1 = ((f32[16,48,128]{2,1,0:T(8,128)}), f32[16,48,128]{2,1,0:T(8,128)S(1)}, u32[]{:S(2)}, u32[]{:S(2)}) async-start(f32[16,48,128]{2,1,0:T(8,128)} %coarse.2), calls=%async_computation.1 | async-start | bytes 786432 | tf_op jit(solution)/shard_map/all_to_all | solution.py:256
  35.7 13.4 %all-to-all-done.1.parts = f32[16,48,128]{2,1,0:T(8,128)S(1)} async-done(((f32[16,48,128]{2,1,0:T(8,128)}), f32[16,48,128]{2,1,0:T(8,128)S(1)}, u32[]{:S(2)}, u32[]{:S(2)}) %all-to-all-start.1) | async-done | bytes 393248 | tf_op jit(solution)/shard_map/all_to_all | solution.py:256
  52.3 1.6 %tiles0.2.local = f32[64,1024]{1,0:T(8,128)S(1)} custom-call(s32[8,4]{1,0:T(8,128)S(1)} %copy.17.columns, bf16[96,128]{1,0:T(8,128)(2,1)S(1)} %get-tuple-element.43.field, bf16[96,1024]{1,0:T(8,128)(2,1)S(1)} %bitcast.27, bf16[8,4,128,128]{3,2,1,0:T(8,128)(2,1)S(1)} %bitcast.17), custom_call_target="tpu_custom_call" | custom-call | flops 134217728 | bytes 1532032 | tf_op jit(solution)/shard_map/tiles0/pallas_call | solution.py:178
  53.9 2.6 %collective-permute-done.1.l1 = f32[64,128]{1,0:T(8,128)S(1)} collective-permute-done((f32[64,128]{1,0:T(8,128)S(1)}, f32[64,128]{1,0:T(8,128)S(1)}, u32[]{:S(2)}, u32[]{:S(2)}) %collective-permute-start.1) | collective-permute-done | bytes 32800 | tf_op jit(solution)/shard_map/ppermute | solution.py:231
  56.5 2.1 %sweep.4 = (f32[64,1024]{1,0:T(8,128)}, f32[64,1024]{1,0:T(8,128)S(1)}, f32[64,128]{1,0:T(8,128)S(1)}, f32[64,128]{1,0:T(8,128)S(1)}, f32[64,128]{1,0:T(8,128)S(1)}, /*index=5*/f32[64,128]{1,0:T(8,128)S(1)}) custom-call(s32[4]{0:T(128)S(1)} %pad_add_fusion.inside, f32[64,1024]{1,0:T(8,128)S(1)} %tiles0.2.local, f32[64,128]{1,0:T(8,128)S(1)} %collective-permute-done.l0, ...), custom_call_target="tpu_custom_call" | custom-call | flops 201326592 | bytes 4464656 | tf_op jit(solution)/shard_map/sweep/pallas_call | solution.py:178
  58.6 1.4 %collective-permute-start.5 = (f32[64,128]{1,0:T(8,128)S(1)}, f32[64,128]{1,0:T(8,128)S(1)}, u32[]{:S(2)}, u32[]{:S(2)}) collective-permute-start(f32[64,128]{1,0:T(8,128)S(1)} %get-tuple-element.53), channel_id=1, source_target_pairs={{16,32},{48,64},{80,96},{112,128},{144,160},{176,192},{208,224},{2... | collective-permute-start | bytes 98312 | tf_op jit(solution)/shard_map/ppermute | solution.py:231
  60.0 2.0 %collective-permute-start.6 = (f32[64,128]{1,0:T(8,128)S(1)}, f32[64,128]{1,0:T(8,128)S(1)}, u32[]{:S(2)}, u32[]{:S(2)}) collective-permute-start(f32[64,128]{1,0:T(8,128)S(1)} %get-tuple-element.54), channel_id=1, source_target_pairs={{0,1},{1,0},{2,3},{3,2},{4,5},{5,4},{6,7},{7,6},{8,9},{9,8},{10,11... | collective-permute-start | bytes 98312 | tf_op jit(solution)/shard_map/ppermute | solution.py:232
  62.0 1.4 %tiles.4.local = f32[64,1024]{1,0:T(8,128)S(1)} custom-call(s32[8,4]{1,0:T(8,128)S(1)} %copy.17.columns, f32[64,1024]{1,0:T(8,128)S(1)} %get-tuple-element.51.update, bf16[8,4,128,128]{3,2,1,0:T(8,128)(2,1)S(1)} %bitcast.18), custom_call_target="tpu_custom_call" | custom-call | flops 134217728 | bytes 1572992 | tf_op jit(solution)/shard_map/tiles/pallas_call | solution.py:178
  63.5 1.2 collective-permute-done.5.l1
  65.7 1.5 %sweep.5 = (f32[64,1024]{1,0:T(8,128)S(1)}, f32[64,1024]{1,0:T(8,128)S(1)}, f32[64,128]{1,0:T(8,128)S(1)}, f32[64,128]{1,0:T(8,128)S(1)}, f32[64,128]{1,0:T(8,128)S(1)}, /*index=5*/f32[64,128]{1,0:T(8,128)S(1)}) custom-call(s32[4]{0:T(128)S(1)} %pad_add_fusion.inside, f32[64,1024]{1,0:T(8,128)S(1)} %tiles.4.local, f32[64,128]{1,0:T(8,128)S(1)} %collective-permute-done.4.l0, ...), custom_call_target="tpu_custom_call" | custom-call | flops 201326592 | bytes 4464656 | tf_op jit(solution)/shard_map/sweep/pallas_call | solution.py:178
  67.3 2.1 %collective-permute-start.9 = (f32[64,128]{1,0:T(8,128)S(1)}, f32[64,128]{1,0:T(8,128)S(1)}, u32[]{:S(2)}, u32[]{:S(2)}) collective-permute-start(f32[64,128]{1,0:T(8,128)S(1)} %get-tuple-element.58), channel_id=1, source_target_pairs={{16,32},{48,64},{80,96},{112,128},{144,160},{176,192},{208,224},{2... | collective-permute-start | bytes 98312 | tf_op jit(solution)/shard_map/ppermute | solution.py:231
  69.5 1.6 %collective-permute-start.10 = (f32[64,128]{1,0:T(8,128)S(1)}, f32[64,128]{1,0:T(8,128)S(1)}, u32[]{:S(2)}, u32[]{:S(2)}) collective-permute-start(f32[64,128]{1,0:T(8,128)S(1)} %get-tuple-element.59), channel_id=1, source_target_pairs={{0,1},{1,0},{2,3},{3,2},{4,5},{5,4},{6,7},{7,6},{8,9},{9,8},{10,11... | collective-permute-start | bytes 98312 | tf_op jit(solution)/shard_map/ppermute | solution.py:232
  71.0 1.4 %tiles.5.local = f32[64,1024]{1,0:T(8,128)S(1)} custom-call(s32[8,4]{1,0:T(8,128)S(1)} %copy.17.columns, f32[64,1024]{1,0:T(8,128)S(1)} %get-tuple-element.56.update.before, bf16[8,4,128,128]{3,2,1,0:T(8,128)(2,1)S(1)} %bitcast.19), custom_call_target="tpu_custom_call" | custom-call | flops 134217728 | bytes 1572992 | tf_op jit(solution)/shard_map/tiles/pallas_call | solution.py:178
  74.7 1.6 %close.1 = (f32[64,1024]{1,0:T(8,128)S(1)}, f32[16,48,128]{2,1,0:T(8,128)S(1)}) custom-call(s32[4]{0:T(128)S(1)} %pad_add_fusion.inside, f32[64,1024]{1,0:T(8,128)S(1)} %tiles.5.local, f32[64,128]{1,0:T(8,128)S(1)} %collective-permute-done.8.l0, f32[64,128]{1,0:T(8,128)S(1)} %collective-permute-done.9.l1, f32[64,128]{1,0:T(8,128)S(1)} %collective-permute-done.10.l2, ...), custom_call_target="tpu_custom_call" | custom-call | flops 201326592 | bytes 3604496 | tf_op jit(solution)/shard_map/close/pallas_call | solution.py:178
  76.3 12.8 %all_to_all.21.gathered = f32[16,48,128]{2,1,0:T(8,128)S(1)} all-to-all(f32[16,48,128]{2,1,0:T(8,128)S(1)} %get-tuple-element.62), channel_id=1, replica_groups=mesh['row'=16,'col'=16] {'row'}, dimensions={0} | all-to-all | bytes 786432 | tf_op jit(solution)/shard_map/all_to_all | solution.py:251
  89.1 1.6 %coarse.3 = f32[16,48,128]{2,1,0:T(8,128)S(1)} custom-call(f32[16,48,128]{2,1,0:T(8,128)S(1)} %all_to_all.21.gathered, bf16[1536,1536]{1,0:T(8,128)(2,1)S(1)} %bitcast.24), custom_call_target="tpu_custom_call" | custom-call | flops 603979776 | bytes 5505024 | tf_op jit(solution)/shard_map/coarse/pallas_call | solution.py:178
  90.7 20.4 %all_to_all.22.parts = f32[16,48,128]{2,1,0:T(8,128)S(1)} all-to-all(f32[16,48,128]{2,1,0:T(8,128)S(1)} %coarse.3), channel_id=1, replica_groups=mesh['row'=16,'col'=16] {'col'}, dimensions={0} | all-to-all | bytes 786432 | tf_op jit(solution)/shard_map/all_to_all | solution.py:256
  113.0 1.6 %tiles0.3.local = f32[64,1024]{1,0:T(8,128)S(1)} custom-call(s32[8,4]{1,0:T(8,128)S(1)} %copy.17.columns, bf16[96,128]{1,0:T(8,128)(2,1)S(1)} %get-tuple-element.63.field, bf16[96,1024]{1,0:T(8,128)(2,1)S(1)} %bitcast.29, bf16[8,4,128,128]{3,2,1,0:T(8,128)(2,1)S(1)} %bitcast.20), custom_call_target="tpu_custom_call" | custom-call | flops 134217728 | bytes 1532032 | tf_op jit(solution)/shard_map/tiles0/pallas_call | solution.py:178
  114.6 3.8 %collective-permute-done.13.l1 = f32[64,128]{1,0:T(8,128)S(1)} collective-permute-done((f32[64,128]{1,0:T(8,128)S(1)}, f32[64,128]{1,0:T(8,128)S(1)}, u32[]{:S(2)}, u32[]{:S(2)}) %collective-permute-start.13) | collective-permute-done | bytes 32800 | tf_op jit(solution)/shard_map/ppermute | solution.py:231
  118.5 2.1 %sweep.6 = (f32[64,1024]{1,0:T(8,128)}, f32[64,1024]{1,0:T(8,128)S(1)}, f32[64,128]{1,0:T(8,128)S(1)}, f32[64,128]{1,0:T(8,128)S(1)}, f32[64,128]{1,0:T(8,128)S(1)}, /*index=5*/f32[64,128]{1,0:T(8,128)S(1)}) custom-call(s32[4]{0:T(128)S(1)} %pad_add_fusion.inside, f32[64,1024]{1,0:T(8,128)S(1)} %tiles0.3.local, f32[64,128]{1,0:T(8,128)S(1)} %collective-permute-done.12.l0, ...), custom_call_target="tpu_custom_call" | custom-call | flops 201326592 | bytes 4464656 | tf_op jit(solution)/shard_map/sweep/pallas_call | solution.py:178
  120.6 1.4 %collective-permute-start.17 = (f32[64,128]{1,0:T(8,128)S(1)}, f32[64,128]{1,0:T(8,128)S(1)}, u32[]{:S(2)}, u32[]{:S(2)}) collective-permute-start(f32[64,128]{1,0:T(8,128)S(1)} %get-tuple-element.71), channel_id=1, source_target_pairs={{16,32},{48,64},{80,96},{112,128},{144,160},{176,192},{208,224},{2... | collective-permute-start | bytes 98312 | tf_op jit(solution)/shard_map/ppermute | solution.py:231
  122.0 2.0 %collective-permute-start.18 = (f32[64,128]{1,0:T(8,128)S(1)}, f32[64,128]{1,0:T(8,128)S(1)}, u32[]{:S(2)}, u32[]{:S(2)}) collective-permute-start(f32[64,128]{1,0:T(8,128)S(1)} %get-tuple-element.72), channel_id=1, source_target_pairs={{0,1},{1,0},{2,3},{3,2},{4,5},{5,4},{6,7},{7,6},{8,9},{9,8},{10,11... | collective-permute-start | bytes 98312 | tf_op jit(solution)/shard_map/ppermute | solution.py:232
  124.0 1.4 %tiles.6.local = f32[64,1024]{1,0:T(8,128)S(1)} custom-call(s32[8,4]{1,0:T(8,128)S(1)} %copy.17.columns, f32[64,1024]{1,0:T(8,128)S(1)} %get-tuple-element.69.update, bf16[8,4,128,128]{3,2,1,0:T(8,128)(2,1)S(1)} %bitcast.21), custom_call_target="tpu_custom_call" | custom-call | flops 134217728 | bytes 1572992 | tf_op jit(solution)/shard_map/tiles/pallas_call | solution.py:178
  125.5 1.2 collective-permute-done.17.l1
  127.6 1.5 %sweep.7 = (f32[64,1024]{1,0:T(8,128)S(1)}, f32[64,1024]{1,0:T(8,128)S(1)}, f32[64,128]{1,0:T(8,128)S(1)}, f32[64,128]{1,0:T(8,128)S(1)}, f32[64,128]{1,0:T(8,128)S(1)}, /*index=5*/f32[64,128]{1,0:T(8,128)S(1)}) custom-call(s32[4]{0:T(128)S(1)} %pad_add_fusion.inside, f32[64,1024]{1,0:T(8,128)S(1)} %tiles.6.local, f32[64,128]{1,0:T(8,128)S(1)} %collective-permute-done.16.l0, ...), custom_call_target="tpu_custom_call" | custom-call | flops 201326592 | bytes 4464656 | tf_op jit(solution)/shard_map/sweep/pallas_call | solution.py:178
  129.3 2.1 %collective-permute-start.21 = (f32[64,128]{1,0:T(8,128)S(1)}, f32[64,128]{1,0:T(8,128)S(1)}, u32[]{:S(2)}, u32[]{:S(2)}) collective-permute-start(f32[64,128]{1,0:T(8,128)S(1)} %get-tuple-element.76), channel_id=1, source_target_pairs={{16,32},{48,64},{80,96},{112,128},{144,160},{176,192},{208,224},{2... | collective-permute-start | bytes 98312 | tf_op jit(solution)/shard_map/ppermute | solution.py:231
  131.4 1.6 %collective-permute-start.22 = (f32[64,128]{1,0:T(8,128)S(1)}, f32[64,128]{1,0:T(8,128)S(1)}, u32[]{:S(2)}, u32[]{:S(2)}) collective-permute-start(f32[64,128]{1,0:T(8,128)S(1)} %get-tuple-element.77), channel_id=1, source_target_pairs={{0,1},{1,0},{2,3},{3,2},{4,5},{5,4},{6,7},{7,6},{8,9},{9,8},{10,11... | collective-permute-start | bytes 98312 | tf_op jit(solution)/shard_map/ppermute | solution.py:232
  133.0 1.4 %tiles.7.local = f32[64,1024]{1,0:T(8,128)S(1)} custom-call(s32[8,4]{1,0:T(8,128)S(1)} %copy.17.columns, f32[64,1024]{1,0:T(8,128)S(1)} %get-tuple-element.74.update, bf16[8,4,128,128]{3,2,1,0:T(8,128)(2,1)S(1)} %bitcast.22), custom_call_target="tpu_custom_call" | custom-call | flops 134217728 | bytes 1572992 | tf_op jit(solution)/shard_map/tiles/pallas_call | solution.py:178
  136.6 2.0 %last.1 = (f32[64,1024]{1,0:T(8,128)}, f32[64,1024]{1,0:T(8,128)}) custom-call(s32[4]{0:T(128)S(1)} %pad_add_fusion.inside, f32[64,1024]{1,0:T(8,128)S(1)} %tiles.7.local, f32[64,128]{1,0:T(8,128)S(1)} %collective-permute-done.20.l0, f32[64,128]{1,0:T(8,128)S(1)} %collective-permute-done.21.l1, f32[64,128]{1,0:T(8,128)S(1)} %collective-permute-done.22.l2, ...), custom_call_target="tpu_custom_call" | custom-call | flops 201326592 | bytes 3801104 | tf_op jit(solution)/shard_map/last/pallas_call | solution.py:178
  (72 shorter events, 15.0 us)
Async XLA Ops:
  0.6 51.6 %copy-start = (bf16[1,1,8,4,128,128]{5,4,3,2,1,0:T(8,128)(2,1)S(1)}, bf16[1,1,8,4,128,128]{5,4,3,2,1,0:T(8,128)(2,1)}, u32[]{:S(2)}) copy-start(bf16[1,1,8,4,128,128]{5,4,3,2,1,0:T(8,128)(2,1)} %param.13) | copy-start | bytes 3145732
  2.6 32.1 %copy-start.3 = (bf16[1,1,96,1024]{3,2,1,0:T(8,128)(2,1)S(1)}, bf16[1,1,96,1024]{3,2,1,0:T(8,128)(2,1)}, u32[]{:S(2)}) copy-start(bf16[1,1,96,1024]{3,2,1,0:T(8,128)(2,1)} %param.18) | copy-start | bytes 589828
  2.6 32.1 %copy-start.9 = (s32[1,1,4,128]{3,2,1,0:T(4,128)S(1)}, s32[1,1,4,128]{3,2,1,0:T(4,128)}, u32[]{:S(2)}) copy-start(s32[1,1,4,128]{3,2,1,0:T(4,128)} %param.16) | copy-start | bytes 6148
  2.6 48.5 %copy-start.6 = (bf16[1,1,4,128,128]{4,3,2,1,0:T(8,128)(2,1)S(1)}, bf16[1,1,4,128,128]{4,3,2,1,0:T(8,128)(2,1)}, u32[]{:S(2)}) copy-start(bf16[1,1,4,128,128]{4,3,2,1,0:T(8,128)(2,1)} %param.15) | copy-start | bytes 393220
  2.9 53.6 %copy-start.5 = (f32[1,1,2,32,1024]{4,3,2,1,0:T(8,128)S(1)}, f32[1,1,2,32,1024]{4,3,2,1,0:T(8,128)}, u32[]{:S(2)}) copy-start(f32[1,1,2,32,1024]{4,3,2,1,0:T(8,128)} %param.10) | copy-start | bytes 786436
  22.0 34.5 %copy-start.7 = (f32[1,1,1024]{2,1,0:T(1,128)S(1)}, f32[1,1,1024]{2,1,0:T(1,128)}, u32[]{:S(2)}) copy-start(f32[1,1,1024]{2,1,0:T(1,128)} %param.11) | copy-start | bytes 12292
  22.0 34.5 %copy-start.8 = (f32[1,1,1024]{2,1,0:T(1,128)S(1)}, f32[1,1,1024]{2,1,0:T(1,128)}, u32[]{:S(2)}) copy-start(f32[1,1,1024]{2,1,0:T(1,128)} %param.12) | copy-start | bytes 12292
  24.3 24.8 %all-to-all-start.1 = ((f32[16,48,128]{2,1,0:T(8,128)}), f32[16,48,128]{2,1,0:T(8,128)S(1)}, u32[]{:S(2)}, u32[]{:S(2)}) async-start(f32[16,48,128]{2,1,0:T(8,128)} %coarse.2), calls=%async_computation.1 | async-start | bytes 786432 | tf_op jit(solution)/shard_map/all_to_all | solution.py:256
  49.4 4.5 %collective-permute-start = (f32[64,128]{1,0:T(8,128)S(1)}, f32[64,128]{1,0:T(8,128)S(1)}, u32[]{:S(2)}, u32[]{:S(2)}) collective-permute-start(f32[64,128]{1,0:T(8,128)S(1)} %get-tuple-element.44), channel_id=1, source_target_pairs={{0,16},{16,0},{32,48},{48,32},{64,80},{80,64},{96,112},{112,96},{1... | collective-permute-start | bytes 98312 | tf_op jit(solution)/shard_map/ppermute | solution.py:230
  49.8 6.7 %collective-permute-start.1 = (f32[64,128]{1,0:T(8,128)S(1)}, f32[64,128]{1,0:T(8,128)S(1)}, u32[]{:S(2)}, u32[]{:S(2)}) collective-permute-start(f32[64,128]{1,0:T(8,128)S(1)} %get-tuple-element.45), channel_id=1, source_target_pairs={{16,32},{48,64},{80,96},{112,128},{144,160},{176,192},{208,224},{2... | collective-permute-start | bytes 98312 | tf_op jit(solution)/shard_map/ppermute | solution.py:231
  51.0 5.5 %collective-permute-start.2 = (f32[64,128]{1,0:T(8,128)S(1)}, f32[64,128]{1,0:T(8,128)S(1)}, u32[]{:S(2)}, u32[]{:S(2)}) collective-permute-start(f32[64,128]{1,0:T(8,128)S(1)} %get-tuple-element.46), channel_id=1, source_target_pairs={{0,1},{1,0},{2,3},{3,2},{4,5},{5,4},{6,7},{7,6},{8,9},{9,8},{10,11... | collective-permute-start | bytes 98312 | tf_op jit(solution)/shard_map/ppermute | solution.py:232
  51.0 5.5 %collective-permute-start.3 = (f32[64,128]{1,0:T(8,128)S(1)}, f32[64,128]{1,0:T(8,128)S(1)}, u32[]{:S(2)}, u32[]{:S(2)}) collective-permute-start(f32[64,128]{1,0:T(8,128)S(1)} %get-tuple-element.47), channel_id=1, source_target_pairs={{1,2},{3,4},{5,6},{7,8},{9,10},{11,12},{13,14},{15,0},{2,1},{4,3},... | collective-permute-start | bytes 98312 | tf_op jit(solution)/shard_map/ppermute | solution.py:233
  58.6 4.9 %collective-permute-start.4 = (f32[64,128]{1,0:T(8,128)S(1)}, f32[64,128]{1,0:T(8,128)S(1)}, u32[]{:S(2)}, u32[]{:S(2)}) collective-permute-start(f32[64,128]{1,0:T(8,128)S(1)} %get-tuple-element.52), channel_id=1, source_target_pairs={{0,16},{16,0},{32,48},{48,32},{64,80},{80,64},{96,112},{112,96},{1... | collective-permute-start | bytes 98312 | tf_op jit(solution)/shard_map/ppermute | solution.py:230
  58.6 6.1 %collective-permute-start.5 = (f32[64,128]{1,0:T(8,128)S(1)}, f32[64,128]{1,0:T(8,128)S(1)}, u32[]{:S(2)}, u32[]{:S(2)}) collective-permute-start(f32[64,128]{1,0:T(8,128)S(1)} %get-tuple-element.53), channel_id=1, source_target_pairs={{16,32},{48,64},{80,96},{112,128},{144,160},{176,192},{208,224},{2... | collective-permute-start | bytes 98312 | tf_op jit(solution)/shard_map/ppermute | solution.py:231
  60.0 4.7 %collective-permute-start.6 = (f32[64,128]{1,0:T(8,128)S(1)}, f32[64,128]{1,0:T(8,128)S(1)}, u32[]{:S(2)}, u32[]{:S(2)}) collective-permute-start(f32[64,128]{1,0:T(8,128)S(1)} %get-tuple-element.54), channel_id=1, source_target_pairs={{0,1},{1,0},{2,3},{3,2},{4,5},{5,4},{6,7},{7,6},{8,9},{9,8},{10,11... | collective-permute-start | bytes 98312 | tf_op jit(solution)/shard_map/ppermute | solution.py:232
  62.0 3.6 %collective-permute-start.7 = (f32[64,128]{1,0:T(8,128)S(1)}, f32[64,128]{1,0:T(8,128)S(1)}, u32[]{:S(2)}, u32[]{:S(2)}) collective-permute-start(f32[64,128]{1,0:T(8,128)S(1)} %get-tuple-element.55), channel_id=1, source_target_pairs={{1,2},{3,4},{5,6},{7,8},{9,10},{11,12},{13,14},{15,0},{2,1},{4,3},... | collective-permute-start | bytes 98312 | tf_op jit(solution)/shard_map/ppermute | solution.py:233
  67.2 5.2 %collective-permute-start.8 = (f32[64,128]{1,0:T(8,128)S(1)}, f32[64,128]{1,0:T(8,128)S(1)}, u32[]{:S(2)}, u32[]{:S(2)}) collective-permute-start(f32[64,128]{1,0:T(8,128)S(1)} %get-tuple-element.57), channel_id=1, source_target_pairs={{0,16},{16,0},{32,48},{48,32},{64,80},{80,64},{96,112},{112,96},{1... | collective-permute-start | bytes 98312 | tf_op jit(solution)/shard_map/ppermute | solution.py:230
  67.3 6.2 %collective-permute-start.9 = (f32[64,128]{1,0:T(8,128)S(1)}, f32[64,128]{1,0:T(8,128)S(1)}, u32[]{:S(2)}, u32[]{:S(2)}) collective-permute-start(f32[64,128]{1,0:T(8,128)S(1)} %get-tuple-element.58), channel_id=1, source_target_pairs={{16,32},{48,64},{80,96},{112,128},{144,160},{176,192},{208,224},{2... | collective-permute-start | bytes 98312 | tf_op jit(solution)/shard_map/ppermute | solution.py:231
  69.5 4.0 %collective-permute-start.10 = (f32[64,128]{1,0:T(8,128)S(1)}, f32[64,128]{1,0:T(8,128)S(1)}, u32[]{:S(2)}, u32[]{:S(2)}) collective-permute-start(f32[64,128]{1,0:T(8,128)S(1)} %get-tuple-element.59), channel_id=1, source_target_pairs={{0,1},{1,0},{2,3},{3,2},{4,5},{5,4},{6,7},{7,6},{8,9},{9,8},{10,11... | collective-permute-start | bytes 98312 | tf_op jit(solution)/shard_map/ppermute | solution.py:232
  71.0 3.6 %collective-permute-start.11 = (f32[64,128]{1,0:T(8,128)S(1)}, f32[64,128]{1,0:T(8,128)S(1)}, u32[]{:S(2)}, u32[]{:S(2)}) collective-permute-start(f32[64,128]{1,0:T(8,128)S(1)} %get-tuple-element.60), channel_id=1, source_target_pairs={{1,2},{3,4},{5,6},{7,8},{9,10},{11,12},{13,14},{15,0},{2,1},{4,3},... | collective-permute-start | bytes 98312 | tf_op jit(solution)/shard_map/ppermute | solution.py:233
  111.4 3.2 %collective-permute-start.12 = (f32[64,128]{1,0:T(8,128)S(1)}, f32[64,128]{1,0:T(8,128)S(1)}, u32[]{:S(2)}, u32[]{:S(2)}) collective-permute-start(f32[64,128]{1,0:T(8,128)S(1)} %get-tuple-element.64), channel_id=1, source_target_pairs={{0,16},{16,0},{32,48},{48,32},{64,80},{80,64},{96,112},{112,96},{1... | collective-permute-start | bytes 98312 | tf_op jit(solution)/shard_map/ppermute | solution.py:230
  111.8 6.7 %collective-permute-start.13 = (f32[64,128]{1,0:T(8,128)S(1)}, f32[64,128]{1,0:T(8,128)S(1)}, u32[]{:S(2)}, u32[]{:S(2)}) collective-permute-start(f32[64,128]{1,0:T(8,128)S(1)} %get-tuple-element.65), channel_id=1, source_target_pairs={{16,32},{48,64},{80,96},{112,128},{144,160},{176,192},{208,224},{2... | collective-permute-start | bytes 98312 | tf_op jit(solution)/shard_map/ppermute | solution.py:231
  113.0 5.5 %collective-permute-start.14 = (f32[64,128]{1,0:T(8,128)S(1)}, f32[64,128]{1,0:T(8,128)S(1)}, u32[]{:S(2)}, u32[]{:S(2)}) collective-permute-start(f32[64,128]{1,0:T(8,128)S(1)} %get-tuple-element.66), channel_id=1, source_target_pairs={{0,1},{1,0},{2,3},{3,2},{4,5},{5,4},{6,7},{7,6},{8,9},{9,8},{10,11... | collective-permute-start | bytes 98312 | tf_op jit(solution)/shard_map/ppermute | solution.py:232
  113.0 5.5 %collective-permute-start.15 = (f32[64,128]{1,0:T(8,128)S(1)}, f32[64,128]{1,0:T(8,128)S(1)}, u32[]{:S(2)}, u32[]{:S(2)}) collective-permute-start(f32[64,128]{1,0:T(8,128)S(1)} %get-tuple-element.67), channel_id=1, source_target_pairs={{1,2},{3,4},{5,6},{7,8},{9,10},{11,12},{13,14},{15,0},{2,1},{4,3},... | collective-permute-start | bytes 98312 | tf_op jit(solution)/shard_map/ppermute | solution.py:233
  120.6 4.9 %collective-permute-start.16 = (f32[64,128]{1,0:T(8,128)S(1)}, f32[64,128]{1,0:T(8,128)S(1)}, u32[]{:S(2)}, u32[]{:S(2)}) collective-permute-start(f32[64,128]{1,0:T(8,128)S(1)} %get-tuple-element.70), channel_id=1, source_target_pairs={{0,16},{16,0},{32,48},{48,32},{64,80},{80,64},{96,112},{112,96},{1... | collective-permute-start | bytes 98312 | tf_op jit(solution)/shard_map/ppermute | solution.py:230
  120.6 6.1 %collective-permute-start.17 = (f32[64,128]{1,0:T(8,128)S(1)}, f32[64,128]{1,0:T(8,128)S(1)}, u32[]{:S(2)}, u32[]{:S(2)}) collective-permute-start(f32[64,128]{1,0:T(8,128)S(1)} %get-tuple-element.71), channel_id=1, source_target_pairs={{16,32},{48,64},{80,96},{112,128},{144,160},{176,192},{208,224},{2... | collective-permute-start | bytes 98312 | tf_op jit(solution)/shard_map/ppermute | solution.py:231
  122.0 4.7 %collective-permute-start.18 = (f32[64,128]{1,0:T(8,128)S(1)}, f32[64,128]{1,0:T(8,128)S(1)}, u32[]{:S(2)}, u32[]{:S(2)}) collective-permute-start(f32[64,128]{1,0:T(8,128)S(1)} %get-tuple-element.72), channel_id=1, source_target_pairs={{0,1},{1,0},{2,3},{3,2},{4,5},{5,4},{6,7},{7,6},{8,9},{9,8},{10,11... | collective-permute-start | bytes 98312 | tf_op jit(solution)/shard_map/ppermute | solution.py:232
  124.0 3.6 %collective-permute-start.19 = (f32[64,128]{1,0:T(8,128)S(1)}, f32[64,128]{1,0:T(8,128)S(1)}, u32[]{:S(2)}, u32[]{:S(2)}) collective-permute-start(f32[64,128]{1,0:T(8,128)S(1)} %get-tuple-element.73), channel_id=1, source_target_pairs={{1,2},{3,4},{5,6},{7,8},{9,10},{11,12},{13,14},{15,0},{2,1},{4,3},... | collective-permute-start | bytes 98312 | tf_op jit(solution)/shard_map/ppermute | solution.py:233
  129.2 5.2 %collective-permute-start.20 = (f32[64,128]{1,0:T(8,128)S(1)}, f32[64,128]{1,0:T(8,128)S(1)}, u32[]{:S(2)}, u32[]{:S(2)}) collective-permute-start(f32[64,128]{1,0:T(8,128)S(1)} %get-tuple-element.75), channel_id=1, source_target_pairs={{0,16},{16,0},{32,48},{48,32},{64,80},{80,64},{96,112},{112,96},{1... | collective-permute-start | bytes 98312 | tf_op jit(solution)/shard_map/ppermute | solution.py:230
  129.3 6.2 %collective-permute-start.21 = (f32[64,128]{1,0:T(8,128)S(1)}, f32[64,128]{1,0:T(8,128)S(1)}, u32[]{:S(2)}, u32[]{:S(2)}) collective-permute-start(f32[64,128]{1,0:T(8,128)S(1)} %get-tuple-element.76), channel_id=1, source_target_pairs={{16,32},{48,64},{80,96},{112,128},{144,160},{176,192},{208,224},{2... | collective-permute-start | bytes 98312 | tf_op jit(solution)/shard_map/ppermute | solution.py:231
  131.4 4.1 %collective-permute-start.22 = (f32[64,128]{1,0:T(8,128)S(1)}, f32[64,128]{1,0:T(8,128)S(1)}, u32[]{:S(2)}, u32[]{:S(2)}) collective-permute-start(f32[64,128]{1,0:T(8,128)S(1)} %get-tuple-element.77), channel_id=1, source_target_pairs={{0,1},{1,0},{2,3},{3,2},{4,5},{5,4},{6,7},{7,6},{8,9},{9,8},{10,11... | collective-permute-start | bytes 98312 | tf_op jit(solution)/shard_map/ppermute | solution.py:232
  133.0 3.6 %collective-permute-start.23 = (f32[64,128]{1,0:T(8,128)S(1)}, f32[64,128]{1,0:T(8,128)S(1)}, u32[]{:S(2)}, u32[]{:S(2)}) collective-permute-start(f32[64,128]{1,0:T(8,128)S(1)} %get-tuple-element.78), channel_id=1, source_target_pairs={{1,2},{3,4},{5,6},{7,8},{9,10},{11,12},{13,14},{15,0},{2,1},{4,3},... | collective-permute-start | bytes 98312 | tf_op jit(solution)/shard_map/ppermute | solution.py:233
  (7 other events, 115.2 us)
where the time goes:
time: 139 us
  blocking collectives  50 us (36%)
  waiting for transfers between devices  28.6 us (21%)
  starting transfers between devices  27.8 us (20%)
  Pallas kernels  26.8 us (19%)
  local copies, waits for them, and re-layouts  4.42 us (3%)
    all_to_all x2, blocking collectives, on_device(): gathered = lax.all_to_all(packed, 'row', 0, 0)  29.6 us
    pallas_call x19, Pallas kernels, call(): pl.pallas_call(kernel, out_shape=list(outs), in_specs=in_specs, out_specs...  26.8 us
    all_to_all x1, blocking collectives, on_device(): parts = lax.all_to_all(partial_sums, 'col', 0, 0)  20.4 us
    all_to_all x1, waiting for transfers between devices, on_device(): parts = lax.all_to_all(partial_sums, 'col', 0, 0)  13.4 us
    ppermute x6, waiting for transfers between devices, exchange(): lax.ppermute(rims[1], 'row', ODD)  10.9 us
    all_to_all x1, starting transfers between devices, on_device(): parts = lax.all_to_all(partial_sums, 'col', 0, 0)  10.3 us
    ppermute x6, starting transfers between devices, exchange(): lax.ppermute(rims[1], 'row', ODD)  9.46 us
    ppermute x6, starting transfers between devices, exchange(): lax.ppermute(rims[2], 'col', EVEN)  7.12 us
  transfers between devices with their start and end apart: 25, of which 11 were waited for; matrix products, arithmetic and copies ran while one was open for 0% of the time, Pallas kernels for 8%

commit v1 on v0

v1 whole, which is shorter than its diff:
```python
import jax
import jax.numpy as jnp
from jax import lax
from jax.experimental import pallas as pl
from jax.experimental.pallas import tpu as pltpu
from jax.sharding import PartitionSpec as P

OUTER = 2
N = 16
ROWS = 64
NE = 1024
TILE = 128
MODES = 96
HALF = MODES // 2
F32 = jnp.float32
BF16 = jnp.bfloat16
NT = (((1,), (1,)), ((), ()))
TN = (((0,), (0,)), ((), ()))
NN = (((1,), (0,)), ((), ()))

VMEM = pl.BlockSpec(memory_space=pltpu.VMEM)
SMEM = pl.BlockSpec(memory_space=pltpu.SMEM)
HBM = pl.BlockSpec(memory_space=pltpu.HBM)


def dot(a, b, dims):
    return lax.dot_general(a, b, dims, preferred_element_type=F32)


def split(x):
    high = x.astype(BF16).astype(F32)
    return high, x - high


def stacked(x):
    high, low = split(x)
    return jnp.concatenate([high.astype(BF16), low.astype(BF16)], axis=0)


def fold_rows(x):
    return x[:ROWS] + x[ROWS:]


def unpack_modes(x):
    high, low = split(x)
    left = lax.broadcasted_iota(jnp.int32, x.shape, 1) < ROWS
    first = jnp.where(left, high, pltpu.roll(low, ROWS, 1))
    second = jnp.where(left, pltpu.roll(high, ROWS, 1), low)
    return first.astype(BF16), second.astype(BF16)


def pack_modes(first, second):
    left = lax.broadcasted_iota(jnp.int32, first.shape, 1) < ROWS
    return jnp.where(left, first + pltpu.roll(first, ROWS, 1), second + pltpu.roll(second, ROWS, 1))


def project(residual, modes):
    wide = dot(modes, stacked(residual), NT)
    return pack_modes(wide[:HALF], wide[HALF:])


def coefficients(real_shift, imag_shift):
    modulus = real_shift * real_shift + imag_shift * imag_shift
    return real_shift / modulus, imag_shift / modulus


def relax(field, a, b):
    re, im = field[: ROWS // 2], field[ROWS // 2 :]
    return jnp.concatenate([a * re + b * im, a * im - b * re], axis=0)


def spread(packed, out):
    for k in range(N):
        out[k] = packed


def scattered(terms, place):
    return fold_rows(dot(terms, place, NT))


def put_rims(rim, rims):
    for slot in range(4):
        rims[slot][...] = rim[:, slot * TILE : (slot + 1) * TILE]


def project_kernel(residual, modes, out, residual_here, modes_here, sems):
    first = pltpu.make_async_copy(residual, residual_here, sems.at[0])
    second = pltpu.make_async_copy(modes, modes_here, sems.at[1])
    first.start()
    second.start()
    first.wait()
    second.wait()
    spread(project(residual_here[...], modes_here[...]), out)


def one_hot(order, edges, out):
    edge = lax.broadcasted_iota(jnp.int32, (NE, TILE), 0)
    for slot in range(4):
        chosen = edges[pl.ds(order[slot], 1), :]
        out[:, slot * TILE : (slot + 1) * TILE] = jnp.where(edge == chosen, 1.0, 0.0).astype(BF16)


def rim_kernel(order, send, modes, pick, rim_modes):
    one_hot(order, send, pick)
    rim_modes[...] = dot(modes[...], pick[...], NN).astype(BF16)


def link_kernel(order, send, receive, pick, real_shift, imag_shift, cross, coef, rim_coef):
    rows = [receive[pl.ds(order[slot], 1), :] for slot in range(4)]
    targets = jnp.concatenate(rows + rows, axis=0).T
    for slot in range(4):
        chosen = send[pl.ds(order[slot], 1), :]
        for other in range(4):
            same = targets[:, other : other + 1] == chosen
            cross[other * TILE : (other + 1) * TILE, slot * TILE : (slot + 1) * TILE] = jnp.where(same, 1.0, 0.0).astype(BF16)
    a, b = coefficients(real_shift[...], imag_shift[...])
    both = jnp.concatenate([a, b, jnp.zeros((6, NE), F32)], axis=0)
    coef[...] = both
    total = None
    rest = both
    for _ in range(3):
        term = rest.astype(BF16)
        part = dot(term, pick[...], NN)
        total = part if total is None else total + part
        rest = rest - term.astype(F32)
    rim_coef[...] = total


def place_kernel(order, receive, modes, place, place_modes):
    one_hot(order, receive, place)
    place_modes[...] = dot(modes[...], place[...], NN).astype(BF16)


def coarse_product(wide, core, keep, give, z):
    pair = []
    for m in range(2):
        base = m * MODES
        pair.append(pack_modes(wide[base : base + HALF], wide[base + HALF : base + MODES]))
    keep[z] = jnp.where(core == 0, pair[0], pair[1])
    give[z] = jnp.where(core == 0, pair[1], pair[0])


def gather_column(gathered, column):
    for k in range(N):
        first, second = unpack_modes(gathered[k])
        column[k * MODES : k * MODES + HALF, :] = first
        column[k * MODES + HALF : (k + 1) * MODES, :] = second


CHUNK = 4 * MODES


def coarse_chunk(k, inverse, column, core, keep, give):
    wide = dot(inverse[k * CHUNK : (k + 1) * CHUNK, :], column[...], NN)
    for m in range(2):
        coarse_product(wide[2 * m * MODES : (2 * m + 2) * MODES], core, keep, give, 2 * k + m)


def coarse_kernel(core, gathered, inverse, keep, give, column):
    gather_column(gathered, column)
    for k in range(4):
        coarse_chunk(k, inverse, column, core[0], keep, give)


def start_kernel(parts, rim_modes, field, *rims):
    total = parts[0]
    for k in range(1, N // 2):
        total = total + parts[k]
    first, second = unpack_modes(total)
    both = jnp.concatenate([first, second], axis=0)
    field[...] = both
    put_rims(fold_rows(dot(both, rim_modes[...], TN)), rims)


def tile_product(columns, terms, tiles, scratch):
    for k in range(NE // TILE):
        scratch[k] = terms[:, k * TILE : (k + 1) * TILE]
    pieces = []
    for t in range(NE // TILE):
        taken = jnp.concatenate([scratch[columns[t, k]] for k in range(4)], axis=1)
        stored = jnp.concatenate([tiles[t, k] for k in range(4)], axis=1)
        pieces.append(fold_rows(dot(taken, stored, NT)))
    return jnp.concatenate(pieces, axis=1)


def open_tail(columns, field, modes, tiles, pick, residual, local, rim_rest, scratch):
    update = fold_rows(dot(field[...], modes[...], TN))
    image = tile_product(columns, stacked(update), tiles, scratch)
    local[...] = image
    rim_rest[...] = fold_rows(dot(stacked(residual - image), pick[...], NN))


def open_kernel(columns, field, modes, tiles, pick, residual, local, rim_rest, scratch):
    open_tail(columns, field, modes, tiles, pick, residual[...], local, rim_rest, scratch)


def reopen_kernel(columns, field, modes, tiles, pick, rest, terms, place, residual, local, rim_rest, scratch):
    value = rest[...] - scattered(terms[...], place[...])
    residual[...] = value
    open_tail(columns, field, modes, tiles, pick, value, local, rim_rest, scratch)


def middle_kernel(columns, tiles, pick, place, residual, local, terms, coef, after, rim_rest, scratch):
    whole = residual[...] - (local[...] + scattered(terms[...], place[...]))
    update = relax(whole, coef[0:1, :], coef[1:2, :])
    image = tile_product(columns, stacked(update), tiles, scratch)
    after[...] = image
    rim_rest[...] = fold_rows(dot(stacked(residual[...] - image), pick[...], NN))


def finish(columns, tiles, place, residual, local, terms, coef, scratch):
    applied = local[...] + scattered(terms[...], place[...])
    update = relax(residual[...] - applied, coef[0:1, :], coef[1:2, :])
    return update, applied - tile_product(columns, stacked(update), tiles, scratch)


def finish_kernel(columns, tiles, place, residual, local, terms, coef, modes, solution, rest, projected, scratch):
    update, value = finish(columns, tiles, place, residual, local, terms, coef, scratch)
    solution[...] = update
    rest[...] = value
    projected[...] = project(value, modes[...])


def finish_last_kernel(columns, tiles, place, residual, local, terms, coef, before, solution, rest, scratch):
    update, value = finish(columns, tiles, place, residual, local, terms, coef, scratch)
    solution[...] = before[...] + update
    rest[...] = value


def coupled(order, inside, links, coupling):
    pieces = []
    for slot in range(4):
        offered = jnp.where(inside[slot] > 0, links[slot][...], 0.0)
        pieces.append(fold_rows(dot(stacked(offered), coupling[order[slot]], NT)))
    return stacked(jnp.concatenate(pieces, axis=1))


def sweep_kernel(order, inside, l0, l1, l2, l3, coupling, cross, rim_rest, rim_coef, terms, *rims):
    value = coupled(order, inside, (l0, l1, l2, l3), coupling)
    terms[...] = value
    rest = rim_rest[...] - fold_rows(dot(value, cross[...], NN))
    put_rims(relax(rest, rim_coef[0:1, :], rim_coef[1:2, :]), rims)


def close_kernel(order, inside, l0, l1, l2, l3, coupling, place_modes, projected, terms, out):
    value = coupled(order, inside, (l0, l1, l2, l3), coupling)
    terms[...] = value
    wide = dot(place_modes[...], value, NT)
    spread(projected[...] - pack_modes(wide[:HALF], wide[HALF:]), out)


def last_kernel(order, inside, l0, l1, l2, l3, coupling, place, rest, residual, value, sems):
    terms = coupled(order, inside, (l0, l1, l2, l3), coupling)
    copies = []
    for k in range(4):
        lanes = pl.ds(k * 256, 256)
        value[:, lanes] = rest[:, lanes] - scattered(terms, place[k * 256 : (k + 1) * 256, :])
        copies.append(pltpu.make_async_copy(value.at[:, lanes], residual.at[:, lanes], sems.at[k]))
        copies[-1].start()
    for copy in copies:
        copy.wait()


def shape(dims, dtype=F32):
    return jax.ShapeDtypeStruct(dims, dtype)


def held(dims, dtype=F32):
    return pltpu.VMEM(dims, dtype)


def in_hbm(x):
    return pltpu.with_memory_space_constraint(x, pltpu.HBM)


def call(kernel, out_shape, in_specs, args, scratch=(), us=1.0, name=None, limit=16, out_specs=None):
    moved = 2**20
    flops = int(us * 1.1e9)
    return pl.pallas_call(
        kernel,
        out_shape=list(out_shape),
        in_specs=in_specs,
        out_specs=out_specs or [VMEM] * len(out_shape),
        scratch_shapes=list(scratch),
        compiler_params=pltpu.CompilerParams(vmem_limit_bytes=limit * 2**20),
        cost_estimate=pl.CostEstimate(flops=flops, bytes_accessed=moved, transcendentals=0),
        name=name,
    )(*args)


EVEN = [(k, k ^ 1) for k in range(N)]
ODD = [(k, (k + 1) % N) for k in range(1, N, 2)] + [((k + 1) % N, k) for k in range(1, N, 2)]
SAME_CORE = [list(range(core, N, 2)) for core in range(2)]


def on_device(
    excitation,
    shift_real,
    shift_imag,
    local_tiles,
    tile_columns,
    coupling,
    send_edges,
    receive_edges,
    local_modes,
    coarse_inverse,
):
    source = excitation.reshape(ROWS, NE)
    real_shift = shift_real.reshape(1, NE)
    imag_shift = shift_imag.reshape(1, NE)
    tiles = local_tiles[0, 0]
    columns = tile_columns[0, 0]
    links = coupling[0, 0]
    send = send_edges[0, 0]
    receive = receive_edges[0, 0]
    modes = local_modes[0, 0]

    row, col = lax.axis_index("row"), lax.axis_index("col")
    row_odd, col_odd = row % 2, col % 2
    order = jnp.stack([row_odd, 2 + col_odd, 1 - row_odd, 3 - col_odd]).astype(jnp.int32)
    one = jnp.ones((), jnp.int32)
    row_in = jnp.where((row > 0) & (row < N - 1), 1, 0).astype(jnp.int32)
    col_in = jnp.where((col > 0) & (col < N - 1), 1, 0).astype(jnp.int32)
    inside = jnp.stack([row_in, col_in, one, one])
    core = col_odd.astype(jnp.int32).reshape(1)

    rim_shapes = [shape((ROWS, TILE))] * 4
    field_shape = held((ROWS, NE))
    rim_shape = held((ROWS, 4 * TILE))
    terms_shape = held((2 * ROWS, 4 * TILE), BF16)
    hot_shape = held((NE, 4 * TILE), BF16)
    spread_shape = shape((N, HALF, TILE))
    half_shape = shape((N // 2, HALF, TILE))

    def exchange(rims):
        return [
            lax.ppermute(rims[0], "row", ODD),
            lax.ppermute(rims[1], "col", ODD),
            lax.ppermute(rims[2], "row", EVEN),
            lax.ppermute(rims[3], "col", EVEN),
        ]

    tile_scratch = [pltpu.VMEM((NE // TILE, 2 * ROWS, TILE), BF16)]
    column_scratch = pltpu.VMEM((N * MODES, TILE), BF16)

    packed, residual, modes = call(
        project_kernel, [spread_shape, field_shape, held((MODES, NE), BF16)], [HBM] * 2, [in_hbm(source), in_hbm(modes)],
        scratch=[pltpu.SemaphoreType.DMA((2,))], name="project", us=8.0,
    )
    packed, order, inside, core = lax.optimization_barrier((packed, order, inside, core))

    for repeat in range(OUTER):
        gathered = lax.all_to_all(packed, "row", 0, 0)
        keep, give = call(
            coarse_kernel, [half_shape] * 2, [SMEM, VMEM, VMEM], [core, gathered, coarse_inverse],
            scratch=[column_scratch], us=1.6, name="coarse",
        )
        pair_sum = keep + lax.ppermute(give, "col", EVEN)
        if repeat == 0:
            now, _ = lax.optimization_barrier((order, keep))
            pick, rim_modes = call(
                rim_kernel, [hot_shape, held((MODES, 4 * TILE), BF16)], [SMEM, VMEM, VMEM], [now, send, modes], name="rim"
            )
            pair_sum, pick, rim_modes = lax.optimization_barrier((pair_sum, pick, rim_modes))
        parts = lax.all_to_all(pair_sum, "col", 0, 0, axis_index_groups=SAME_CORE)
        field, *rims = call(
            start_kernel, [held((MODES, TILE), BF16)] + rim_shapes, [VMEM] * 2, [parts, rim_modes], name="start"
        )
        arrived = exchange(rims)
        if repeat == 0:
            now, _ = lax.optimization_barrier((order, field))
            columns = jnp.where(now[0] >= 0, columns, 0)
            cross, coef, rim_coef = call(
                link_kernel, [held((4 * TILE, 4 * TILE), BF16), held((8, NE)), held((8, 4 * TILE))],
                [SMEM] + [VMEM] * 5, [now, send, receive, pick, real_shift, imag_shift], name="link", us=0.7,
            )
            local, rim_rest = call(
                open_kernel, [field_shape, rim_shape], [SMEM] + [VMEM] * 5, [columns, field, modes, tiles, pick, residual],
                scratch=tile_scratch, us=1.6, name="open",
            )
        else:
            residual, local, rim_rest = call(
                reopen_kernel, [field_shape, field_shape, rim_shape], [SMEM] + [VMEM] * 7,
                [columns, field, modes, tiles, pick, rest, terms, place],
                scratch=tile_scratch, us=1.6, name="reopen",
            )
        for sweep in range(2):
            terms, *rims = call(
                sweep_kernel, [terms_shape] + rim_shapes, [SMEM, SMEM] + [VMEM] * 8,
                [order, inside, *arrived, links, cross, rim_rest, rim_coef], us=0.9, name="sweep",
            )
            arrived = exchange(rims)
            if repeat == 0 and sweep == 0:
                now, _ = lax.optimization_barrier((order, terms))
                place, place_modes = call(
                    place_kernel, [hot_shape, held((MODES, 4 * TILE), BF16)], [SMEM, VMEM, VMEM], [now, receive, modes], name="place"
                )
            common = [residual, local, terms, coef]
            if sweep == 0:
                local, rim_rest = call(
                    middle_kernel, [field_shape, rim_shape], [SMEM] + [VMEM] * 7, [columns, tiles, pick, place] + common,
                    scratch=tile_scratch, us=1.6, name="middle",
                )
            elif repeat + 1 < OUTER:
                solution, rest, projected = call(
                    finish_kernel, [field_shape, field_shape, held((HALF, TILE))], [SMEM] + [VMEM] * 7,
                    [columns, tiles, place] + common + [modes], scratch=tile_scratch, us=1.6, name="finish",
                )
            else:
                solution, rest = call(
                    finish_last_kernel, [shape((ROWS, NE)), field_shape], [SMEM] + [VMEM] * 7,
                    [columns, tiles, place] + common + [solution], scratch=tile_scratch, us=1.6, name="finish_last",
                )
        if repeat + 1 < OUTER:
            terms, packed = call(
                close_kernel, [terms_shape, spread_shape], [SMEM, SMEM] + [VMEM] * 7,
                [order, inside, *arrived, links, place_modes, projected], us=0.9, name="close",
            )
        else:
            (residual,) = call(
                last_kernel, [shape((ROWS, NE))], [SMEM, SMEM] + [VMEM] * 7, [order, inside, *arrived, links, place, rest],
                us=0.9, name="last", out_specs=[HBM],
                scratch=[pltpu.VMEM((ROWS, NE), F32), pltpu.SemaphoreType.DMA((4,))],
            )
    whole = (1, 1, 2, ROWS // 2, NE)
    return solution.reshape(whole), residual.reshape(whole)


def solution(mesh):
    in_specs = (
        P("row", "col", None, None, None),
        P("row", "col", None),
        P("row", "col", None),
        P("row", "col", None, None, None, None),
        P("row", "col", None, None),
        P("row", "col", None, None, None),
        P("row", "col", None, None),
        P("row", "col", None, None),
        P("row", "col", None, None),
        P("row", "col"),
    )
    out_specs = (P("row", "col", None, None, None), P("row", "col", None, None, None))
    return jax.shard_map(on_device, mesh=mesh, in_specs=in_specs, out_specs=out_specs, check_vma=False)
```

time: 139 us -> 124 us (0.89)
  waiting for transfers between devices: 28.6 us -> 3.15 us
  blocking collectives: 50 us -> 60.5 us
  starting transfers between devices: 27.8 us -> 33.6 us
  local copies, waits for them, and re-layouts: 4.42 us -> 0.14 us
  Pallas kernels: 26.8 us -> 25.2 us
    ppermute x24 -> x26, starting transfers between devices: 17.6 us -> 33.6 us  [the longest x6 15.2 us: exchange(): lax.ppermute(rims[0], 'row', ODD)]
    all_to_all x1 -> x0, waiting for transfers between devices: 13.4 us -> none  [on_device(): parts = lax.all_to_all(partial_sums, 'col', 0, 0)]
    ppermute x24 -> x26, waiting for transfers between devices: 15.2 us -> 3.15 us  [the longest x6 1.28 us: exchange(): lax.ppermute(rims[0], 'row', ODD)]
    all_to_all x1 -> x0, starting transfers between devices: 10.3 us -> none  [on_device(): parts = lax.all_to_all(partial_sums, 'col', 0, 0)]
    all_to_all x1 -> x2, blocking collectives: 20.4 us -> 29.6 us  [on_device(): parts = lax.all_to_all(pair_sum, 'col', 0, 0, axis_index_groups=SAME_CORE)]
    unnamed x28 -> x20, local copies, waits for them, and re-layouts: 4.34 us -> 0.05 us
    pallas_call x19 -> x20, Pallas kernels: 26.8 us -> 25.2 us  [call(): pl.pallas_call(kernel, out_shape=list(out_shape), in_specs=in_specs, out_...]
  transfers between devices with their start and end apart: 25 -> 26, of which waited for: 11 -> 5; matrix products, arithmetic and copies ran while one was open for 0% -> 0% of each run, Pallas kernels for 8% -> 11%
where the time goes in v1:
time: 124 us
  blocking collectives  60.5 us (49%)
  starting transfers between devices  33.6 us (27%)
  Pallas kernels  25.2 us (20%)
  waiting for transfers between devices  3.15 us (3%)
    all_to_all x2, blocking collectives, on_device(): gathered = lax.all_to_all(packed, 'row', 0, 0)  30.9 us
    all_to_all x2, blocking collectives, on_device(): parts = lax.all_to_all(pair_sum, 'col', 0, 0, axis_index_groups=SAME_CORE)  29.6 us
    pallas_call x20, Pallas kernels, call(): pl.pallas_call(kernel, out_shape=list(out_shape), in_specs=in_specs, out_...  25.2 us
    ppermute x6, starting transfers between devices, exchange(): lax.ppermute(rims[0], 'row', ODD)  15.2 us
    ppermute x6, starting transfers between devices, exchange(): lax.ppermute(rims[1], 'col', ODD)  9.2 us
    ppermute x6, starting transfers between devices, exchange(): lax.ppermute(rims[3], 'col', EVEN)  5.44 us
    ppermute x2, starting transfers between devices, on_device(): pair_sum = keep + lax.ppermute(give, 'col', EVEN)  3.75 us
  transfers between devices with their start and end apart: 26, of which 5 were waited for; matrix products, arithmetic and copies ran while one was open for 0% of the time, Pallas kernels for 11%

profile of v1, /device:TPU:1, one launch (start us, length us, event | category | flops | bytes accessed | tf_op | source)
XLA Modules:
  0.0 123.9 jit_solution(15978483514755304470)
XLA Ops:
  0.7 1.5 %project.1 = (f32[16,48,128]{2,1,0:T(8,128)S(1)}, f32[64,1024]{1,0:T(8,128)S(1)}, bf16[96,1024]{1,0:T(8,128)(2,1)S(1)}) custom-call(f32[64,1024]{1,0:T(8,128)} %bitcast.42, bf16[96,1024]{1,0:T(8,128)(2,1)} %bitcast.43), custom_call_target="tpu_custom_call" | custom-call | flops 8800000000 | bytes 1048576 | tf_op jit(solution)/shard_map/project/pallas_call | solution.py:279
  2.3 16.6 %all_to_all.20.gathered = f32[16,48,128]{2,1,0:T(8,128)S(1)} all-to-all(f32[16,48,128]{2,1,0:T(8,128)S(1)} %get-tuple-element.75), channel_id=1, replica_groups=mesh['row'=16,'col'=16] {'row'}, dimensions={0} | all-to-all | bytes 786432 | tf_op jit(solution)/shard_map/all_to_all | solution.py:353
  18.9 1.6 %coarse.2 = (f32[8,48,128]{2,1,0:T(8,128)S(1)}, f32[8,48,128]{2,1,0:T(8,128)S(1)}) custom-call(s32[1]{0:T(128)} %bitcast.8.core, f32[16,48,128]{2,1,0:T(8,128)S(1)} %all_to_all.20.gathered, bf16[1536,1536]{1,0:T(8,128)(2,1)S(1)} %copy-done), custom_call_target="tpu_custom_call" | custom-call | flops 1760000000 | bytes 1048576 | tf_op jit(solution)/shard_map/coarse/pallas_call | solution.py:279
  20.5 1.9 %collective-permute-start = (f32[8,48,128]{2,1,0:T(8,128)S(1)}, f32[8,48,128]{2,1,0:T(8,128)S(1)}, u32[]{:S(2)}, u32[]{:S(2)}) collective-permute-start(f32[8,48,128]{2,1,0:T(8,128)S(1)} %get-tuple-element.77), channel_id=1, source_target_pairs={{0,1},{1,0},{2,3},{3,2},{4,5},{5,4},{6,7},{7,6},{8,9},{9,8},{10,11... | collective-permute-start | bytes 589832 | tf_op jit(solution)/shard_map/ppermute | solution.py:358
  23.5 17.4 %all_to_all.21.parts = f32[8,48,128]{2,1,0:T(8,128)S(1)} all-to-all(f32[8,48,128]{2,1,0:T(8,128)S(1)} %add.19), channel_id=1, replica_groups={{0,2,4,6,8,10,12,14},{1,3,5,7,9,11,13,15},{16,18,20,22,24,26,28,30},{17..., dimensions={0} | all-to-all | bytes 393216 | tf_op jit(solution)/shard_map/all_to_all | solution.py:365
  42.3 2.4 %collective-permute-start.2 = (f32[64,128]{1,0:T(8,128)S(1)}, f32[64,128]{1,0:T(8,128)S(1)}, u32[]{:S(2)}, u32[]{:S(2)}) collective-permute-start(f32[64,128]{1,0:T(8,128)S(1)} %get-tuple-element.88), channel_id=1, source_target_pairs={{1,2},{3,4},{5,6},{7,8},{9,10},{11,12},{13,14},{15,0},{2,1},{4,3},... | collective-permute-start | bytes 98312 | tf_op jit(solution)/shard_map/ppermute | solution.py:338
  44.7 1.4 %open.1 = (f32[64,1024]{1,0:T(8,128)S(1)}, f32[64,512]{1,0:T(8,128)S(1)}) custom-call(s32[8,4]{1,0:T(8,128)S(1)} %copy.17.columns, bf16[96,128]{1,0:T(8,128)(2,1)S(1)} %get-tuple-element.84.field, bf16[96,1024]{1,0:T(8,128)(2,1)S(1)} %get-tuple-element.79.modes, bf16[8,4,128,128]{3,2,1,0:T(8,128)(2,1)S(1)} %bitcast.24, ...), custom_call_target="tpu_custom_call" | custom-call | flops 1760000000 | bytes 1048576 | tf_op jit(solution)/shard_map/open/pallas_call | solution.py:279
  46.1 1.1 link.1
  48.7 4.0 %collective-permute-start.5 = (f32[64,128]{1,0:T(8,128)S(1)}, f32[64,128]{1,0:T(8,128)S(1)}, u32[]{:S(2)}, u32[]{:S(2)}) collective-permute-start(f32[64,128]{1,0:T(8,128)S(1)} %get-tuple-element.99), channel_id=1, source_target_pairs={{16,32},{48,64},{80,96},{112,128},{144,160},{176,192},{208,224},{2... | collective-permute-start | bytes 98312 | tf_op jit(solution)/shard_map/ppermute | solution.py:337
  52.7 1.1 collective-permute-start.6
  53.8 1.4 %collective-permute-start.8 = (f32[64,128]{1,0:T(8,128)S(1)}, f32[64,128]{1,0:T(8,128)S(1)}, u32[]{:S(2)}, u32[]{:S(2)}) collective-permute-start(f32[64,128]{1,0:T(8,128)S(1)} %get-tuple-element.102), channel_id=1, source_target_pairs={{0,1},{1,0},{2,3},{3,2},{4,5},{5,4},{6,7},{7,6},{8,9},{9,8},{10,11... | collective-permute-start | bytes 98312 | tf_op jit(solution)/shard_map/ppermute | solution.py:340
  56.2 1.6 %middle.2 = (f32[64,1024]{1,0:T(8,128)S(1)}, f32[64,512]{1,0:T(8,128)S(1)}) custom-call(s32[8,4]{1,0:T(8,128)S(1)} %copy.17.columns, bf16[8,4,128,128]{3,2,1,0:T(8,128)(2,1)S(1)} %bitcast.25, bf16[1024,512]{1,0:T(8,128)(2,1)S(1)} %get-tuple-element.91.pick, bf16[1024,512]{1,0:T(8,128)(2,1)S(1)} %get-tuple-element.98.place, ...), custom_call_target="tpu_custom_call" | custom-call | flops 1760000000 | bytes 1048576 | tf_op jit(solution)/shard_map/middle/pallas_call | solution.py:279
  58.9 2.1 %collective-permute-start.9 = (f32[64,128]{1,0:T(8,128)S(1)}, f32[64,128]{1,0:T(8,128)S(1)}, u32[]{:S(2)}, u32[]{:S(2)}) collective-permute-start(f32[64,128]{1,0:T(8,128)S(1)} %get-tuple-element.106), channel_id=1, source_target_pairs={{16,32},{48,64},{80,96},{112,128},{144,160},{176,192},{208,224},{2... | collective-permute-start | bytes 98312 | tf_op jit(solution)/shard_map/ppermute | solution.py:337
  61.0 1.1 collective-permute-start.10
  62.1 1.4 %collective-permute-start.12 = (f32[64,128]{1,0:T(8,128)S(1)}, f32[64,128]{1,0:T(8,128)S(1)}, u32[]{:S(2)}, u32[]{:S(2)}) collective-permute-start(f32[64,128]{1,0:T(8,128)S(1)} %get-tuple-element.109), channel_id=1, source_target_pairs={{0,1},{1,0},{2,3},{3,2},{4,5},{5,4},{6,7},{7,6},{8,9},{9,8},{10,11... | collective-permute-start | bytes 98312 | tf_op jit(solution)/shard_map/ppermute | solution.py:340
  63.5 1.8 %finish.1 = (f32[64,1024]{1,0:T(8,128)S(1)}, f32[64,1024]{1,0:T(8,128)S(1)}, f32[48,128]{1,0:T(8,128)S(1)}) custom-call(s32[8,4]{1,0:T(8,128)S(1)} %copy.17.columns, bf16[8,4,128,128]{3,2,1,0:T(8,128)(2,1)S(1)} %bitcast.26, bf16[1024,512]{1,0:T(8,128)(2,1)S(1)} %get-tuple-element.98.place, f32[64,1024]{1,0:T(8,128)S(1)} %get-tuple-element.93.residual, ...), custom_call_target="tpu_custom_call" | custom-call | flops 1760000000 | bytes 1048576 | tf_op jit(solution)/shard_map/finish/pallas_call | solution.py:279
  66.3 14.3 %all_to_all.22.gathered = f32[16,48,128]{2,1,0:T(8,128)S(1)} all-to-all(f32[16,48,128]{2,1,0:T(8,128)S(1)} %get-tuple-element.114), channel_id=1, replica_groups=mesh['row'=16,'col'=16] {'row'}, dimensions={0} | all-to-all | bytes 786432 | tf_op jit(solution)/shard_map/all_to_all | solution.py:353
  80.7 1.6 %coarse.3 = (f32[8,48,128]{2,1,0:T(8,128)S(1)}, f32[8,48,128]{2,1,0:T(8,128)S(1)}) custom-call(s32[1]{0:T(128)} %bitcast.8.core, f32[16,48,128]{2,1,0:T(8,128)S(1)} %all_to_all.22.gathered, bf16[1536,1536]{1,0:T(8,128)(2,1)S(1)} %bitcast.23), custom_call_target="tpu_custom_call" | custom-call | flops 1760000000 | bytes 1048576 | tf_op jit(solution)/shard_map/coarse/pallas_call | solution.py:279
  82.2 1.8 %collective-permute-start.13 = (f32[8,48,128]{2,1,0:T(8,128)S(1)}, f32[8,48,128]{2,1,0:T(8,128)S(1)}, u32[]{:S(2)}, u32[]{:S(2)}) collective-permute-start(f32[8,48,128]{2,1,0:T(8,128)S(1)} %get-tuple-element.116), channel_id=1, source_target_pairs={{0,1},{1,0},{2,3},{3,2},{4,5},{5,4},{6,7},{7,6},{8,9},{9,8},{10,11... | collective-permute-start | bytes 589832 | tf_op jit(solution)/shard_map/ppermute | solution.py:358
  84.1 1.1 collective-permute-done.13
  85.2 12.2 %all_to_all.23.parts = f32[8,48,128]{2,1,0:T(8,128)S(1)} all-to-all(f32[8,48,128]{2,1,0:T(8,128)S(1)} %add.20), channel_id=1, replica_groups={{0,2,4,6,8,10,12,14},{1,3,5,7,9,11,13,15},{16,18,20,22,24,26,28,30},{17..., dimensions={0} | all-to-all | bytes 393216 | tf_op jit(solution)/shard_map/all_to_all | solution.py:365
  98.6 2.4 %collective-permute-start.15 = (f32[64,128]{1,0:T(8,128)S(1)}, f32[64,128]{1,0:T(8,128)S(1)}, u32[]{:S(2)}, u32[]{:S(2)}) collective-permute-start(f32[64,128]{1,0:T(8,128)S(1)} %get-tuple-element.123), channel_id=1, source_target_pairs={{1,2},{3,4},{5,6},{7,8},{9,10},{11,12},{13,14},{15,0},{2,1},{4,3},... | collective-permute-start | bytes 98312 | tf_op jit(solution)/shard_map/ppermute | solution.py:338
  101.0 1.7 %reopen.1 = (f32[64,1024]{1,0:T(8,128)S(1)}, f32[64,1024]{1,0:T(8,128)S(1)}, f32[64,512]{1,0:T(8,128)S(1)}) custom-call(s32[8,4]{1,0:T(8,128)S(1)} %copy.17.columns, bf16[96,128]{1,0:T(8,128)(2,1)S(1)} %get-tuple-element.117.field, bf16[96,1024]{1,0:T(8,128)(2,1)S(1)} %get-tuple-element.79.modes, bf16[8,4,128,128]{3,2,1,0:T(8,128)(2,1)S(1)} %bitcast.27, ...), custom_call_target="tpu_custom_call" | custom-call | flops 1760000000 | bytes 1048576 | tf_op jit(solution)/shard_map/reopen/pallas_call | solution.py:279
  105.1 4.0 %collective-permute-start.18 = (f32[64,128]{1,0:T(8,128)S(1)}, f32[64,128]{1,0:T(8,128)S(1)}, u32[]{:S(2)}, u32[]{:S(2)}) collective-permute-start(f32[64,128]{1,0:T(8,128)S(1)} %get-tuple-element.129), channel_id=1, source_target_pairs={{16,32},{48,64},{80,96},{112,128},{144,160},{176,192},{208,224},{2... | collective-permute-start | bytes 98312 | tf_op jit(solution)/shard_map/ppermute | solution.py:337
  109.1 1.1 collective-permute-start.19
  110.2 1.4 %collective-permute-start.21 = (f32[64,128]{1,0:T(8,128)S(1)}, f32[64,128]{1,0:T(8,128)S(1)}, u32[]{:S(2)}, u32[]{:S(2)}) collective-permute-start(f32[64,128]{1,0:T(8,128)S(1)} %get-tuple-element.132), channel_id=1, source_target_pairs={{0,1},{1,0},{2,3},{3,2},{4,5},{5,4},{6,7},{7,6},{8,9},{9,8},{10,11... | collective-permute-start | bytes 98312 | tf_op jit(solution)/shard_map/ppermute | solution.py:340
  111.5 1.6 %middle.3 = (f32[64,1024]{1,0:T(8,128)S(1)}, f32[64,512]{1,0:T(8,128)S(1)}) custom-call(s32[8,4]{1,0:T(8,128)S(1)} %copy.17.columns, bf16[8,4,128,128]{3,2,1,0:T(8,128)(2,1)S(1)} %bitcast.28, bf16[1024,512]{1,0:T(8,128)(2,1)S(1)} %get-tuple-element.91.pick, bf16[1024,512]{1,0:T(8,128)(2,1)S(1)} %get-tuple-element.98.place, ...), custom_call_target="tpu_custom_call" | custom-call | flops 1760000000 | bytes 1048576 | tf_op jit(solution)/shard_map/middle/pallas_call | solution.py:279
  114.1 3.2 %collective-permute-start.22 = (f32[64,128]{1,0:T(8,128)S(1)}, f32[64,128]{1,0:T(8,128)S(1)}, u32[]{:S(2)}, u32[]{:S(2)}) collective-permute-start(f32[64,128]{1,0:T(8,128)S(1)} %get-tuple-element.137), channel_id=1, source_target_pairs={{16,32},{48,64},{80,96},{112,128},{144,160},{176,192},{208,224},{2... | collective-permute-start | bytes 98312 | tf_op jit(solution)/shard_map/ppermute | solution.py:337
  117.3 1.1 collective-permute-start.23
  118.4 1.4 %collective-permute-start.25 = (f32[64,128]{1,0:T(8,128)S(1)}, f32[64,128]{1,0:T(8,128)S(1)}, u32[]{:S(2)}, u32[]{:S(2)}) collective-permute-start(f32[64,128]{1,0:T(8,128)S(1)} %get-tuple-element.140), channel_id=1, source_target_pairs={{0,1},{1,0},{2,3},{3,2},{4,5},{5,4},{6,7},{7,6},{8,9},{9,8},{10,11... | collective-permute-start | bytes 98312 | tf_op jit(solution)/shard_map/ppermute | solution.py:340
  119.8 2.1 %finish_last.1 = (f32[64,1024]{1,0:T(8,128)}, f32[64,1024]{1,0:T(8,128)S(1)}) custom-call(s32[8,4]{1,0:T(8,128)S(1)} %copy.17.columns, bf16[8,4,128,128]{3,2,1,0:T(8,128)(2,1)S(1)} %bitcast.29, bf16[1024,512]{1,0:T(8,128)(2,1)S(1)} %get-tuple-element.98.place, f32[64,1024]{1,0:T(8,128)S(1)} %get-tuple-element.120.residual, ...), custom_call_target="tpu_custom_call" | custom-call | flops 1760000000 | bytes 1048576 | tf_op jit(solution)/shard_map/finish_last/pallas_call | solution.py:279
  121.9 1.8 %last.1 = f32[64,1024]{1,0:T(8,128)} custom-call(s32[4]{0:T(128)S(1)} %get-tuple-element.97.order, s32[4]{0:T(128)S(1)} %get-tuple-element.86.inside, f32[64,128]{1,0:T(8,128)S(1)} %collective-permute-done.22.l0, f32[64,128]{1,0:T(8,128)S(1)} %collective-permute-done.23.l1, f32[64,128]{1,0:T(8,128)S(1)} %collective-permute-done.24.l2, ...), custom_call_target="tpu_custom_call" | custom-call | flops 990000000 | bytes 1048576 | tf_op jit(solution)/shard_map/last/pallas_call | solution.py:279
  (71 shorter events, 11.6 us)
Async XLA Ops:
  0.7 18.2 %copy-start = (bf16[1536,1536]{1,0:T(8,128)(2,1)S(1)}, bf16[1536,1536]{1,0:T(8,128)(2,1)}, u32[]{:S(2)}) copy-start(bf16[1536,1536]{1,0:T(8,128)(2,1)} %inverse.3) | copy-start | bytes 14155780
  2.2 20.2 %copy-start.5 = (s32[1,1,4,128]{3,2,1,0:T(4,128)S(1)}, s32[1,1,4,128]{3,2,1,0:T(4,128)}, u32[]{:S(2)}) copy-start(s32[1,1,4,128]{3,2,1,0:T(4,128)} %param.16) | copy-start | bytes 6148
  20.4 20.8 %copy-start.7 = (s32[1,1,8,4]{2,3,1,0:T(4,128)S(1)}, s32[1,1,8,4]{2,3,1,0:T(4,128)}, u32[]{:S(2)}) copy-start(s32[1,1,8,4]{2,3,1,0:T(4,128)} %param.14) | copy-start | bytes 388
  20.5 24.2 %copy-start.1 = (bf16[1,1,8,4,128,128]{5,4,3,2,1,0:T(8,128)(2,1)S(1)}, bf16[1,1,8,4,128,128]{5,4,3,2,1,0:T(8,128)(2,1)}, u32[]{:S(2)}) copy-start(bf16[1,1,8,4,128,128]{5,4,3,2,1,0:T(8,128)(2,1)} %param.13) | copy-start | bytes 3145732
  20.5 3.0 %collective-permute-start = (f32[8,48,128]{2,1,0:T(8,128)S(1)}, f32[8,48,128]{2,1,0:T(8,128)S(1)}, u32[]{:S(2)}, u32[]{:S(2)}) collective-permute-start(f32[8,48,128]{2,1,0:T(8,128)S(1)} %get-tuple-element.77), channel_id=1, source_target_pairs={{0,1},{1,0},{2,3},{3,2},{4,5},{5,4},{6,7},{7,6},{8,9},{9,8},{10,11... | collective-permute-start | bytes 589832 | tf_op jit(solution)/shard_map/ppermute | solution.py:358
  41.3 6.1 %collective-permute-start.1 = (f32[64,128]{1,0:T(8,128)S(1)}, f32[64,128]{1,0:T(8,128)S(1)}, u32[]{:S(2)}, u32[]{:S(2)}) collective-permute-start(f32[64,128]{1,0:T(8,128)S(1)} %get-tuple-element.87), channel_id=1, source_target_pairs={{16,32},{48,64},{80,96},{112,128},{144,160},{176,192},{208,224},{2... | collective-permute-start | bytes 98312 | tf_op jit(solution)/shard_map/ppermute | solution.py:337
  42.3 5.2 %collective-permute-start.2 = (f32[64,128]{1,0:T(8,128)S(1)}, f32[64,128]{1,0:T(8,128)S(1)}, u32[]{:S(2)}, u32[]{:S(2)}) collective-permute-start(f32[64,128]{1,0:T(8,128)S(1)} %get-tuple-element.88), channel_id=1, source_target_pairs={{1,2},{3,4},{5,6},{7,8},{9,10},{11,12},{13,14},{15,0},{2,1},{4,3},... | collective-permute-start | bytes 98312 | tf_op jit(solution)/shard_map/ppermute | solution.py:338
  44.7 3.1 %collective-permute-start.3 = (f32[64,128]{1,0:T(8,128)S(1)}, f32[64,128]{1,0:T(8,128)S(1)}, u32[]{:S(2)}, u32[]{:S(2)}) collective-permute-start(f32[64,128]{1,0:T(8,128)S(1)} %get-tuple-element.89), channel_id=1, source_target_pairs={{0,16},{16,0},{32,48},{48,32},{64,80},{80,64},{96,112},{112,96},{1... | collective-permute-start | bytes 98312 | tf_op jit(solution)/shard_map/ppermute | solution.py:339
  44.7 3.1 %collective-permute-start.4 = (f32[64,128]{1,0:T(8,128)S(1)}, f32[64,128]{1,0:T(8,128)S(1)}, u32[]{:S(2)}, u32[]{:S(2)}) collective-permute-start(f32[64,128]{1,0:T(8,128)S(1)} %get-tuple-element.90), channel_id=1, source_target_pairs={{0,1},{1,0},{2,3},{3,2},{4,5},{5,4},{6,7},{7,6},{8,9},{9,8},{10,11... | collective-permute-start | bytes 98312 | tf_op jit(solution)/shard_map/ppermute | solution.py:340
  48.7 9.1 %collective-permute-start.5 = (f32[64,128]{1,0:T(8,128)S(1)}, f32[64,128]{1,0:T(8,128)S(1)}, u32[]{:S(2)}, u32[]{:S(2)}) collective-permute-start(f32[64,128]{1,0:T(8,128)S(1)} %get-tuple-element.99), channel_id=1, source_target_pairs={{16,32},{48,64},{80,96},{112,128},{144,160},{176,192},{208,224},{2... | collective-permute-start | bytes 98312 | tf_op jit(solution)/shard_map/ppermute | solution.py:337
  52.7 5.2 %collective-permute-start.6 = (f32[64,128]{1,0:T(8,128)S(1)}, f32[64,128]{1,0:T(8,128)S(1)}, u32[]{:S(2)}, u32[]{:S(2)}) collective-permute-start(f32[64,128]{1,0:T(8,128)S(1)} %get-tuple-element.100), channel_id=1, source_target_pairs={{1,2},{3,4},{5,6},{7,8},{9,10},{11,12},{13,14},{15,0},{2,1},{4,3},... | collective-permute-start | bytes 98312 | tf_op jit(solution)/shard_map/ppermute | solution.py:338
  53.8 4.1 %collective-permute-start.7 = (f32[64,128]{1,0:T(8,128)S(1)}, f32[64,128]{1,0:T(8,128)S(1)}, u32[]{:S(2)}, u32[]{:S(2)}) collective-permute-start(f32[64,128]{1,0:T(8,128)S(1)} %get-tuple-element.101), channel_id=1, source_target_pairs={{0,16},{16,0},{32,48},{48,32},{64,80},{80,64},{96,112},{112,96},{1... | collective-permute-start | bytes 98312 | tf_op jit(solution)/shard_map/ppermute | solution.py:339
  53.8 4.1 %collective-permute-start.8 = (f32[64,128]{1,0:T(8,128)S(1)}, f32[64,128]{1,0:T(8,128)S(1)}, u32[]{:S(2)}, u32[]{:S(2)}) collective-permute-start(f32[64,128]{1,0:T(8,128)S(1)} %get-tuple-element.102), channel_id=1, source_target_pairs={{0,1},{1,0},{2,3},{3,2},{4,5},{5,4},{6,7},{7,6},{8,9},{9,8},{10,11... | collective-permute-start | bytes 98312 | tf_op jit(solution)/shard_map/ppermute | solution.py:340
  57.9 22.7 %slice-start = ((s8[4718592]{0:T(1024)(128)(4,1)}), s8[4194304]{0:T(1024)(128)(4,1)S(1)}, s32[]{:S(2)}) async-start(s8[4718592]{0:T(1024)(128)(4,1)} %bitcast.22), calls=%async_computation.4 | async-start | bytes 8388608
  58.9 6.4 %collective-permute-start.9 = (f32[64,128]{1,0:T(8,128)S(1)}, f32[64,128]{1,0:T(8,128)S(1)}, u32[]{:S(2)}, u32[]{:S(2)}) collective-permute-start(f32[64,128]{1,0:T(8,128)S(1)} %get-tuple-element.106), channel_id=1, source_target_pairs={{16,32},{48,64},{80,96},{112,128},{144,160},{176,192},{208,224},{2... | collective-permute-start | bytes 98312 | tf_op jit(solution)/shard_map/ppermute | solution.py:337
  61.0 4.3 %collective-permute-start.10 = (f32[64,128]{1,0:T(8,128)S(1)}, f32[64,128]{1,0:T(8,128)S(1)}, u32[]{:S(2)}, u32[]{:S(2)}) collective-permute-start(f32[64,128]{1,0:T(8,128)S(1)} %get-tuple-element.107), channel_id=1, source_target_pairs={{1,2},{3,4},{5,6},{7,8},{9,10},{11,12},{13,14},{15,0},{2,1},{4,3},... | collective-permute-start | bytes 98312 | tf_op jit(solution)/shard_map/ppermute | solution.py:338
  62.1 3.2 %collective-permute-start.11 = (f32[64,128]{1,0:T(8,128)S(1)}, f32[64,128]{1,0:T(8,128)S(1)}, u32[]{:S(2)}, u32[]{:S(2)}) collective-permute-start(f32[64,128]{1,0:T(8,128)S(1)} %get-tuple-element.108), channel_id=1, source_target_pairs={{0,16},{16,0},{32,48},{48,32},{64,80},{80,64},{96,112},{112,96},{1... | collective-permute-start | bytes 98312 | tf_op jit(solution)/shard_map/ppermute | solution.py:339
  62.1 3.2 %collective-permute-start.12 = (f32[64,128]{1,0:T(8,128)S(1)}, f32[64,128]{1,0:T(8,128)S(1)}, u32[]{:S(2)}, u32[]{:S(2)}) collective-permute-start(f32[64,128]{1,0:T(8,128)S(1)} %get-tuple-element.109), channel_id=1, source_target_pairs={{0,1},{1,0},{2,3},{3,2},{4,5},{5,4},{6,7},{7,6},{8,9},{9,8},{10,11... | collective-permute-start | bytes 98312 | tf_op jit(solution)/shard_map/ppermute | solution.py:340
  63.4 17.2 %slice-start.1 = ((s8[4718592]{0:T(1024)(128)(4,1)}), s8[524288]{0:T(1024)(128)(4,1)S(1)}, s32[]{:S(2)}) async-start(s8[4718592]{0:T(1024)(128)(4,1)} %bitcast.22), calls=%async_computation.5 | async-start | bytes 1048576
  82.2 2.9 %collective-permute-start.13 = (f32[8,48,128]{2,1,0:T(8,128)S(1)}, f32[8,48,128]{2,1,0:T(8,128)S(1)}, u32[]{:S(2)}, u32[]{:S(2)}) collective-permute-start(f32[8,48,128]{2,1,0:T(8,128)S(1)} %get-tuple-element.116), channel_id=1, source_target_pairs={{0,1},{1,0},{2,3},{3,2},{4,5},{5,4},{6,7},{7,6},{8,9},{9,8},{10,11... | collective-permute-start | bytes 589832 | tf_op jit(solution)/shard_map/ppermute | solution.py:358
  97.6 6.2 %collective-permute-start.14 = (f32[64,128]{1,0:T(8,128)S(1)}, f32[64,128]{1,0:T(8,128)S(1)}, u32[]{:S(2)}, u32[]{:S(2)}) collective-permute-start(f32[64,128]{1,0:T(8,128)S(1)} %get-tuple-element.122), channel_id=1, source_target_pairs={{16,32},{48,64},{80,96},{112,128},{144,160},{176,192},{208,224},{2... | collective-permute-start | bytes 98312 | tf_op jit(solution)/shard_map/ppermute | solution.py:337
  98.6 5.2 %collective-permute-start.15 = (f32[64,128]{1,0:T(8,128)S(1)}, f32[64,128]{1,0:T(8,128)S(1)}, u32[]{:S(2)}, u32[]{:S(2)}) collective-permute-start(f32[64,128]{1,0:T(8,128)S(1)} %get-tuple-element.123), channel_id=1, source_target_pairs={{1,2},{3,4},{5,6},{7,8},{9,10},{11,12},{13,14},{15,0},{2,1},{4,3},... | collective-permute-start | bytes 98312 | tf_op jit(solution)/shard_map/ppermute | solution.py:338
  101.0 3.1 %collective-permute-start.16 = (f32[64,128]{1,0:T(8,128)S(1)}, f32[64,128]{1,0:T(8,128)S(1)}, u32[]{:S(2)}, u32[]{:S(2)}) collective-permute-start(f32[64,128]{1,0:T(8,128)S(1)} %get-tuple-element.124), channel_id=1, source_target_pairs={{0,16},{16,0},{32,48},{48,32},{64,80},{80,64},{96,112},{112,96},{1... | collective-permute-start | bytes 98312 | tf_op jit(solution)/shard_map/ppermute | solution.py:339
  101.0 3.1 %collective-permute-start.17 = (f32[64,128]{1,0:T(8,128)S(1)}, f32[64,128]{1,0:T(8,128)S(1)}, u32[]{:S(2)}, u32[]{:S(2)}) collective-permute-start(f32[64,128]{1,0:T(8,128)S(1)} %get-tuple-element.125), channel_id=1, source_target_pairs={{0,1},{1,0},{2,3},{3,2},{4,5},{5,4},{6,7},{7,6},{8,9},{9,8},{10,11... | collective-permute-start | bytes 98312 | tf_op jit(solution)/shard_map/ppermute | solution.py:340
  105.1 8.1 %collective-permute-start.18 = (f32[64,128]{1,0:T(8,128)S(1)}, f32[64,128]{1,0:T(8,128)S(1)}, u32[]{:S(2)}, u32[]{:S(2)}) collective-permute-start(f32[64,128]{1,0:T(8,128)S(1)} %get-tuple-element.129), channel_id=1, source_target_pairs={{16,32},{48,64},{80,96},{112,128},{144,160},{176,192},{208,224},{2... | collective-permute-start | bytes 98312 | tf_op jit(solution)/shard_map/ppermute | solution.py:337
  109.1 4.1 %collective-permute-start.19 = (f32[64,128]{1,0:T(8,128)S(1)}, f32[64,128]{1,0:T(8,128)S(1)}, u32[]{:S(2)}, u32[]{:S(2)}) collective-permute-start(f32[64,128]{1,0:T(8,128)S(1)} %get-tuple-element.130), channel_id=1, source_target_pairs={{1,2},{3,4},{5,6},{7,8},{9,10},{11,12},{13,14},{15,0},{2,1},{4,3},... | collective-permute-start | bytes 98312 | tf_op jit(solution)/shard_map/ppermute | solution.py:338
  110.2 3.1 %collective-permute-start.20 = (f32[64,128]{1,0:T(8,128)S(1)}, f32[64,128]{1,0:T(8,128)S(1)}, u32[]{:S(2)}, u32[]{:S(2)}) collective-permute-start(f32[64,128]{1,0:T(8,128)S(1)} %get-tuple-element.131), channel_id=1, source_target_pairs={{0,16},{16,0},{32,48},{48,32},{64,80},{80,64},{96,112},{112,96},{1... | collective-permute-start | bytes 98312 | tf_op jit(solution)/shard_map/ppermute | solution.py:339
  110.2 3.1 %collective-permute-start.21 = (f32[64,128]{1,0:T(8,128)S(1)}, f32[64,128]{1,0:T(8,128)S(1)}, u32[]{:S(2)}, u32[]{:S(2)}) collective-permute-start(f32[64,128]{1,0:T(8,128)S(1)} %get-tuple-element.132), channel_id=1, source_target_pairs={{0,1},{1,0},{2,3},{3,2},{4,5},{5,4},{6,7},{7,6},{8,9},{9,8},{10,11... | collective-permute-start | bytes 98312 | tf_op jit(solution)/shard_map/ppermute | solution.py:340
  114.1 7.7 %collective-permute-start.22 = (f32[64,128]{1,0:T(8,128)S(1)}, f32[64,128]{1,0:T(8,128)S(1)}, u32[]{:S(2)}, u32[]{:S(2)}) collective-permute-start(f32[64,128]{1,0:T(8,128)S(1)} %get-tuple-element.137), channel_id=1, source_target_pairs={{16,32},{48,64},{80,96},{112,128},{144,160},{176,192},{208,224},{2... | collective-permute-start | bytes 98312 | tf_op jit(solution)/shard_map/ppermute | solution.py:337
  117.3 4.5 %collective-permute-start.23 = (f32[64,128]{1,0:T(8,128)S(1)}, f32[64,128]{1,0:T(8,128)S(1)}, u32[]{:S(2)}, u32[]{:S(2)}) collective-permute-start(f32[64,128]{1,0:T(8,128)S(1)} %get-tuple-element.138), channel_id=1, source_target_pairs={{1,2},{3,4},{5,6},{7,8},{9,10},{11,12},{13,14},{15,0},{2,1},{4,3},... | collective-permute-start | bytes 98312 | tf_op jit(solution)/shard_map/ppermute | solution.py:338
  118.4 3.4 %collective-permute-start.24 = (f32[64,128]{1,0:T(8,128)S(1)}, f32[64,128]{1,0:T(8,128)S(1)}, u32[]{:S(2)}, u32[]{:S(2)}) collective-permute-start(f32[64,128]{1,0:T(8,128)S(1)} %get-tuple-element.139), channel_id=1, source_target_pairs={{0,16},{16,0},{32,48},{48,32},{64,80},{80,64},{96,112},{112,96},{1... | collective-permute-start | bytes 98312 | tf_op jit(solution)/shard_map/ppermute | solution.py:339
  118.4 3.5 %collective-permute-start.25 = (f32[64,128]{1,0:T(8,128)S(1)}, f32[64,128]{1,0:T(8,128)S(1)}, u32[]{:S(2)}, u32[]{:S(2)}) collective-permute-start(f32[64,128]{1,0:T(8,128)S(1)} %get-tuple-element.140), channel_id=1, source_target_pairs={{0,1},{1,0},{2,3},{3,2},{4,5},{5,4},{6,7},{7,6},{8,9},{9,8},{10,11... | collective-permute-start | bytes 98312 | tf_op jit(solution)/shard_map/ppermute | solution.py:340
  (4 other events, 22.3 us)

commit v2 on v1

--- a/solution.py
+++ b/solution.py
@@ -105,7 +105,9 @@
     rim_modes[...] = dot(modes[...], pick[...], NN).astype(BF16)
 
 
-def link_kernel(order, send, receive, pick, real_shift, imag_shift, cross, coef, rim_coef):
+def link_kernel(order, send, receive, pick, real_shift, imag_shift, coupling, cross, coef, rim_coef, links):
+    for slot in range(4):
+        links[slot] = coupling[order[slot]].astype(F32).T.astype(BF16)
     rows = [receive[pl.ds(order[slot], 1), :] for slot in range(4)]
     targets = jnp.concatenate(rows + rows, axis=0).T
     for slot in range(4):
@@ -131,15 +133,6 @@
     place_modes[...] = dot(modes[...], place[...], NN).astype(BF16)
 
 
-def coarse_product(wide, core, keep, give, z):
-    pair = []
-    for m in range(2):
-        base = m * MODES
-        pair.append(pack_modes(wide[base : base + HALF], wide[base + HALF : base + MODES]))
-    keep[z] = jnp.where(core == 0, pair[0], pair[1])
-    give[z] = jnp.where(core == 0, pair[1], pair[0])
-
-
 def gather_column(gathered, column):
     for k in range(N):
         first, second = unpack_modes(gathered[k])
@@ -147,19 +140,23 @@
         column[k * MODES + HALF : (k + 1) * MODES, :] = second
 
 
-CHUNK = 4 * MODES
-
-
-def coarse_chunk(k, inverse, column, core, keep, give):
-    wide = dot(inverse[k * CHUNK : (k + 1) * CHUNK, :], column[...], NN)
-    for m in range(2):
-        coarse_product(wide[2 * m * MODES : (2 * m + 2) * MODES], core, keep, give, 2 * k + m)
-
-
-def coarse_kernel(core, gathered, inverse, keep, give, column):
+def half_product(parity, inverse, column, out):
+    for k in range(0, N // 2, 4):
+        starts = [pl.multiple_of((2 * z + parity) * MODES, MODES) for z in range(k, k + 4)]
+        rows = jnp.concatenate([inverse[pl.ds(start, MODES), :] for start in starts], axis=0)
+        wide = dot(rows, column[...], NN)
+        for z in range(4):
+            base = z * MODES
+            out[k + z] = pack_modes(wide[base : base + HALF], wide[base + HALF : base + MODES])
+
+
+def give_kernel(core, gathered, inverse, give, column):
     gather_column(gathered, column)
-    for k in range(4):
-        coarse_chunk(k, inverse, column, core[0], keep, give)
+    half_product(1 - core[0], inverse, column, give)
+
+
+def keep_kernel(core, column, inverse, keep):
+    half_product(core[0], inverse, column, keep)
 
 
 def start_kernel(parts, rim_modes, field, *rims):
@@ -227,30 +224,30 @@
     rest[...] = value
 
 
-def coupled(order, inside, links, coupling):
+def coupled(inside, rims, links):
     pieces = []
     for slot in range(4):
-        offered = jnp.where(inside[slot] > 0, links[slot][...], 0.0)
-        pieces.append(fold_rows(dot(stacked(offered), coupling[order[slot]], NT)))
+        offered = jnp.where(inside[slot] > 0, rims[slot][...], 0.0)
+        pieces.append(fold_rows(dot(stacked(offered), links[slot], NN)))
     return stacked(jnp.concatenate(pieces, axis=1))
 
 
-def sweep_kernel(order, inside, l0, l1, l2, l3, coupling, cross, rim_rest, rim_coef, terms, *rims):
-    value = coupled(order, inside, (l0, l1, l2, l3), coupling)
+def sweep_kernel(inside, l0, l1, l2, l3, links, cross, rim_rest, rim_coef, terms, *rims):
+    value = coupled(inside, (l0, l1, l2, l3), links)
     terms[...] = value
     rest = rim_rest[...] - fold_rows(dot(value, cross[...], NN))
     put_rims(relax(rest, rim_coef[0:1, :], rim_coef[1:2, :]), rims)
 
 
-def close_kernel(order, inside, l0, l1, l2, l3, coupling, place_modes, projected, terms, out):
-    value = coupled(order, inside, (l0, l1, l2, l3), coupling)
+def close_kernel(inside, l0, l1, l2, l3, links, place_modes, projected, terms, out):
+    value = coupled(inside, (l0, l1, l2, l3), links)
     terms[...] = value
     wide = dot(place_modes[...], value, NT)
     spread(projected[...] - pack_modes(wide[:HALF], wide[HALF:]), out)
 
 
-def last_kernel(order, inside, l0, l1, l2, l3, coupling, place, rest, residual, value, sems):
-    terms = coupled(order, inside, (l0, l1, l2, l3), coupling)
+def last_kernel(inside, l0, l1, l2, l3, links, place, rest, residual, value, sems):
+    terms = coupled(inside, (l0, l1, l2, l3), links)
     copies = []
     for k in range(4):
         lanes = pl.ds(k * 256, 256)
@@ -289,7 +286,18 @@
 
 
 EVEN = [(k, k ^ 1) for k in range(N)]
-ODD = [(k, (k + 1) % N) for k in range(1, N, 2)] + [((k + 1) % N, k) for k in range(1, N, 2)]
+
+
+def odd(k):
+    return k - 1 if k % 2 == 0 else k + 1
+
+
+def permutation(partner):
+    return [(N * i + j, N * partner(i, j)[0] + partner(i, j)[1]) for i in range(N) for j in range(N)]
+
+
+ROW_ODD = permutation(lambda i, j: (i, j ^ 1) if i in (0, N - 1) else (odd(i), j))
+COL_ODD = permutation(lambda i, j: (i ^ 1, j) if j in (0, N - 1) else (i, odd(j)))
 SAME_CORE = [list(range(core, N, 2)) for core in range(2)]
 
 
@@ -310,7 +318,6 @@
     imag_shift = shift_imag.reshape(1, NE)
     tiles = local_tiles[0, 0]
     columns = tile_columns[0, 0]
-    links = coupling[0, 0]
     send = send_edges[0, 0]
     receive = receive_edges[0, 0]
     modes = local_modes[0, 0]
@@ -334,14 +341,13 @@
 
     def exchange(rims):
         return [
-            lax.ppermute(rims[0], "row", ODD),
-            lax.ppermute(rims[1], "col", ODD),
+            lax.ppermute(rims[0], ("row", "col"), ROW_ODD),
+            lax.ppermute(rims[1], ("row", "col"), COL_ODD),
             lax.ppermute(rims[2], "row", EVEN),
             lax.ppermute(rims[3], "col", EVEN),
         ]
 
     tile_scratch = [pltpu.VMEM((NE // TILE, 2 * ROWS, TILE), BF16)]
-    column_scratch = pltpu.VMEM((N * MODES, TILE), BF16)
 
     packed, residual, modes = call(
         project_kernel, [spread_shape, field_shape, held((MODES, NE), BF16)], [HBM] * 2, [in_hbm(source), in_hbm(modes)],
@@ -351,13 +357,16 @@
 
     for repeat in range(OUTER):
         gathered = lax.all_to_all(packed, "row", 0, 0)
-        keep, give = call(
-            coarse_kernel, [half_shape] * 2, [SMEM, VMEM, VMEM], [core, gathered, coarse_inverse],
-            scratch=[column_scratch], us=1.6, name="coarse",
+        give, column = call(
+            give_kernel, [half_shape, held((N * MODES, TILE), BF16)], [SMEM, VMEM, VMEM], [core, gathered, coarse_inverse],
+            us=0.9, name="give",
+        )
+        (keep,) = call(
+            keep_kernel, [half_shape], [SMEM, VMEM, VMEM], [core, column, coarse_inverse], us=0.9, name="keep",
         )
         pair_sum = keep + lax.ppermute(give, "col", EVEN)
         if repeat == 0:
-            now, _ = lax.optimization_barrier((order, keep))
+            now, _ = lax.optimization_barrier((order, give))
             pick, rim_modes = call(
                 rim_kernel, [hot_shape, held((MODES, 4 * TILE), BF16)], [SMEM, VMEM, VMEM], [now, send, modes], name="rim"
             )
@@ -370,9 +379,9 @@
         if repeat == 0:
             now, _ = lax.optimization_barrier((order, field))
             columns = jnp.where(now[0] >= 0, columns, 0)
-            cross, coef, rim_coef = call(
-                link_kernel, [held((4 * TILE, 4 * TILE), BF16), held((8, NE)), held((8, 4 * TILE))],
-                [SMEM] + [VMEM] * 5, [now, send, receive, pick, real_shift, imag_shift], name="link", us=0.7,
+            cross, coef, rim_coef, links = call(
+                link_kernel, [held((4 * TILE, 4 * TILE), BF16), held((8, NE)), held((8, 4 * TILE)), held((4, TILE, TILE), BF16)],
+                [SMEM] + [VMEM] * 6, [now, send, receive, pick, real_shift, imag_shift, coupling[0, 0]], name="link", us=0.7,
             )
             local, rim_rest = call(
                 open_kernel, [field_shape, rim_shape], [SMEM] + [VMEM] * 5, [columns, field, modes, tiles, pick, residual],
@@ -386,8 +395,8 @@
             )
         for sweep in range(2):
             terms, *rims = call(
-                sweep_kernel, [terms_shape] + rim_shapes, [SMEM, SMEM] + [VMEM] * 8,
-                [order, inside, *arrived, links, cross, rim_rest, rim_coef], us=0.9, name="sweep",
+                sweep_kernel, [terms_shape] + rim_shapes, [SMEM] + [VMEM] * 8,
+                [inside, *arrived, links, cross, rim_rest, rim_coef], us=0.9, name="sweep",
             )
             arrived = exchange(rims)
             if repeat == 0 and sweep == 0:
@@ -413,12 +422,12 @@
                 )
         if repeat + 1 < OUTER:
             terms, packed = call(
-                close_kernel, [terms_shape, spread_shape], [SMEM, SMEM] + [VMEM] * 7,
-                [order, inside, *arrived, links, place_modes, projected], us=0.9, name="close",
+                close_kernel, [terms_shape, spread_shape], [SMEM] + [VMEM] * 7,
+                [inside, *arrived, links, place_modes, projected], us=0.9, name="close",
             )
         else:
             (residual,) = call(
-                last_kernel, [shape((ROWS, NE))], [SMEM, SMEM] + [VMEM] * 7, [order, inside, *arrived, links, place, rest],
+                last_kernel, [shape((ROWS, NE))], [SMEM] + [VMEM] * 7, [inside, *arrived, links, place, rest],
                 us=0.9, name="last", out_specs=[HBM],
                 scratch=[pltpu.VMEM((ROWS, NE), F32), pltpu.SemaphoreType.DMA((4,))],
             )

time: 124 us -> 117 us (0.944)
  starting transfers between devices: 33.6 us -> 27.4 us
  waiting for transfers between devices: 3.15 us -> 0.29 us
  blocking collectives: 60.5 us -> 62.5 us
    ppermute x12, starting transfers between devices: 24.4 us -> 9.51 us  [the longest x6 6.7 us: exchange(): lax.ppermute(rims[0], ('row', 'col'), ROW_ODD)]
    ppermute x6, starting transfers between devices: 0.02 us -> 6.58 us  [exchange(): lax.ppermute(rims[2], 'row', EVEN)]
    all_to_all x2, blocking collectives: 29.6 us -> 31.2 us  [on_device(): parts = lax.all_to_all(pair_sum, 'col', 0, 0, axis_index_groups=SAME_CORE)]
    ppermute x12, waiting for transfers between devices: 1.3 us -> 0.03 us  [the longest x6 0.02 us: exchange(): lax.ppermute(rims[1], ('row', 'col'), COL_ODD)]
    pallas_call x20 -> x22, Pallas kernels: 25.2 us -> 25.4 us  [call(): pl.pallas_call(kernel, out_shape=list(out_shape), in_specs=in_specs, out_...]
  transfers between devices with their start and end apart: 26 -> 26, of which waited for: 5 -> 1; matrix products, arithmetic and copies ran while one was open for 0% -> 0% of each run, Pallas kernels for 11% -> 13%
where the time goes in v2:
time: 117 us
  blocking collectives  62.5 us (53%)
  starting transfers between devices  27.4 us (23%)
  Pallas kernels  25.4 us (22%)
  between operations  1.3 us (1%)
    all_to_all x2, blocking collectives, on_device(): gathered = lax.all_to_all(packed, 'row', 0, 0)  31.3 us
    all_to_all x2, blocking collectives, on_device(): parts = lax.all_to_all(pair_sum, 'col', 0, 0, axis_index_groups=SAME_CORE)  31.2 us
    pallas_call x22, Pallas kernels, call(): pl.pallas_call(kernel, out_shape=list(out_shape), in_specs=in_specs, out_...  25.4 us
    ppermute x6, starting transfers between devices, exchange(): lax.ppermute(rims[0], ('row', 'col'), ROW_ODD)  6.7 us
    ppermute x6, starting transfers between devices, exchange(): lax.ppermute(rims[3], 'col', EVEN)  6.65 us
    ppermute x6, starting transfers between devices, exchange(): lax.ppermute(rims[2], 'row', EVEN)  6.58 us
    ppermute x2, starting transfers between devices, on_device(): pair_sum = keep + lax.ppermute(give, 'col', EVEN)  4.67 us
    ppermute x6, starting transfers between devices, exchange(): lax.ppermute(rims[1], ('row', 'col'), COL_ODD)  2.8 us
  transfers between devices with their start and end apart: 26, of which 1 were waited for; matrix products, arithmetic and copies ran while one was open for 0% of the time, Pallas kernels for 13%

profile of v2, /device:TPU:1, one launch (start us, length us, event | category | flops | bytes accessed | tf_op | source)
XLA Modules:
  0.0 117.2 jit_solution(15742323890380689230)
XLA Ops:
  0.7 1.5 %project.1 = (f32[16,48,128]{2,1,0:T(8,128)S(1)}, f32[64,1024]{1,0:T(8,128)S(1)}, bf16[96,1024]{1,0:T(8,128)(2,1)S(1)}) custom-call(f32[64,1024]{1,0:T(8,128)} %bitcast.37, bf16[96,1024]{1,0:T(8,128)(2,1)} %bitcast.38), custom_call_target="tpu_custom_call" | custom-call | flops 8800000000 | bytes 1048576 | tf_op jit(solution)/shard_map/project/pallas_call | solution.py:276
  2.3 16.6 %all_to_all.20.gathered = f32[16,48,128]{2,1,0:T(8,128)S(1)} all-to-all(f32[16,48,128]{2,1,0:T(8,128)S(1)} %get-tuple-element.76), channel_id=1, replica_groups=mesh['row'=16,'col'=16] {'row'}, dimensions={0} | all-to-all | bytes 786432 | tf_op jit(solution)/shard_map/all_to_all | solution.py:359
  18.9 1.0 give.2
  19.8 1.9 %collective-permute-start = (f32[8,48,128]{2,1,0:T(8,128)S(1)}, f32[8,48,128]{2,1,0:T(8,128)S(1)}, u32[]{:S(2)}, u32[]{:S(2)}) collective-permute-start(f32[8,48,128]{2,1,0:T(8,128)S(1)} %get-tuple-element.78), channel_id=1, source_target_pairs={{0,1},{1,0},{2,3},{3,2},{4,5},{5,4},{6,7},{7,6},{8,9},{9,8},{10,11... | collective-permute-start | bytes 589832 | tf_op jit(solution)/shard_map/ppermute | solution.py:367
  22.6 1.0 rim.1
  23.7 18.8 %all_to_all.21.parts = f32[8,48,128]{2,1,0:T(8,128)S(1)} all-to-all(f32[8,48,128]{2,1,0:T(8,128)S(1)} %add.19), channel_id=1, replica_groups={{0,2,4,6,8,10,12,14},{1,3,5,7,9,11,13,15},{16,18,20,22,24,26,28,30},{17..., dimensions={0} | all-to-all | bytes 393216 | tf_op jit(solution)/shard_map/all_to_all | solution.py:374
  44.3 1.4 %collective-permute-start.4 = (f32[64,128]{1,0:T(8,128)S(1)}, f32[64,128]{1,0:T(8,128)S(1)}, u32[]{:S(2)}, u32[]{:S(2)}) collective-permute-start(f32[64,128]{1,0:T(8,128)S(1)} %get-tuple-element.91), channel_id=1, source_target_pairs={{0,1},{1,0},{2,3},{3,2},{4,5},{5,4},{6,7},{7,6},{8,9},{9,8},{10,11... | collective-permute-start | bytes 98312 | tf_op jit(solution)/shard_map/ppermute | solution.py:347
  45.7 1.4 %open.1 = (f32[64,1024]{1,0:T(8,128)S(1)}, f32[64,512]{1,0:T(8,128)S(1)}) custom-call(s32[8,4]{1,0:T(8,128)S(1)} %copy.17.columns, bf16[96,128]{1,0:T(8,128)(2,1)S(1)} %get-tuple-element.85.field, bf16[96,1024]{1,0:T(8,128)(2,1)S(1)} %get-tuple-element.80.modes, bf16[8,4,128,128]{3,2,1,0:T(8,128)(2,1)S(1)} %bitcast.24, ...), custom_call_target="tpu_custom_call" | custom-call | flops 1760000000 | bytes 1048576 | tf_op jit(solution)/shard_map/open/pallas_call | solution.py:276
  47.2 1.1 link.1
  49.3 1.0 collective-permute-start.6
  50.3 1.3 %collective-permute-start.7 = (f32[64,128]{1,0:T(8,128)S(1)}, f32[64,128]{1,0:T(8,128)S(1)}, u32[]{:S(2)}, u32[]{:S(2)}) collective-permute-start(f32[64,128]{1,0:T(8,128)S(1)} %get-tuple-element.103), channel_id=1, source_target_pairs={{0,16},{16,0},{32,48},{48,32},{64,80},{80,64},{96,112},{112,96},{1... | collective-permute-start | bytes 98312 | tf_op jit(solution)/shard_map/ppermute | solution.py:346
  52.4 1.0 place.1
  53.4 1.7 %middle.2 = (f32[64,1024]{1,0:T(8,128)S(1)}, f32[64,512]{1,0:T(8,128)S(1)}) custom-call(s32[8,4]{1,0:T(8,128)S(1)} %copy.17.columns, bf16[8,4,128,128]{3,2,1,0:T(8,128)(2,1)S(1)} %bitcast.25, bf16[1024,512]{1,0:T(8,128)(2,1)S(1)} %get-tuple-element.92.pick, bf16[1024,512]{1,0:T(8,128)(2,1)S(1)} %get-tuple-element.100.place, ...), custom_call_target="tpu_custom_call" | custom-call | flops 1760000000 | bytes 1048576 | tf_op jit(solution)/shard_map/middle/pallas_call | solution.py:276
  56.1 1.2 %collective-permute-start.9 = (f32[64,128]{1,0:T(8,128)S(1)}, f32[64,128]{1,0:T(8,128)S(1)}, u32[]{:S(2)}, u32[]{:S(2)}) collective-permute-start(f32[64,128]{1,0:T(8,128)S(1)} %get-tuple-element.108), channel_id=1, source_target_pairs={{0,1},{1,0},{2,3},{3,2},{4,5},{5,4},{6,7},{7,6},{8,9},{9,8},{10,11... | collective-permute-start | bytes 98312 | tf_op jit(solution)/shard_map/ppermute | solution.py:344
  57.5 2.7 %collective-permute-start.11 = (f32[64,128]{1,0:T(8,128)S(1)}, f32[64,128]{1,0:T(8,128)S(1)}, u32[]{:S(2)}, u32[]{:S(2)}) collective-permute-start(f32[64,128]{1,0:T(8,128)S(1)} %get-tuple-element.110), channel_id=1, source_target_pairs={{0,16},{16,0},{32,48},{48,32},{64,80},{80,64},{96,112},{112,96},{1... | collective-permute-start | bytes 98312 | tf_op jit(solution)/shard_map/ppermute | solution.py:346
  60.2 1.8 %finish.1 = (f32[64,1024]{1,0:T(8,128)S(1)}, f32[64,1024]{1,0:T(8,128)S(1)}, f32[48,128]{1,0:T(8,128)S(1)}) custom-call(s32[8,4]{1,0:T(8,128)S(1)} %copy.17.columns, bf16[8,4,128,128]{3,2,1,0:T(8,128)(2,1)S(1)} %bitcast.26, bf16[1024,512]{1,0:T(8,128)(2,1)S(1)} %get-tuple-element.100.place, f32[64,1024]{1,0:T(8,128)S(1)} %get-tuple-element.95.residual, ...), custom_call_target="tpu_custom_call" | custom-call | flops 1760000000 | bytes 1048576 | tf_op jit(solution)/shard_map/finish/pallas_call | solution.py:276
  62.0 1.0 close.1
  63.0 14.7 %all_to_all.22.gathered = f32[16,48,128]{2,1,0:T(8,128)S(1)} all-to-all(f32[16,48,128]{2,1,0:T(8,128)S(1)} %get-tuple-element.116), channel_id=1, replica_groups=mesh['row'=16,'col'=16] {'row'}, dimensions={0} | all-to-all | bytes 786432 | tf_op jit(solution)/shard_map/all_to_all | solution.py:359
  77.8 1.0 give.3
  78.7 2.8 %collective-permute-start.13 = (f32[8,48,128]{2,1,0:T(8,128)S(1)}, f32[8,48,128]{2,1,0:T(8,128)S(1)}, u32[]{:S(2)}, u32[]{:S(2)}) collective-permute-start(f32[8,48,128]{2,1,0:T(8,128)S(1)} %get-tuple-element.118), channel_id=1, source_target_pairs={{0,1},{1,0},{2,3},{3,2},{4,5},{5,4},{6,7},{7,6},{8,9},{9,8},{10,11... | collective-permute-start | bytes 589832 | tf_op jit(solution)/shard_map/ppermute | solution.py:367
  82.6 12.4 %all_to_all.23.parts = f32[8,48,128]{2,1,0:T(8,128)S(1)} all-to-all(f32[8,48,128]{2,1,0:T(8,128)S(1)} %add.20), channel_id=1, replica_groups={{0,2,4,6,8,10,12,14},{1,3,5,7,9,11,13,15},{16,18,20,22,24,26,28,30},{17..., dimensions={0} | all-to-all | bytes 393216 | tf_op jit(solution)/shard_map/all_to_all | solution.py:374
  95.3 1.5 %collective-permute-start.14 = (f32[64,128]{1,0:T(8,128)S(1)}, f32[64,128]{1,0:T(8,128)S(1)}, u32[]{:S(2)}, u32[]{:S(2)}) collective-permute-start(f32[64,128]{1,0:T(8,128)S(1)} %get-tuple-element.124), channel_id=1, source_target_pairs={{0,1},{1,0},{2,3},{3,2},{4,5},{5,4},{6,7},{7,6},{8,9},{9,8},{10,11... | collective-permute-start | bytes 98312 | tf_op jit(solution)/shard_map/ppermute | solution.py:344
  97.5 1.4 %collective-permute-start.17 = (f32[64,128]{1,0:T(8,128)S(1)}, f32[64,128]{1,0:T(8,128)S(1)}, u32[]{:S(2)}, u32[]{:S(2)}) collective-permute-start(f32[64,128]{1,0:T(8,128)S(1)} %get-tuple-element.127), channel_id=1, source_target_pairs={{0,1},{1,0},{2,3},{3,2},{4,5},{5,4},{6,7},{7,6},{8,9},{9,8},{10,11... | collective-permute-start | bytes 98312 | tf_op jit(solution)/shard_map/ppermute | solution.py:347
  98.9 1.7 %reopen.1 = (f32[64,1024]{1,0:T(8,128)S(1)}, f32[64,1024]{1,0:T(8,128)S(1)}, f32[64,512]{1,0:T(8,128)S(1)}) custom-call(s32[8,4]{1,0:T(8,128)S(1)} %copy.17.columns, bf16[96,128]{1,0:T(8,128)(2,1)S(1)} %get-tuple-element.119.field, bf16[96,1024]{1,0:T(8,128)(2,1)S(1)} %get-tuple-element.80.modes, bf16[8,4,128,128]{3,2,1,0:T(8,128)(2,1)S(1)} %bitcast.27, ...), custom_call_target="tpu_custom_call" | custom-call | flops 1760000000 | bytes 1048576 | tf_op jit(solution)/shard_map/reopen/pallas_call | solution.py:276
  102.5 1.0 collective-permute-start.19
  104.2 1.6 %collective-permute-start.21 = (f32[64,128]{1,0:T(8,128)S(1)}, f32[64,128]{1,0:T(8,128)S(1)}, u32[]{:S(2)}, u32[]{:S(2)}) collective-permute-start(f32[64,128]{1,0:T(8,128)S(1)} %get-tuple-element.134), channel_id=1, source_target_pairs={{0,1},{1,0},{2,3},{3,2},{4,5},{5,4},{6,7},{7,6},{8,9},{9,8},{10,11... | collective-permute-start | bytes 98312 | tf_op jit(solution)/shard_map/ppermute | solution.py:347
  105.8 1.6 %middle.3 = (f32[64,1024]{1,0:T(8,128)S(1)}, f32[64,512]{1,0:T(8,128)S(1)}) custom-call(s32[8,4]{1,0:T(8,128)S(1)} %copy.17.columns, bf16[8,4,128,128]{3,2,1,0:T(8,128)(2,1)S(1)} %bitcast.28, bf16[1024,512]{1,0:T(8,128)(2,1)S(1)} %get-tuple-element.92.pick, bf16[1024,512]{1,0:T(8,128)(2,1)S(1)} %get-tuple-element.100.place, ...), custom_call_target="tpu_custom_call" | custom-call | flops 1760000000 | bytes 1048576 | tf_op jit(solution)/shard_map/middle/pallas_call | solution.py:276
  108.5 2.3 %collective-permute-start.22 = (f32[64,128]{1,0:T(8,128)S(1)}, f32[64,128]{1,0:T(8,128)S(1)}, u32[]{:S(2)}, u32[]{:S(2)}) collective-permute-start(f32[64,128]{1,0:T(8,128)S(1)} %get-tuple-element.139), channel_id=1, source_target_pairs={{0,1},{1,0},{2,3},{3,2},{4,5},{5,4},{6,7},{7,6},{8,9},{9,8},{10,11... | collective-permute-start | bytes 98312 | tf_op jit(solution)/shard_map/ppermute | solution.py:344
  110.7 1.0 collective-permute-start.24
  111.8 1.4 %collective-permute-start.25 = (f32[64,128]{1,0:T(8,128)S(1)}, f32[64,128]{1,0:T(8,128)S(1)}, u32[]{:S(2)}, u32[]{:S(2)}) collective-permute-start(f32[64,128]{1,0:T(8,128)S(1)} %get-tuple-element.142), channel_id=1, source_target_pairs={{0,1},{1,0},{2,3},{3,2},{4,5},{5,4},{6,7},{7,6},{8,9},{9,8},{10,11... | collective-permute-start | bytes 98312 | tf_op jit(solution)/shard_map/ppermute | solution.py:347
  113.2 2.1 %finish_last.1 = (f32[64,1024]{1,0:T(8,128)}, f32[64,1024]{1,0:T(8,128)S(1)}) custom-call(s32[8,4]{1,0:T(8,128)S(1)} %copy.17.columns, bf16[8,4,128,128]{3,2,1,0:T(8,128)(2,1)S(1)} %bitcast.29, bf16[1024,512]{1,0:T(8,128)(2,1)S(1)} %get-tuple-element.100.place, f32[64,1024]{1,0:T(8,128)S(1)} %get-tuple-element.122.residual, ...), custom_call_target="tpu_custom_call" | custom-call | flops 1760000000 | bytes 1048576 | tf_op jit(solution)/shard_map/finish_last/pallas_call | solution.py:276
  115.3 1.8 %last.1 = f32[64,1024]{1,0:T(8,128)} custom-call(s32[4]{0:T(128)S(1)} %get-tuple-element.87.inside, f32[64,128]{1,0:T(8,128)S(1)} %collective-permute-done.22.l0, f32[64,128]{1,0:T(8,128)S(1)} %collective-permute-done.23.l1, f32[64,128]{1,0:T(8,128)S(1)} %collective-permute-done.24.l2, f32[64,128]{1,0:T(8,128)S(1)} %collective-permute-done.25.l3, ...), custom_call_target="tpu_custom_call" | custom-call | flops 990000000 | bytes 1048576 | tf_op jit(solution)/shard_map/last/pallas_call | solution.py:276
  (73 shorter events, 11.1 us)
Async XLA Ops:
  0.7 18.2 %copy-start = (bf16[1536,1536]{1,0:T(8,128)(2,1)S(1)}, bf16[1536,1536]{1,0:T(8,128)(2,1)}, u32[]{:S(2)}) copy-start(bf16[1536,1536]{1,0:T(8,128)(2,1)} %inverse.7) | copy-start | bytes 14155780
  19.8 3.8 %collective-permute-start = (f32[8,48,128]{2,1,0:T(8,128)S(1)}, f32[8,48,128]{2,1,0:T(8,128)S(1)}, u32[]{:S(2)}, u32[]{:S(2)}) collective-permute-start(f32[8,48,128]{2,1,0:T(8,128)S(1)} %get-tuple-element.78), channel_id=1, source_target_pairs={{0,1},{1,0},{2,3},{3,2},{4,5},{5,4},{6,7},{7,6},{8,9},{9,8},{10,11... | collective-permute-start | bytes 589832 | tf_op jit(solution)/shard_map/ppermute | solution.py:367
  22.6 20.2 %copy-start.7 = (s32[1,1,8,4]{2,3,1,0:T(4,128)S(1)}, s32[1,1,8,4]{2,3,1,0:T(4,128)}, u32[]{:S(2)}) copy-start(s32[1,1,8,4]{2,3,1,0:T(4,128)} %param.14) | copy-start | bytes 388
  22.6 23.1 %copy-start.1 = (bf16[1,1,8,4,128,128]{5,4,3,2,1,0:T(8,128)(2,1)S(1)}, bf16[1,1,8,4,128,128]{5,4,3,2,1,0:T(8,128)(2,1)}, u32[]{:S(2)}) copy-start(bf16[1,1,8,4,128,128]{5,4,3,2,1,0:T(8,128)(2,1)} %param.13) | copy-start | bytes 3145732
  42.5 4.7 %copy-start.6 = (s32[1,1,4,128]{3,2,1,0:T(4,128)S(1)}, s32[1,1,4,128]{3,2,1,0:T(4,128)}, u32[]{:S(2)}) copy-start(s32[1,1,4,128]{3,2,1,0:T(4,128)} %param.17) | copy-start | bytes 6148
  42.9 5.3 %collective-permute-start.1 = (f32[64,128]{1,0:T(8,128)S(1)}, f32[64,128]{1,0:T(8,128)S(1)}, u32[]{:S(2)}, u32[]{:S(2)}) collective-permute-start(f32[64,128]{1,0:T(8,128)S(1)} %get-tuple-element.88), channel_id=1, source_target_pairs={{0,1},{1,0},{2,3},{3,2},{4,5},{5,4},{6,7},{7,6},{8,9},{9,8},{10,11... | collective-permute-start | bytes 98312 | tf_op jit(solution)/shard_map/ppermute | solution.py:344
  43.6 4.6 %collective-permute-start.2 = (f32[64,128]{1,0:T(8,128)S(1)}, f32[64,128]{1,0:T(8,128)S(1)}, u32[]{:S(2)}, u32[]{:S(2)}) collective-permute-start(f32[64,128]{1,0:T(8,128)S(1)} %get-tuple-element.89), channel_id=1, source_target_pairs={{0,16},{1,2},{2,1},{3,4},{4,3},{5,6},{6,5},{7,8},{8,7},{9,10},{10,... | collective-permute-start | bytes 98312 | tf_op jit(solution)/shard_map/ppermute | solution.py:345
  43.9 4.4 %collective-permute-start.3 = (f32[64,128]{1,0:T(8,128)S(1)}, f32[64,128]{1,0:T(8,128)S(1)}, u32[]{:S(2)}, u32[]{:S(2)}) collective-permute-start(f32[64,128]{1,0:T(8,128)S(1)} %get-tuple-element.90), channel_id=1, source_target_pairs={{0,16},{16,0},{32,48},{48,32},{64,80},{80,64},{96,112},{112,96},{1... | collective-permute-start | bytes 98312 | tf_op jit(solution)/shard_map/ppermute | solution.py:346
  44.3 4.0 %collective-permute-start.4 = (f32[64,128]{1,0:T(8,128)S(1)}, f32[64,128]{1,0:T(8,128)S(1)}, u32[]{:S(2)}, u32[]{:S(2)}) collective-permute-start(f32[64,128]{1,0:T(8,128)S(1)} %get-tuple-element.91), channel_id=1, source_target_pairs={{0,1},{1,0},{2,3},{3,2},{4,5},{5,4},{6,7},{7,6},{8,9},{9,8},{10,11... | collective-permute-start | bytes 98312 | tf_op jit(solution)/shard_map/ppermute | solution.py:347
  49.2 6.0 %collective-permute-start.5 = (f32[64,128]{1,0:T(8,128)S(1)}, f32[64,128]{1,0:T(8,128)S(1)}, u32[]{:S(2)}, u32[]{:S(2)}) collective-permute-start(f32[64,128]{1,0:T(8,128)S(1)} %get-tuple-element.101), channel_id=1, source_target_pairs={{0,1},{1,0},{2,3},{3,2},{4,5},{5,4},{6,7},{7,6},{8,9},{9,8},{10,11... | collective-permute-start | bytes 98312 | tf_op jit(solution)/shard_map/ppermute | solution.py:344
  49.3 5.8 %collective-permute-start.6 = (f32[64,128]{1,0:T(8,128)S(1)}, f32[64,128]{1,0:T(8,128)S(1)}, u32[]{:S(2)}, u32[]{:S(2)}) collective-permute-start(f32[64,128]{1,0:T(8,128)S(1)} %get-tuple-element.102), channel_id=1, source_target_pairs={{0,16},{1,2},{2,1},{3,4},{4,3},{5,6},{6,5},{7,8},{8,7},{9,10},{10,... | collective-permute-start | bytes 98312 | tf_op jit(solution)/shard_map/ppermute | solution.py:345
  50.3 4.8 %collective-permute-start.7 = (f32[64,128]{1,0:T(8,128)S(1)}, f32[64,128]{1,0:T(8,128)S(1)}, u32[]{:S(2)}, u32[]{:S(2)}) collective-permute-start(f32[64,128]{1,0:T(8,128)S(1)} %get-tuple-element.103), channel_id=1, source_target_pairs={{0,16},{16,0},{32,48},{48,32},{64,80},{80,64},{96,112},{112,96},{1... | collective-permute-start | bytes 98312 | tf_op jit(solution)/shard_map/ppermute | solution.py:346
  51.6 3.5 %collective-permute-start.8 = (f32[64,128]{1,0:T(8,128)S(1)}, f32[64,128]{1,0:T(8,128)S(1)}, u32[]{:S(2)}, u32[]{:S(2)}) collective-permute-start(f32[64,128]{1,0:T(8,128)S(1)} %get-tuple-element.104), channel_id=1, source_target_pairs={{0,1},{1,0},{2,3},{3,2},{4,5},{5,4},{6,7},{7,6},{8,9},{9,8},{10,11... | collective-permute-start | bytes 98312 | tf_op jit(solution)/shard_map/ppermute | solution.py:347
  56.1 5.9 %collective-permute-start.9 = (f32[64,128]{1,0:T(8,128)S(1)}, f32[64,128]{1,0:T(8,128)S(1)}, u32[]{:S(2)}, u32[]{:S(2)}) collective-permute-start(f32[64,128]{1,0:T(8,128)S(1)} %get-tuple-element.108), channel_id=1, source_target_pairs={{0,1},{1,0},{2,3},{3,2},{4,5},{5,4},{6,7},{7,6},{8,9},{9,8},{10,11... | collective-permute-start | bytes 98312 | tf_op jit(solution)/shard_map/ppermute | solution.py:344
  57.3 4.7 %collective-permute-start.10 = (f32[64,128]{1,0:T(8,128)S(1)}, f32[64,128]{1,0:T(8,128)S(1)}, u32[]{:S(2)}, u32[]{:S(2)}) collective-permute-start(f32[64,128]{1,0:T(8,128)S(1)} %get-tuple-element.109), channel_id=1, source_target_pairs={{0,16},{1,2},{2,1},{3,4},{4,3},{5,6},{6,5},{7,8},{8,7},{9,10},{10,... | collective-permute-start | bytes 98312 | tf_op jit(solution)/shard_map/ppermute | solution.py:345
  57.5 4.6 %collective-permute-start.11 = (f32[64,128]{1,0:T(8,128)S(1)}, f32[64,128]{1,0:T(8,128)S(1)}, u32[]{:S(2)}, u32[]{:S(2)}) collective-permute-start(f32[64,128]{1,0:T(8,128)S(1)} %get-tuple-element.110), channel_id=1, source_target_pairs={{0,16},{16,0},{32,48},{48,32},{64,80},{80,64},{96,112},{112,96},{1... | collective-permute-start | bytes 98312 | tf_op jit(solution)/shard_map/ppermute | solution.py:346
  60.2 1.8 %collective-permute-start.12 = (f32[64,128]{1,0:T(8,128)S(1)}, f32[64,128]{1,0:T(8,128)S(1)}, u32[]{:S(2)}, u32[]{:S(2)}) collective-permute-start(f32[64,128]{1,0:T(8,128)S(1)} %get-tuple-element.111), channel_id=1, source_target_pairs={{0,1},{1,0},{2,3},{3,2},{4,5},{5,4},{6,7},{7,6},{8,9},{9,8},{10,11... | collective-permute-start | bytes 98312 | tf_op jit(solution)/shard_map/ppermute | solution.py:347
  60.2 17.6 %slice-start = ((s8[4718592]{0:T(1024)(128)(4,1)}), s8[4194304]{0:T(1024)(128)(4,1)S(1)}, s32[]{:S(2)}) async-start(s8[4718592]{0:T(1024)(128)(4,1)} %bitcast.21), calls=%async_computation.4 | async-start | bytes 8388608
  60.2 17.6 %slice-start.1 = ((s8[4718592]{0:T(1024)(128)(4,1)}), s8[524288]{0:T(1024)(128)(4,1)S(1)}, s32[]{:S(2)}) async-start(s8[4718592]{0:T(1024)(128)(4,1)} %bitcast.21), calls=%async_computation.5 | async-start | bytes 1048576
  78.7 3.8 %collective-permute-start.13 = (f32[8,48,128]{2,1,0:T(8,128)S(1)}, f32[8,48,128]{2,1,0:T(8,128)S(1)}, u32[]{:S(2)}, u32[]{:S(2)}) collective-permute-start(f32[8,48,128]{2,1,0:T(8,128)S(1)} %get-tuple-element.118), channel_id=1, source_target_pairs={{0,1},{1,0},{2,3},{3,2},{4,5},{5,4},{6,7},{7,6},{8,9},{9,8},{10,11... | collective-permute-start | bytes 589832 | tf_op jit(solution)/shard_map/ppermute | solution.py:367
  95.3 5.3 %collective-permute-start.14 = (f32[64,128]{1,0:T(8,128)S(1)}, f32[64,128]{1,0:T(8,128)S(1)}, u32[]{:S(2)}, u32[]{:S(2)}) collective-permute-start(f32[64,128]{1,0:T(8,128)S(1)} %get-tuple-element.124), channel_id=1, source_target_pairs={{0,1},{1,0},{2,3},{3,2},{4,5},{5,4},{6,7},{7,6},{8,9},{9,8},{10,11... | collective-permute-start | bytes 98312 | tf_op jit(solution)/shard_map/ppermute | solution.py:344
  96.8 3.9 %collective-permute-start.15 = (f32[64,128]{1,0:T(8,128)S(1)}, f32[64,128]{1,0:T(8,128)S(1)}, u32[]{:S(2)}, u32[]{:S(2)}) collective-permute-start(f32[64,128]{1,0:T(8,128)S(1)} %get-tuple-element.125), channel_id=1, source_target_pairs={{0,16},{1,2},{2,1},{3,4},{4,3},{5,6},{6,5},{7,8},{8,7},{9,10},{10,... | collective-permute-start | bytes 98312 | tf_op jit(solution)/shard_map/ppermute | solution.py:345
  97.1 3.6 %collective-permute-start.16 = (f32[64,128]{1,0:T(8,128)S(1)}, f32[64,128]{1,0:T(8,128)S(1)}, u32[]{:S(2)}, u32[]{:S(2)}) collective-permute-start(f32[64,128]{1,0:T(8,128)S(1)} %get-tuple-element.126), channel_id=1, source_target_pairs={{0,16},{16,0},{32,48},{48,32},{64,80},{80,64},{96,112},{112,96},{1... | collective-permute-start | bytes 98312 | tf_op jit(solution)/shard_map/ppermute | solution.py:346
  97.5 3.2 %collective-permute-start.17 = (f32[64,128]{1,0:T(8,128)S(1)}, f32[64,128]{1,0:T(8,128)S(1)}, u32[]{:S(2)}, u32[]{:S(2)}) collective-permute-start(f32[64,128]{1,0:T(8,128)S(1)} %get-tuple-element.127), channel_id=1, source_target_pairs={{0,1},{1,0},{2,3},{3,2},{4,5},{5,4},{6,7},{7,6},{8,9},{9,8},{10,11... | collective-permute-start | bytes 98312 | tf_op jit(solution)/shard_map/ppermute | solution.py:347
  101.6 5.9 %collective-permute-start.18 = (f32[64,128]{1,0:T(8,128)S(1)}, f32[64,128]{1,0:T(8,128)S(1)}, u32[]{:S(2)}, u32[]{:S(2)}) collective-permute-start(f32[64,128]{1,0:T(8,128)S(1)} %get-tuple-element.131), channel_id=1, source_target_pairs={{0,1},{1,0},{2,3},{3,2},{4,5},{5,4},{6,7},{7,6},{8,9},{9,8},{10,11... | collective-permute-start | bytes 98312 | tf_op jit(solution)/shard_map/ppermute | solution.py:344
  102.5 5.0 %collective-permute-start.19 = (f32[64,128]{1,0:T(8,128)S(1)}, f32[64,128]{1,0:T(8,128)S(1)}, u32[]{:S(2)}, u32[]{:S(2)}) collective-permute-start(f32[64,128]{1,0:T(8,128)S(1)} %get-tuple-element.132), channel_id=1, source_target_pairs={{0,16},{1,2},{2,1},{3,4},{4,3},{5,6},{6,5},{7,8},{8,7},{9,10},{10,... | collective-permute-start | bytes 98312 | tf_op jit(solution)/shard_map/ppermute | solution.py:345
  103.5 4.0 %collective-permute-start.20 = (f32[64,128]{1,0:T(8,128)S(1)}, f32[64,128]{1,0:T(8,128)S(1)}, u32[]{:S(2)}, u32[]{:S(2)}) collective-permute-start(f32[64,128]{1,0:T(8,128)S(1)} %get-tuple-element.133), channel_id=1, source_target_pairs={{0,16},{16,0},{32,48},{48,32},{64,80},{80,64},{96,112},{112,96},{1... | collective-permute-start | bytes 98312 | tf_op jit(solution)/shard_map/ppermute | solution.py:346
  104.2 3.3 %collective-permute-start.21 = (f32[64,128]{1,0:T(8,128)S(1)}, f32[64,128]{1,0:T(8,128)S(1)}, u32[]{:S(2)}, u32[]{:S(2)}) collective-permute-start(f32[64,128]{1,0:T(8,128)S(1)} %get-tuple-element.134), channel_id=1, source_target_pairs={{0,1},{1,0},{2,3},{3,2},{4,5},{5,4},{6,7},{7,6},{8,9},{9,8},{10,11... | collective-permute-start | bytes 98312 | tf_op jit(solution)/shard_map/ppermute | solution.py:347
  108.5 6.8 %collective-permute-start.22 = (f32[64,128]{1,0:T(8,128)S(1)}, f32[64,128]{1,0:T(8,128)S(1)}, u32[]{:S(2)}, u32[]{:S(2)}) collective-permute-start(f32[64,128]{1,0:T(8,128)S(1)} %get-tuple-element.139), channel_id=1, source_target_pairs={{0,1},{1,0},{2,3},{3,2},{4,5},{5,4},{6,7},{7,6},{8,9},{9,8},{10,11... | collective-permute-start | bytes 98312 | tf_op jit(solution)/shard_map/ppermute | solution.py:344
  110.7 4.5 %collective-permute-start.23 = (f32[64,128]{1,0:T(8,128)S(1)}, f32[64,128]{1,0:T(8,128)S(1)}, u32[]{:S(2)}, u32[]{:S(2)}) collective-permute-start(f32[64,128]{1,0:T(8,128)S(1)} %get-tuple-element.140), channel_id=1, source_target_pairs={{0,16},{1,2},{2,1},{3,4},{4,3},{5,6},{6,5},{7,8},{8,7},{9,10},{10,... | collective-permute-start | bytes 98312 | tf_op jit(solution)/shard_map/ppermute | solution.py:345
  110.7 4.5 %collective-permute-start.24 = (f32[64,128]{1,0:T(8,128)S(1)}, f32[64,128]{1,0:T(8,128)S(1)}, u32[]{:S(2)}, u32[]{:S(2)}) collective-permute-start(f32[64,128]{1,0:T(8,128)S(1)} %get-tuple-element.141), channel_id=1, source_target_pairs={{0,16},{16,0},{32,48},{48,32},{64,80},{80,64},{96,112},{112,96},{1... | collective-permute-start | bytes 98312 | tf_op jit(solution)/shard_map/ppermute | solution.py:346
  111.8 3.5 %collective-permute-start.25 = (f32[64,128]{1,0:T(8,128)S(1)}, f32[64,128]{1,0:T(8,128)S(1)}, u32[]{:S(2)}, u32[]{:S(2)}) collective-permute-start(f32[64,128]{1,0:T(8,128)S(1)} %get-tuple-element.142), channel_id=1, source_target_pairs={{0,1},{1,0},{2,3},{3,2},{4,5},{5,4},{6,7},{7,6},{8,9},{9,8},{10,11... | collective-permute-start | bytes 98312 | tf_op jit(solution)/shard_map/ppermute | solution.py:347
  (4 other events, 17.7 us)

commit v3 on v2

--- a/solution.py
+++ b/solution.py
@@ -75,7 +75,7 @@
 
 
 def scattered(terms, place):
-    return fold_rows(dot(terms, place, NT))
+    return fold_rows(dot(terms, place, NN))
 
 
 def put_rims(rim, rims):
@@ -108,8 +108,7 @@
 def link_kernel(order, send, receive, pick, real_shift, imag_shift, coupling, cross, coef, rim_coef, links):
     for slot in range(4):
         links[slot] = coupling[order[slot]].astype(F32).T.astype(BF16)
-    rows = [receive[pl.ds(order[slot], 1), :] for slot in range(4)]
-    targets = jnp.concatenate(rows + rows, axis=0).T
+    targets = targets_of(order, receive)
     for slot in range(4):
         chosen = send[pl.ds(order[slot], 1), :]
         for other in range(4):
@@ -128,9 +127,18 @@
     rim_coef[...] = total
 
 
+def targets_of(order, receive):
+    rows = [receive[pl.ds(order[slot], 1), :] for slot in range(4)]
+    return jnp.concatenate(rows + rows, axis=0).T
+
+
 def place_kernel(order, receive, modes, place, place_modes):
-    one_hot(order, receive, place)
-    place_modes[...] = dot(modes[...], place[...], NN).astype(BF16)
+    targets = targets_of(order, receive)
+    edge = lax.broadcasted_iota(jnp.int32, (TILE, NE), 1)
+    for slot in range(4):
+        same = edge == targets[:, slot : slot + 1]
+        place[slot * TILE : (slot + 1) * TILE, :] = jnp.where(same, 1.0, 0.0).astype(BF16)
+    place_modes[...] = dot(modes[...], place[...], NT).astype(BF16)
 
 
 def gather_column(gathered, column):
@@ -251,7 +259,7 @@
     copies = []
     for k in range(4):
         lanes = pl.ds(k * 256, 256)
-        value[:, lanes] = rest[:, lanes] - scattered(terms, place[k * 256 : (k + 1) * 256, :])
+        value[:, lanes] = rest[:, lanes] - scattered(terms, place[:, k * 256 : (k + 1) * 256])
         copies.append(pltpu.make_async_copy(value.at[:, lanes], residual.at[:, lanes], sems.at[k]))
         copies[-1].start()
     for copy in copies:
@@ -402,7 +410,7 @@
             if repeat == 0 and sweep == 0:
                 now, _ = lax.optimization_barrier((order, terms))
                 place, place_modes = call(
-                    place_kernel, [hot_shape, held((MODES, 4 * TILE), BF16)], [SMEM, VMEM, VMEM], [now, receive, modes], name="place"
+                    place_kernel, [held((4 * TILE, NE), BF16), held((MODES, 4 * TILE), BF16)], [SMEM, VMEM, VMEM], [now, receive, modes], name="place"
                 )
             common = [residual, local, terms, coef]
             if sweep == 0:

time: 117 us -> 117 us (level)
  transfers between devices with their start and end apart: 26 -> 26, of which waited for: 1 -> 1; matrix products, arithmetic and copies ran while one was open for 0% -> 0% of each run, Pallas kernels for 13% -> 12%
where the time goes in v3:
time: 117 us
  blocking collectives  62.6 us (54%)
  starting transfers between devices  27.8 us (24%)
  Pallas kernels  24.7 us (21%)
  between operations  1.3 us (1%)
    all_to_all x2, blocking collectives, on_device(): gathered = lax.all_to_all(packed, 'row', 0, 0)  31.4 us
    all_to_all x2, blocking collectives, on_device(): parts = lax.all_to_all(pair_sum, 'col', 0, 0, axis_index_groups=SAME_CORE)  31.2 us
    pallas_call x22, Pallas kernels, call(): pl.pallas_call(kernel, out_shape=list(out_shape), in_specs=in_specs, out_...  24.7 us
    ppermute x6, starting transfers between devices, exchange(): lax.ppermute(rims[0], ('row', 'col'), ROW_ODD)  6.99 us
    ppermute x6, starting transfers between devices, exchange(): lax.ppermute(rims[3], 'col', EVEN)  6.82 us
    ppermute x6, starting transfers between devices, exchange(): lax.ppermute(rims[2], 'row', EVEN)  6.43 us
    ppermute x2, starting transfers between devices, on_device(): pair_sum = keep + lax.ppermute(give, 'col', EVEN)  4.75 us
    ppermute x6, starting transfers between devices, exchange(): lax.ppermute(rims[1], ('row', 'col'), COL_ODD)  2.84 us
  transfers between devices with their start and end apart: 26, of which 1 were waited for; matrix products, arithmetic and copies ran while one was open for 0% of the time, Pallas kernels for 12%

profile of v3, /device:TPU:1, one launch (start us, length us, event | category | flops | bytes accessed | tf_op | source)
XLA Modules:
  0.0 117.0 jit_solution(9630992883229757517)
XLA Ops:
  0.7 1.5 %project.1 = (f32[16,48,128]{2,1,0:T(8,128)S(1)}, f32[64,1024]{1,0:T(8,128)S(1)}, bf16[96,1024]{1,0:T(8,128)(2,1)S(1)}) custom-call(f32[64,1024]{1,0:T(8,128)} %bitcast.37, bf16[96,1024]{1,0:T(8,128)(2,1)} %bitcast.38), custom_call_target="tpu_custom_call" | custom-call | flops 8800000000 | bytes 1048576 | tf_op jit(solution)/shard_map/project/pallas_call | solution.py:284
  2.3 16.6 %all_to_all.20.gathered = f32[16,48,128]{2,1,0:T(8,128)S(1)} all-to-all(f32[16,48,128]{2,1,0:T(8,128)S(1)} %get-tuple-element.76), channel_id=1, replica_groups=mesh['row'=16,'col'=16] {'row'}, dimensions={0} | all-to-all | bytes 786432 | tf_op jit(solution)/shard_map/all_to_all | solution.py:367
  18.9 1.0 give.2
  19.8 1.9 %collective-permute-start = (f32[8,48,128]{2,1,0:T(8,128)S(1)}, f32[8,48,128]{2,1,0:T(8,128)S(1)}, u32[]{:S(2)}, u32[]{:S(2)}) collective-permute-start(f32[8,48,128]{2,1,0:T(8,128)S(1)} %get-tuple-element.78), channel_id=1, source_target_pairs={{0,1},{1,0},{2,3},{3,2},{4,5},{5,4},{6,7},{7,6},{8,9},{9,8},{10,11... | collective-permute-start | bytes 589832 | tf_op jit(solution)/shard_map/ppermute | solution.py:375
  22.6 1.0 rim.1
  23.7 18.8 %all_to_all.21.parts = f32[8,48,128]{2,1,0:T(8,128)S(1)} all-to-all(f32[8,48,128]{2,1,0:T(8,128)S(1)} %add.19), channel_id=1, replica_groups={{0,2,4,6,8,10,12,14},{1,3,5,7,9,11,13,15},{16,18,20,22,24,26,28,30},{17..., dimensions={0} | all-to-all | bytes 393216 | tf_op jit(solution)/shard_map/all_to_all | solution.py:382
  44.3 1.4 %collective-permute-start.4 = (f32[64,128]{1,0:T(8,128)S(1)}, f32[64,128]{1,0:T(8,128)S(1)}, u32[]{:S(2)}, u32[]{:S(2)}) collective-permute-start(f32[64,128]{1,0:T(8,128)S(1)} %get-tuple-element.91), channel_id=1, source_target_pairs={{0,1},{1,0},{2,3},{3,2},{4,5},{5,4},{6,7},{7,6},{8,9},{9,8},{10,11... | collective-permute-start | bytes 98312 | tf_op jit(solution)/shard_map/ppermute | solution.py:355
  45.7 1.4 %open.1 = (f32[64,1024]{1,0:T(8,128)S(1)}, f32[64,512]{1,0:T(8,128)S(1)}) custom-call(s32[8,4]{1,0:T(8,128)S(1)} %copy.17.columns, bf16[96,128]{1,0:T(8,128)(2,1)S(1)} %get-tuple-element.85.field, bf16[96,1024]{1,0:T(8,128)(2,1)S(1)} %get-tuple-element.80.modes, bf16[8,4,128,128]{3,2,1,0:T(8,128)(2,1)S(1)} %bitcast.24, ...), custom_call_target="tpu_custom_call" | custom-call | flops 1760000000 | bytes 1048576 | tf_op jit(solution)/shard_map/open/pallas_call | solution.py:284
  47.2 1.1 link.1
  49.3 1.0 collective-permute-start.6
  50.3 1.3 %collective-permute-start.7 = (f32[64,128]{1,0:T(8,128)S(1)}, f32[64,128]{1,0:T(8,128)S(1)}, u32[]{:S(2)}, u32[]{:S(2)}) collective-permute-start(f32[64,128]{1,0:T(8,128)S(1)} %get-tuple-element.103), channel_id=1, source_target_pairs={{0,16},{16,0},{32,48},{48,32},{64,80},{80,64},{96,112},{112,96},{1... | collective-permute-start | bytes 98312 | tf_op jit(solution)/shard_map/ppermute | solution.py:354
  52.4 1.2 %place.1 = (bf16[512,1024]{1,0:T(8,128)(2,1)S(1)}, bf16[96,512]{1,0:T(8,128)(2,1)S(1)}) custom-call(s32[4]{0:T(128)S(1)} %get-tuple-element.99.order, s32[4,128]{1,0:T(4,128)S(1)} %bitcast.36, bf16[96,1024]{1,0:T(8,128)(2,1)S(1)} %get-tuple-element.80.modes), custom_call_target="tpu_custom_call" | custom-call | flops 1100000000 | bytes 1048576 | tf_op jit(solution)/shard_map/place/pallas_call | solution.py:284
  53.7 1.5 %middle.2 = (f32[64,1024]{1,0:T(8,128)S(1)}, f32[64,512]{1,0:T(8,128)S(1)}) custom-call(s32[8,4]{1,0:T(8,128)S(1)} %copy.17.columns, bf16[8,4,128,128]{3,2,1,0:T(8,128)(2,1)S(1)} %bitcast.25, bf16[1024,512]{1,0:T(8,128)(2,1)S(1)} %get-tuple-element.92.pick, bf16[512,1024]{1,0:T(8,128)(2,1)S(1)} %get-tuple-element.100.place, ...), custom_call_target="tpu_custom_call" | custom-call | flops 1760000000 | bytes 1048576 | tf_op jit(solution)/shard_map/middle/pallas_call | solution.py:284
  56.1 1.2 collective-permute-start.9
  57.5 2.8 %collective-permute-start.11 = (f32[64,128]{1,0:T(8,128)S(1)}, f32[64,128]{1,0:T(8,128)S(1)}, u32[]{:S(2)}, u32[]{:S(2)}) collective-permute-start(f32[64,128]{1,0:T(8,128)S(1)} %get-tuple-element.110), channel_id=1, source_target_pairs={{0,16},{16,0},{32,48},{48,32},{64,80},{80,64},{96,112},{112,96},{1... | collective-permute-start | bytes 98312 | tf_op jit(solution)/shard_map/ppermute | solution.py:354
  60.3 1.6 %finish.1 = (f32[64,1024]{1,0:T(8,128)S(1)}, f32[64,1024]{1,0:T(8,128)S(1)}, f32[48,128]{1,0:T(8,128)S(1)}) custom-call(s32[8,4]{1,0:T(8,128)S(1)} %copy.17.columns, bf16[8,4,128,128]{3,2,1,0:T(8,128)(2,1)S(1)} %bitcast.26, bf16[512,1024]{1,0:T(8,128)(2,1)S(1)} %get-tuple-element.100.place, f32[64,1024]{1,0:T(8,128)S(1)} %get-tuple-element.95.residual, ...), custom_call_target="tpu_custom_call" | custom-call | flops 1760000000 | bytes 1048576 | tf_op jit(solution)/shard_map/finish/pallas_call | solution.py:284
  61.9 1.0 close.1
  62.9 14.8 %all_to_all.22.gathered = f32[16,48,128]{2,1,0:T(8,128)S(1)} all-to-all(f32[16,48,128]{2,1,0:T(8,128)S(1)} %get-tuple-element.116), channel_id=1, replica_groups=mesh['row'=16,'col'=16] {'row'}, dimensions={0} | all-to-all | bytes 786432 | tf_op jit(solution)/shard_map/all_to_all | solution.py:367
  77.7 0.9 give.3
  78.7 2.8 %collective-permute-start.13 = (f32[8,48,128]{2,1,0:T(8,128)S(1)}, f32[8,48,128]{2,1,0:T(8,128)S(1)}, u32[]{:S(2)}, u32[]{:S(2)}) collective-permute-start(f32[8,48,128]{2,1,0:T(8,128)S(1)} %get-tuple-element.118), channel_id=1, source_target_pairs={{0,1},{1,0},{2,3},{3,2},{4,5},{5,4},{6,7},{7,6},{8,9},{9,8},{10,11... | collective-permute-start | bytes 589832 | tf_op jit(solution)/shard_map/ppermute | solution.py:375
  82.6 12.4 %all_to_all.23.parts = f32[8,48,128]{2,1,0:T(8,128)S(1)} all-to-all(f32[8,48,128]{2,1,0:T(8,128)S(1)} %add.20), channel_id=1, replica_groups={{0,2,4,6,8,10,12,14},{1,3,5,7,9,11,13,15},{16,18,20,22,24,26,28,30},{17..., dimensions={0} | all-to-all | bytes 393216 | tf_op jit(solution)/shard_map/all_to_all | solution.py:382
  95.3 1.5 %collective-permute-start.14 = (f32[64,128]{1,0:T(8,128)S(1)}, f32[64,128]{1,0:T(8,128)S(1)}, u32[]{:S(2)}, u32[]{:S(2)}) collective-permute-start(f32[64,128]{1,0:T(8,128)S(1)} %get-tuple-element.124), channel_id=1, source_target_pairs={{0,1},{1,0},{2,3},{3,2},{4,5},{5,4},{6,7},{7,6},{8,9},{9,8},{10,11... | collective-permute-start | bytes 98312 | tf_op jit(solution)/shard_map/ppermute | solution.py:352
  97.5 1.4 %collective-permute-start.17 = (f32[64,128]{1,0:T(8,128)S(1)}, f32[64,128]{1,0:T(8,128)S(1)}, u32[]{:S(2)}, u32[]{:S(2)}) collective-permute-start(f32[64,128]{1,0:T(8,128)S(1)} %get-tuple-element.127), channel_id=1, source_target_pairs={{0,1},{1,0},{2,3},{3,2},{4,5},{5,4},{6,7},{7,6},{8,9},{9,8},{10,11... | collective-permute-start | bytes 98312 | tf_op jit(solution)/shard_map/ppermute | solution.py:355
  98.9 1.5 %reopen.1 = (f32[64,1024]{1,0:T(8,128)S(1)}, f32[64,1024]{1,0:T(8,128)S(1)}, f32[64,512]{1,0:T(8,128)S(1)}) custom-call(s32[8,4]{1,0:T(8,128)S(1)} %copy.17.columns, bf16[96,128]{1,0:T(8,128)(2,1)S(1)} %get-tuple-element.119.field, bf16[96,1024]{1,0:T(8,128)(2,1)S(1)} %get-tuple-element.80.modes, bf16[8,4,128,128]{3,2,1,0:T(8,128)(2,1)S(1)} %bitcast.27, ...), custom_call_target="tpu_custom_call" | custom-call | flops 1760000000 | bytes 1048576 | tf_op jit(solution)/shard_map/reopen/pallas_call | solution.py:284
  101.4 1.1 collective-permute-start.18
  102.5 1.0 collective-permute-start.19
  104.2 1.6 %collective-permute-start.21 = (f32[64,128]{1,0:T(8,128)S(1)}, f32[64,128]{1,0:T(8,128)S(1)}, u32[]{:S(2)}, u32[]{:S(2)}) collective-permute-start(f32[64,128]{1,0:T(8,128)S(1)} %get-tuple-element.134), channel_id=1, source_target_pairs={{0,1},{1,0},{2,3},{3,2},{4,5},{5,4},{6,7},{7,6},{8,9},{9,8},{10,11... | collective-permute-start | bytes 98312 | tf_op jit(solution)/shard_map/ppermute | solution.py:355
  105.9 1.5 %middle.3 = (f32[64,1024]{1,0:T(8,128)S(1)}, f32[64,512]{1,0:T(8,128)S(1)}) custom-call(s32[8,4]{1,0:T(8,128)S(1)} %copy.17.columns, bf16[8,4,128,128]{3,2,1,0:T(8,128)(2,1)S(1)} %bitcast.28, bf16[1024,512]{1,0:T(8,128)(2,1)S(1)} %get-tuple-element.92.pick, bf16[512,1024]{1,0:T(8,128)(2,1)S(1)} %get-tuple-element.100.place, ...), custom_call_target="tpu_custom_call" | custom-call | flops 1760000000 | bytes 1048576 | tf_op jit(solution)/shard_map/middle/pallas_call | solution.py:284
  108.3 2.4 %collective-permute-start.22 = (f32[64,128]{1,0:T(8,128)S(1)}, f32[64,128]{1,0:T(8,128)S(1)}, u32[]{:S(2)}, u32[]{:S(2)}) collective-permute-start(f32[64,128]{1,0:T(8,128)S(1)} %get-tuple-element.139), channel_id=1, source_target_pairs={{0,1},{1,0},{2,3},{3,2},{4,5},{5,4},{6,7},{7,6},{8,9},{9,8},{10,11... | collective-permute-start | bytes 98312 | tf_op jit(solution)/shard_map/ppermute | solution.py:352
  111.6 1.6 %collective-permute-start.25 = (f32[64,128]{1,0:T(8,128)S(1)}, f32[64,128]{1,0:T(8,128)S(1)}, u32[]{:S(2)}, u32[]{:S(2)}) collective-permute-start(f32[64,128]{1,0:T(8,128)S(1)} %get-tuple-element.142), channel_id=1, source_target_pairs={{0,1},{1,0},{2,3},{3,2},{4,5},{5,4},{6,7},{7,6},{8,9},{9,8},{10,11... | collective-permute-start | bytes 98312 | tf_op jit(solution)/shard_map/ppermute | solution.py:355
  113.2 1.9 %finish_last.1 = (f32[64,1024]{1,0:T(8,128)}, f32[64,1024]{1,0:T(8,128)S(1)}) custom-call(s32[8,4]{1,0:T(8,128)S(1)} %copy.17.columns, bf16[8,4,128,128]{3,2,1,0:T(8,128)(2,1)S(1)} %bitcast.29, bf16[512,1024]{1,0:T(8,128)(2,1)S(1)} %get-tuple-element.100.place, f32[64,1024]{1,0:T(8,128)S(1)} %get-tuple-element.122.residual, ...), custom_call_target="tpu_custom_call" | custom-call | flops 1760000000 | bytes 1048576 | tf_op jit(solution)/shard_map/finish_last/pallas_call | solution.py:284
  115.2 1.7 %last.1 = f32[64,1024]{1,0:T(8,128)} custom-call(s32[4]{0:T(128)S(1)} %get-tuple-element.87.inside, f32[64,128]{1,0:T(8,128)S(1)} %collective-permute-done.22.l0, f32[64,128]{1,0:T(8,128)S(1)} %collective-permute-done.23.l1, f32[64,128]{1,0:T(8,128)S(1)} %collective-permute-done.24.l2, f32[64,128]{1,0:T(8,128)S(1)} %collective-permute-done.25.l3, ...), custom_call_target="tpu_custom_call" | custom-call | flops 990000000 | bytes 1048576 | tf_op jit(solution)/shard_map/last/pallas_call | solution.py:284
  (73 shorter events, 11.1 us)
Async XLA Ops:
  0.7 18.2 %copy-start = (bf16[1536,1536]{1,0:T(8,128)(2,1)S(1)}, bf16[1536,1536]{1,0:T(8,128)(2,1)}, u32[]{:S(2)}) copy-start(bf16[1536,1536]{1,0:T(8,128)(2,1)} %inverse.7) | copy-start | bytes 14155780
  19.8 3.8 %collective-permute-start = (f32[8,48,128]{2,1,0:T(8,128)S(1)}, f32[8,48,128]{2,1,0:T(8,128)S(1)}, u32[]{:S(2)}, u32[]{:S(2)}) collective-permute-start(f32[8,48,128]{2,1,0:T(8,128)S(1)} %get-tuple-element.78), channel_id=1, source_target_pairs={{0,1},{1,0},{2,3},{3,2},{4,5},{5,4},{6,7},{7,6},{8,9},{9,8},{10,11... | collective-permute-start | bytes 589832 | tf_op jit(solution)/shard_map/ppermute | solution.py:375
  22.6 20.2 %copy-start.7 = (s32[1,1,8,4]{2,3,1,0:T(4,128)S(1)}, s32[1,1,8,4]{2,3,1,0:T(4,128)}, u32[]{:S(2)}) copy-start(s32[1,1,8,4]{2,3,1,0:T(4,128)} %param.14) | copy-start | bytes 388
  22.6 23.1 %copy-start.1 = (bf16[1,1,8,4,128,128]{5,4,3,2,1,0:T(8,128)(2,1)S(1)}, bf16[1,1,8,4,128,128]{5,4,3,2,1,0:T(8,128)(2,1)}, u32[]{:S(2)}) copy-start(bf16[1,1,8,4,128,128]{5,4,3,2,1,0:T(8,128)(2,1)} %param.13) | copy-start | bytes 3145732
  42.5 4.7 %copy-start.6 = (s32[1,1,4,128]{3,2,1,0:T(4,128)S(1)}, s32[1,1,4,128]{3,2,1,0:T(4,128)}, u32[]{:S(2)}) copy-start(s32[1,1,4,128]{3,2,1,0:T(4,128)} %param.17) | copy-start | bytes 6148
  42.9 5.3 %collective-permute-start.1 = (f32[64,128]{1,0:T(8,128)S(1)}, f32[64,128]{1,0:T(8,128)S(1)}, u32[]{:S(2)}, u32[]{:S(2)}) collective-permute-start(f32[64,128]{1,0:T(8,128)S(1)} %get-tuple-element.88), channel_id=1, source_target_pairs={{0,1},{1,0},{2,3},{3,2},{4,5},{5,4},{6,7},{7,6},{8,9},{9,8},{10,11... | collective-permute-start | bytes 98312 | tf_op jit(solution)/shard_map/ppermute | solution.py:352
  43.6 4.6 %collective-permute-start.2 = (f32[64,128]{1,0:T(8,128)S(1)}, f32[64,128]{1,0:T(8,128)S(1)}, u32[]{:S(2)}, u32[]{:S(2)}) collective-permute-start(f32[64,128]{1,0:T(8,128)S(1)} %get-tuple-element.89), channel_id=1, source_target_pairs={{0,16},{1,2},{2,1},{3,4},{4,3},{5,6},{6,5},{7,8},{8,7},{9,10},{10,... | collective-permute-start | bytes 98312 | tf_op jit(solution)/shard_map/ppermute | solution.py:353
  43.9 4.4 %collective-permute-start.3 = (f32[64,128]{1,0:T(8,128)S(1)}, f32[64,128]{1,0:T(8,128)S(1)}, u32[]{:S(2)}, u32[]{:S(2)}) collective-permute-start(f32[64,128]{1,0:T(8,128)S(1)} %get-tuple-element.90), channel_id=1, source_target_pairs={{0,16},{16,0},{32,48},{48,32},{64,80},{80,64},{96,112},{112,96},{1... | collective-permute-start | bytes 98312 | tf_op jit(solution)/shard_map/ppermute | solution.py:354
  44.3 4.0 %collective-permute-start.4 = (f32[64,128]{1,0:T(8,128)S(1)}, f32[64,128]{1,0:T(8,128)S(1)}, u32[]{:S(2)}, u32[]{:S(2)}) collective-permute-start(f32[64,128]{1,0:T(8,128)S(1)} %get-tuple-element.91), channel_id=1, source_target_pairs={{0,1},{1,0},{2,3},{3,2},{4,5},{5,4},{6,7},{7,6},{8,9},{9,8},{10,11... | collective-permute-start | bytes 98312 | tf_op jit(solution)/shard_map/ppermute | solution.py:355
  49.2 6.0 %collective-permute-start.5 = (f32[64,128]{1,0:T(8,128)S(1)}, f32[64,128]{1,0:T(8,128)S(1)}, u32[]{:S(2)}, u32[]{:S(2)}) collective-permute-start(f32[64,128]{1,0:T(8,128)S(1)} %get-tuple-element.101), channel_id=1, source_target_pairs={{0,1},{1,0},{2,3},{3,2},{4,5},{5,4},{6,7},{7,6},{8,9},{9,8},{10,11... | collective-permute-start | bytes 98312 | tf_op jit(solution)/shard_map/ppermute | solution.py:352
  49.3 5.9 %collective-permute-start.6 = (f32[64,128]{1,0:T(8,128)S(1)}, f32[64,128]{1,0:T(8,128)S(1)}, u32[]{:S(2)}, u32[]{:S(2)}) collective-permute-start(f32[64,128]{1,0:T(8,128)S(1)} %get-tuple-element.102), channel_id=1, source_target_pairs={{0,16},{1,2},{2,1},{3,4},{4,3},{5,6},{6,5},{7,8},{8,7},{9,10},{10,... | collective-permute-start | bytes 98312 | tf_op jit(solution)/shard_map/ppermute | solution.py:353
  50.3 4.8 %collective-permute-start.7 = (f32[64,128]{1,0:T(8,128)S(1)}, f32[64,128]{1,0:T(8,128)S(1)}, u32[]{:S(2)}, u32[]{:S(2)}) collective-permute-start(f32[64,128]{1,0:T(8,128)S(1)} %get-tuple-element.103), channel_id=1, source_target_pairs={{0,16},{16,0},{32,48},{48,32},{64,80},{80,64},{96,112},{112,96},{1... | collective-permute-start | bytes 98312 | tf_op jit(solution)/shard_map/ppermute | solution.py:354
  51.6 3.6 %collective-permute-start.8 = (f32[64,128]{1,0:T(8,128)S(1)}, f32[64,128]{1,0:T(8,128)S(1)}, u32[]{:S(2)}, u32[]{:S(2)}) collective-permute-start(f32[64,128]{1,0:T(8,128)S(1)} %get-tuple-element.104), channel_id=1, source_target_pairs={{0,1},{1,0},{2,3},{3,2},{4,5},{5,4},{6,7},{7,6},{8,9},{9,8},{10,11... | collective-permute-start | bytes 98312 | tf_op jit(solution)/shard_map/ppermute | solution.py:355
  56.1 5.8 %collective-permute-start.9 = (f32[64,128]{1,0:T(8,128)S(1)}, f32[64,128]{1,0:T(8,128)S(1)}, u32[]{:S(2)}, u32[]{:S(2)}) collective-permute-start(f32[64,128]{1,0:T(8,128)S(1)} %get-tuple-element.108), channel_id=1, source_target_pairs={{0,1},{1,0},{2,3},{3,2},{4,5},{5,4},{6,7},{7,6},{8,9},{9,8},{10,11... | collective-permute-start | bytes 98312 | tf_op jit(solution)/shard_map/ppermute | solution.py:352
  57.3 4.6 %collective-permute-start.10 = (f32[64,128]{1,0:T(8,128)S(1)}, f32[64,128]{1,0:T(8,128)S(1)}, u32[]{:S(2)}, u32[]{:S(2)}) collective-permute-start(f32[64,128]{1,0:T(8,128)S(1)} %get-tuple-element.109), channel_id=1, source_target_pairs={{0,16},{1,2},{2,1},{3,4},{4,3},{5,6},{6,5},{7,8},{8,7},{9,10},{10,... | collective-permute-start | bytes 98312 | tf_op jit(solution)/shard_map/ppermute | solution.py:353
  57.5 4.4 %collective-permute-start.11 = (f32[64,128]{1,0:T(8,128)S(1)}, f32[64,128]{1,0:T(8,128)S(1)}, u32[]{:S(2)}, u32[]{:S(2)}) collective-permute-start(f32[64,128]{1,0:T(8,128)S(1)} %get-tuple-element.110), channel_id=1, source_target_pairs={{0,16},{16,0},{32,48},{48,32},{64,80},{80,64},{96,112},{112,96},{1... | collective-permute-start | bytes 98312 | tf_op jit(solution)/shard_map/ppermute | solution.py:354
  60.3 1.7 %collective-permute-start.12 = (f32[64,128]{1,0:T(8,128)S(1)}, f32[64,128]{1,0:T(8,128)S(1)}, u32[]{:S(2)}, u32[]{:S(2)}) collective-permute-start(f32[64,128]{1,0:T(8,128)S(1)} %get-tuple-element.111), channel_id=1, source_target_pairs={{0,1},{1,0},{2,3},{3,2},{4,5},{5,4},{6,7},{7,6},{8,9},{9,8},{10,11... | collective-permute-start | bytes 98312 | tf_op jit(solution)/shard_map/ppermute | solution.py:355
  60.3 17.5 %slice-start = ((s8[4718592]{0:T(1024)(128)(4,1)}), s8[4194304]{0:T(1024)(128)(4,1)S(1)}, s32[]{:S(2)}) async-start(s8[4718592]{0:T(1024)(128)(4,1)} %bitcast.21), calls=%async_computation.4 | async-start | bytes 8388608
  60.3 17.5 %slice-start.1 = ((s8[4718592]{0:T(1024)(128)(4,1)}), s8[524288]{0:T(1024)(128)(4,1)S(1)}, s32[]{:S(2)}) async-start(s8[4718592]{0:T(1024)(128)(4,1)} %bitcast.21), calls=%async_computation.5 | async-start | bytes 1048576
  78.7 3.9 %collective-permute-start.13 = (f32[8,48,128]{2,1,0:T(8,128)S(1)}, f32[8,48,128]{2,1,0:T(8,128)S(1)}, u32[]{:S(2)}, u32[]{:S(2)}) collective-permute-start(f32[8,48,128]{2,1,0:T(8,128)S(1)} %get-tuple-element.118), channel_id=1, source_target_pairs={{0,1},{1,0},{2,3},{3,2},{4,5},{5,4},{6,7},{7,6},{8,9},{9,8},{10,11... | collective-permute-start | bytes 589832 | tf_op jit(solution)/shard_map/ppermute | solution.py:375
  95.3 5.2 %collective-permute-start.14 = (f32[64,128]{1,0:T(8,128)S(1)}, f32[64,128]{1,0:T(8,128)S(1)}, u32[]{:S(2)}, u32[]{:S(2)}) collective-permute-start(f32[64,128]{1,0:T(8,128)S(1)} %get-tuple-element.124), channel_id=1, source_target_pairs={{0,1},{1,0},{2,3},{3,2},{4,5},{5,4},{6,7},{7,6},{8,9},{9,8},{10,11... | collective-permute-start | bytes 98312 | tf_op jit(solution)/shard_map/ppermute | solution.py:352
  96.8 3.7 %collective-permute-start.15 = (f32[64,128]{1,0:T(8,128)S(1)}, f32[64,128]{1,0:T(8,128)S(1)}, u32[]{:S(2)}, u32[]{:S(2)}) collective-permute-start(f32[64,128]{1,0:T(8,128)S(1)} %get-tuple-element.125), channel_id=1, source_target_pairs={{0,16},{1,2},{2,1},{3,4},{4,3},{5,6},{6,5},{7,8},{8,7},{9,10},{10,... | collective-permute-start | bytes 98312 | tf_op jit(solution)/shard_map/ppermute | solution.py:353
  97.1 3.4 %collective-permute-start.16 = (f32[64,128]{1,0:T(8,128)S(1)}, f32[64,128]{1,0:T(8,128)S(1)}, u32[]{:S(2)}, u32[]{:S(2)}) collective-permute-start(f32[64,128]{1,0:T(8,128)S(1)} %get-tuple-element.126), channel_id=1, source_target_pairs={{0,16},{16,0},{32,48},{48,32},{64,80},{80,64},{96,112},{112,96},{1... | collective-permute-start | bytes 98312 | tf_op jit(solution)/shard_map/ppermute | solution.py:354
  97.5 3.0 %collective-permute-start.17 = (f32[64,128]{1,0:T(8,128)S(1)}, f32[64,128]{1,0:T(8,128)S(1)}, u32[]{:S(2)}, u32[]{:S(2)}) collective-permute-start(f32[64,128]{1,0:T(8,128)S(1)} %get-tuple-element.127), channel_id=1, source_target_pairs={{0,1},{1,0},{2,3},{3,2},{4,5},{5,4},{6,7},{7,6},{8,9},{9,8},{10,11... | collective-permute-start | bytes 98312 | tf_op jit(solution)/shard_map/ppermute | solution.py:355
  101.4 5.9 %collective-permute-start.18 = (f32[64,128]{1,0:T(8,128)S(1)}, f32[64,128]{1,0:T(8,128)S(1)}, u32[]{:S(2)}, u32[]{:S(2)}) collective-permute-start(f32[64,128]{1,0:T(8,128)S(1)} %get-tuple-element.131), channel_id=1, source_target_pairs={{0,1},{1,0},{2,3},{3,2},{4,5},{5,4},{6,7},{7,6},{8,9},{9,8},{10,11... | collective-permute-start | bytes 98312 | tf_op jit(solution)/shard_map/ppermute | solution.py:352
  102.5 4.8 %collective-permute-start.19 = (f32[64,128]{1,0:T(8,128)S(1)}, f32[64,128]{1,0:T(8,128)S(1)}, u32[]{:S(2)}, u32[]{:S(2)}) collective-permute-start(f32[64,128]{1,0:T(8,128)S(1)} %get-tuple-element.132), channel_id=1, source_target_pairs={{0,16},{1,2},{2,1},{3,4},{4,3},{5,6},{6,5},{7,8},{8,7},{9,10},{10,... | collective-permute-start | bytes 98312 | tf_op jit(solution)/shard_map/ppermute | solution.py:353
  103.6 3.8 %collective-permute-start.20 = (f32[64,128]{1,0:T(8,128)S(1)}, f32[64,128]{1,0:T(8,128)S(1)}, u32[]{:S(2)}, u32[]{:S(2)}) collective-permute-start(f32[64,128]{1,0:T(8,128)S(1)} %get-tuple-element.133), channel_id=1, source_target_pairs={{0,16},{16,0},{32,48},{48,32},{64,80},{80,64},{96,112},{112,96},{1... | collective-permute-start | bytes 98312 | tf_op jit(solution)/shard_map/ppermute | solution.py:354
  104.2 3.2 %collective-permute-start.21 = (f32[64,128]{1,0:T(8,128)S(1)}, f32[64,128]{1,0:T(8,128)S(1)}, u32[]{:S(2)}, u32[]{:S(2)}) collective-permute-start(f32[64,128]{1,0:T(8,128)S(1)} %get-tuple-element.134), channel_id=1, source_target_pairs={{0,1},{1,0},{2,3},{3,2},{4,5},{5,4},{6,7},{7,6},{8,9},{9,8},{10,11... | collective-permute-start | bytes 98312 | tf_op jit(solution)/shard_map/ppermute | solution.py:355
  108.3 6.8 %collective-permute-start.22 = (f32[64,128]{1,0:T(8,128)S(1)}, f32[64,128]{1,0:T(8,128)S(1)}, u32[]{:S(2)}, u32[]{:S(2)}) collective-permute-start(f32[64,128]{1,0:T(8,128)S(1)} %get-tuple-element.139), channel_id=1, source_target_pairs={{0,1},{1,0},{2,3},{3,2},{4,5},{5,4},{6,7},{7,6},{8,9},{9,8},{10,11... | collective-permute-start | bytes 98312 | tf_op jit(solution)/shard_map/ppermute | solution.py:352
  110.8 4.4 %collective-permute-start.23 = (f32[64,128]{1,0:T(8,128)S(1)}, f32[64,128]{1,0:T(8,128)S(1)}, u32[]{:S(2)}, u32[]{:S(2)}) collective-permute-start(f32[64,128]{1,0:T(8,128)S(1)} %get-tuple-element.140), channel_id=1, source_target_pairs={{0,16},{1,2},{2,1},{3,4},{4,3},{5,6},{6,5},{7,8},{8,7},{9,10},{10,... | collective-permute-start | bytes 98312 | tf_op jit(solution)/shard_map/ppermute | solution.py:353
  110.8 4.4 %collective-permute-start.24 = (f32[64,128]{1,0:T(8,128)S(1)}, f32[64,128]{1,0:T(8,128)S(1)}, u32[]{:S(2)}, u32[]{:S(2)}) collective-permute-start(f32[64,128]{1,0:T(8,128)S(1)} %get-tuple-element.141), channel_id=1, source_target_pairs={{0,16},{16,0},{32,48},{48,32},{64,80},{80,64},{96,112},{112,96},{1... | collective-permute-start | bytes 98312 | tf_op jit(solution)/shard_map/ppermute | solution.py:354
  111.6 3.5 %collective-permute-start.25 = (f32[64,128]{1,0:T(8,128)S(1)}, f32[64,128]{1,0:T(8,128)S(1)}, u32[]{:S(2)}, u32[]{:S(2)}) collective-permute-start(f32[64,128]{1,0:T(8,128)S(1)} %get-tuple-element.142), channel_id=1, source_target_pairs={{0,1},{1,0},{2,3},{3,2},{4,5},{5,4},{6,7},{7,6},{8,9},{9,8},{10,11... | collective-permute-start | bytes 98312 | tf_op jit(solution)/shard_map/ppermute | solution.py:355
  (4 other events, 17.7 us)

commit v4 on v3

--- a/solution.py
+++ b/solution.py
@@ -332,11 +332,11 @@
 
     row, col = lax.axis_index("row"), lax.axis_index("col")
     row_odd, col_odd = row % 2, col % 2
-    order = jnp.stack([row_odd, 2 + col_odd, 1 - row_odd, 3 - col_odd]).astype(jnp.int32)
+    order = jnp.stack([row_odd, 1 - row_odd, 2 + col_odd, 3 - col_odd]).astype(jnp.int32)
     one = jnp.ones((), jnp.int32)
     row_in = jnp.where((row > 0) & (row < N - 1), 1, 0).astype(jnp.int32)
     col_in = jnp.where((col > 0) & (col < N - 1), 1, 0).astype(jnp.int32)
-    inside = jnp.stack([row_in, col_in, one, one])
+    inside = jnp.stack([row_in, one, col_in, one])
     core = col_odd.astype(jnp.int32).reshape(1)
 
     rim_shapes = [shape((ROWS, TILE))] * 4
@@ -350,8 +350,8 @@
     def exchange(rims):
         return [
             lax.ppermute(rims[0], ("row", "col"), ROW_ODD),
-            lax.ppermute(rims[1], ("row", "col"), COL_ODD),
-            lax.ppermute(rims[2], "row", EVEN),
+            lax.ppermute(rims[1], "row", EVEN),
+            lax.ppermute(rims[2], ("row", "col"), COL_ODD),
             lax.ppermute(rims[3], "col", EVEN),
         ]
 

time: 117 us -> 118 us (level)
    ppermute x6, starting transfers between devices: 6.82 us -> 3.93 us  [exchange(): lax.ppermute(rims[3], 'col', EVEN)]
    ppermute x12, starting transfers between devices: 9.27 us -> 12.1 us  [the longest x6 7.81 us: exchange(): lax.ppermute(rims[2], ('row', 'col'), COL_ODD)]
where the time goes in v4:
time: 118 us; the launch traced here: 117 us
  blocking collectives  63.4 us (54%)
  starting transfers between devices  27.3 us (23%)
  Pallas kernels  24.7 us (21%)
  between operations  1.3 us (1%)
    all_to_all x2, blocking collectives, on_device(): gathered = lax.all_to_all(packed, 'row', 0, 0)  32.2 us
    all_to_all x2, blocking collectives, on_device(): parts = lax.all_to_all(pair_sum, 'col', 0, 0, axis_index_groups=SAME_CORE)  31.2 us
    pallas_call x22, Pallas kernels, call(): pl.pallas_call(kernel, out_shape=list(out_shape), in_specs=in_specs, out_...  24.7 us
    ppermute x6, starting transfers between devices, exchange(): lax.ppermute(rims[2], ('row', 'col'), COL_ODD)  7.81 us
    ppermute x6, starting transfers between devices, exchange(): lax.ppermute(rims[0], ('row', 'col'), ROW_ODD)  6.98 us
    ppermute x6, starting transfers between devices, exchange(): lax.ppermute(rims[1], 'row', EVEN)  4.29 us
    ppermute x2, starting transfers between devices, on_device(): pair_sum = keep + lax.ppermute(give, 'col', EVEN)  4.28 us
    ppermute x6, starting transfers between devices, exchange(): lax.ppermute(rims[3], 'col', EVEN)  3.93 us
  transfers between devices with their start and end apart: 26, of which 1 were waited for; matrix products, arithmetic and copies ran while one was open for 0% of the time, Pallas kernels for 12%

profile of v4, /device:TPU:1, one launch (start us, length us, event | category | flops | bytes accessed | tf_op | source)
XLA Modules:
  0.0 117.2 jit_solution(5944881813613454919)
XLA Ops:
  0.7 1.5 %project.1 = (f32[16,48,128]{2,1,0:T(8,128)S(1)}, f32[64,1024]{1,0:T(8,128)S(1)}, bf16[96,1024]{1,0:T(8,128)(2,1)S(1)}) custom-call(f32[64,1024]{1,0:T(8,128)} %bitcast.37, bf16[96,1024]{1,0:T(8,128)(2,1)} %bitcast.38), custom_call_target="tpu_custom_call" | custom-call | flops 8800000000 | bytes 1048576 | tf_op jit(solution)/shard_map/project/pallas_call | solution.py:284
  2.2 16.7 %all_to_all.20.gathered = f32[16,48,128]{2,1,0:T(8,128)S(1)} all-to-all(f32[16,48,128]{2,1,0:T(8,128)S(1)} %get-tuple-element.76), channel_id=1, replica_groups=mesh['row'=16,'col'=16] {'row'}, dimensions={0} | all-to-all | bytes 786432 | tf_op jit(solution)/shard_map/all_to_all | solution.py:367
  19.9 1.9 %collective-permute-start = (f32[8,48,128]{2,1,0:T(8,128)S(1)}, f32[8,48,128]{2,1,0:T(8,128)S(1)}, u32[]{:S(2)}, u32[]{:S(2)}) collective-permute-start(f32[8,48,128]{2,1,0:T(8,128)S(1)} %get-tuple-element.78), channel_id=1, source_target_pairs={{0,1},{1,0},{2,3},{3,2},{4,5},{5,4},{6,7},{7,6},{8,9},{9,8},{10,11... | collective-permute-start | bytes 589832 | tf_op jit(solution)/shard_map/ppermute | solution.py:375
  22.7 1.0 rim.1
  23.8 18.8 %all_to_all.21.parts = f32[8,48,128]{2,1,0:T(8,128)S(1)} all-to-all(f32[8,48,128]{2,1,0:T(8,128)S(1)} %add.19), channel_id=1, replica_groups={{0,2,4,6,8,10,12,14},{1,3,5,7,9,11,13,15},{16,18,20,22,24,26,28,30},{17..., dimensions={0} | all-to-all | bytes 393216 | tf_op jit(solution)/shard_map/all_to_all | solution.py:382
  43.7 1.0 collective-permute-start.3
  44.7 1.1 collective-permute-start.4
  45.8 1.4 %open.1 = (f32[64,1024]{1,0:T(8,128)S(1)}, f32[64,512]{1,0:T(8,128)S(1)}) custom-call(s32[8,4]{1,0:T(8,128)S(1)} %copy.17.columns, bf16[96,128]{1,0:T(8,128)(2,1)S(1)} %get-tuple-element.85.field, bf16[96,1024]{1,0:T(8,128)(2,1)S(1)} %get-tuple-element.80.modes, bf16[8,4,128,128]{3,2,1,0:T(8,128)(2,1)S(1)} %bitcast.24, ...), custom_call_target="tpu_custom_call" | custom-call | flops 1760000000 | bytes 1048576 | tf_op jit(solution)/shard_map/open/pallas_call | solution.py:284
  47.3 1.1 link.1
  49.4 1.9 %collective-permute-start.6 = (f32[64,128]{1,0:T(8,128)S(1)}, f32[64,128]{1,0:T(8,128)S(1)}, u32[]{:S(2)}, u32[]{:S(2)}) collective-permute-start(f32[64,128]{1,0:T(8,128)S(1)} %get-tuple-element.102), channel_id=1, source_target_pairs={{0,16},{16,0},{32,48},{48,32},{64,80},{80,64},{96,112},{112,96},{1... | collective-permute-start | bytes 98312 | tf_op jit(solution)/shard_map/ppermute | solution.py:353
  52.5 1.2 %place.1 = (bf16[512,1024]{1,0:T(8,128)(2,1)S(1)}, bf16[96,512]{1,0:T(8,128)(2,1)S(1)}) custom-call(s32[4]{0:T(128)S(1)} %get-tuple-element.99.order, s32[4,128]{1,0:T(4,128)S(1)} %bitcast.36, bf16[96,1024]{1,0:T(8,128)(2,1)S(1)} %get-tuple-element.80.modes), custom_call_target="tpu_custom_call" | custom-call | flops 1100000000 | bytes 1048576 | tf_op jit(solution)/shard_map/place/pallas_call | solution.py:284
  53.8 1.5 %middle.2 = (f32[64,1024]{1,0:T(8,128)S(1)}, f32[64,512]{1,0:T(8,128)S(1)}) custom-call(s32[8,4]{1,0:T(8,128)S(1)} %copy.17.columns, bf16[8,4,128,128]{3,2,1,0:T(8,128)(2,1)S(1)} %bitcast.25, bf16[1024,512]{1,0:T(8,128)(2,1)S(1)} %get-tuple-element.92.pick, bf16[512,1024]{1,0:T(8,128)(2,1)S(1)} %get-tuple-element.100.place, ...), custom_call_target="tpu_custom_call" | custom-call | flops 1760000000 | bytes 1048576 | tf_op jit(solution)/shard_map/middle/pallas_call | solution.py:284
  56.2 1.2 collective-permute-start.9
  57.4 1.3 %collective-permute-start.10 = (f32[64,128]{1,0:T(8,128)S(1)}, f32[64,128]{1,0:T(8,128)S(1)}, u32[]{:S(2)}, u32[]{:S(2)}) collective-permute-start(f32[64,128]{1,0:T(8,128)S(1)} %get-tuple-element.109), channel_id=1, source_target_pairs={{0,16},{16,0},{32,48},{48,32},{64,80},{80,64},{96,112},{112,96},{1... | collective-permute-start | bytes 98312 | tf_op jit(solution)/shard_map/ppermute | solution.py:353
  58.7 1.7 %collective-permute-start.11 = (f32[64,128]{1,0:T(8,128)S(1)}, f32[64,128]{1,0:T(8,128)S(1)}, u32[]{:S(2)}, u32[]{:S(2)}) collective-permute-start(f32[64,128]{1,0:T(8,128)S(1)} %get-tuple-element.110), channel_id=1, source_target_pairs={{0,16},{1,2},{2,1},{3,4},{4,3},{5,6},{6,5},{7,8},{8,7},{9,10},{10,... | collective-permute-start | bytes 98312 | tf_op jit(solution)/shard_map/ppermute | solution.py:354
  60.4 1.6 %finish.1 = (f32[64,1024]{1,0:T(8,128)S(1)}, f32[64,1024]{1,0:T(8,128)S(1)}, f32[48,128]{1,0:T(8,128)S(1)}) custom-call(s32[8,4]{1,0:T(8,128)S(1)} %copy.17.columns, bf16[8,4,128,128]{3,2,1,0:T(8,128)(2,1)S(1)} %bitcast.26, bf16[512,1024]{1,0:T(8,128)(2,1)S(1)} %get-tuple-element.100.place, f32[64,1024]{1,0:T(8,128)S(1)} %get-tuple-element.95.residual, ...), custom_call_target="tpu_custom_call" | custom-call | flops 1760000000 | bytes 1048576 | tf_op jit(solution)/shard_map/finish/pallas_call | solution.py:284
  62.0 1.0 close.1
  63.0 15.5 %all_to_all.22.gathered = f32[16,48,128]{2,1,0:T(8,128)S(1)} all-to-all(f32[16,48,128]{2,1,0:T(8,128)S(1)} %get-tuple-element.116), channel_id=1, replica_groups=mesh['row'=16,'col'=16] {'row'}, dimensions={0} | all-to-all | bytes 786432 | tf_op jit(solution)/shard_map/all_to_all | solution.py:367
  79.5 2.4 %collective-permute-start.13 = (f32[8,48,128]{2,1,0:T(8,128)S(1)}, f32[8,48,128]{2,1,0:T(8,128)S(1)}, u32[]{:S(2)}, u32[]{:S(2)}) collective-permute-start(f32[8,48,128]{2,1,0:T(8,128)S(1)} %get-tuple-element.118), channel_id=1, source_target_pairs={{0,1},{1,0},{2,3},{3,2},{4,5},{5,4},{6,7},{7,6},{8,9},{9,8},{10,11... | collective-permute-start | bytes 589832 | tf_op jit(solution)/shard_map/ppermute | solution.py:375
  83.0 12.4 %all_to_all.23.parts = f32[8,48,128]{2,1,0:T(8,128)S(1)} all-to-all(f32[8,48,128]{2,1,0:T(8,128)S(1)} %add.20), channel_id=1, replica_groups={{0,2,4,6,8,10,12,14},{1,3,5,7,9,11,13,15},{16,18,20,22,24,26,28,30},{17..., dimensions={0} | all-to-all | bytes 393216 | tf_op jit(solution)/shard_map/all_to_all | solution.py:382
  95.7 1.5 %collective-permute-start.14 = (f32[64,128]{1,0:T(8,128)S(1)}, f32[64,128]{1,0:T(8,128)S(1)}, u32[]{:S(2)}, u32[]{:S(2)}) collective-permute-start(f32[64,128]{1,0:T(8,128)S(1)} %get-tuple-element.124), channel_id=1, source_target_pairs={{0,1},{1,0},{2,3},{3,2},{4,5},{5,4},{6,7},{7,6},{8,9},{9,8},{10,11... | collective-permute-start | bytes 98312 | tf_op jit(solution)/shard_map/ppermute | solution.py:352
  97.2 1.0 collective-permute-start.16
  98.2 1.1 collective-permute-start.17
  99.3 1.5 %reopen.1 = (f32[64,1024]{1,0:T(8,128)S(1)}, f32[64,1024]{1,0:T(8,128)S(1)}, f32[64,512]{1,0:T(8,128)S(1)}) custom-call(s32[8,4]{1,0:T(8,128)S(1)} %copy.17.columns, bf16[96,128]{1,0:T(8,128)(2,1)S(1)} %get-tuple-element.119.field, bf16[96,1024]{1,0:T(8,128)(2,1)S(1)} %get-tuple-element.80.modes, bf16[8,4,128,128]{3,2,1,0:T(8,128)(2,1)S(1)} %bitcast.27, ...), custom_call_target="tpu_custom_call" | custom-call | flops 1760000000 | bytes 1048576 | tf_op jit(solution)/shard_map/reopen/pallas_call | solution.py:284
  101.8 1.1 collective-permute-start.18
  102.9 1.0 collective-permute-start.19
  103.9 1.7 %collective-permute-start.20 = (f32[64,128]{1,0:T(8,128)S(1)}, f32[64,128]{1,0:T(8,128)S(1)}, u32[]{:S(2)}, u32[]{:S(2)}) collective-permute-start(f32[64,128]{1,0:T(8,128)S(1)} %get-tuple-element.133), channel_id=1, source_target_pairs={{0,16},{1,2},{2,1},{3,4},{4,3},{5,6},{6,5},{7,8},{8,7},{9,10},{10,... | collective-permute-start | bytes 98312 | tf_op jit(solution)/shard_map/ppermute | solution.py:354
  106.0 1.5 %middle.3 = (f32[64,1024]{1,0:T(8,128)S(1)}, f32[64,512]{1,0:T(8,128)S(1)}) custom-call(s32[8,4]{1,0:T(8,128)S(1)} %copy.17.columns, bf16[8,4,128,128]{3,2,1,0:T(8,128)(2,1)S(1)} %bitcast.28, bf16[1024,512]{1,0:T(8,128)(2,1)S(1)} %get-tuple-element.92.pick, bf16[512,1024]{1,0:T(8,128)(2,1)S(1)} %get-tuple-element.100.place, ...), custom_call_target="tpu_custom_call" | custom-call | flops 1760000000 | bytes 1048576 | tf_op jit(solution)/shard_map/middle/pallas_call | solution.py:284
  108.5 2.4 %collective-permute-start.22 = (f32[64,128]{1,0:T(8,128)S(1)}, f32[64,128]{1,0:T(8,128)S(1)}, u32[]{:S(2)}, u32[]{:S(2)}) collective-permute-start(f32[64,128]{1,0:T(8,128)S(1)} %get-tuple-element.139), channel_id=1, source_target_pairs={{0,1},{1,0},{2,3},{3,2},{4,5},{5,4},{6,7},{7,6},{8,9},{9,8},{10,11... | collective-permute-start | bytes 98312 | tf_op jit(solution)/shard_map/ppermute | solution.py:352
  111.1 1.6 %collective-permute-start.24 = (f32[64,128]{1,0:T(8,128)S(1)}, f32[64,128]{1,0:T(8,128)S(1)}, u32[]{:S(2)}, u32[]{:S(2)}) collective-permute-start(f32[64,128]{1,0:T(8,128)S(1)} %get-tuple-element.141), channel_id=1, source_target_pairs={{0,16},{1,2},{2,1},{3,4},{4,3},{5,6},{6,5},{7,8},{8,7},{9,10},{10,... | collective-permute-start | bytes 98312 | tf_op jit(solution)/shard_map/ppermute | solution.py:354
  113.5 1.9 %finish_last.1 = (f32[64,1024]{1,0:T(8,128)}, f32[64,1024]{1,0:T(8,128)S(1)}) custom-call(s32[8,4]{1,0:T(8,128)S(1)} %copy.17.columns, bf16[8,4,128,128]{3,2,1,0:T(8,128)(2,1)S(1)} %bitcast.29, bf16[512,1024]{1,0:T(8,128)(2,1)S(1)} %get-tuple-element.100.place, f32[64,1024]{1,0:T(8,128)S(1)} %get-tuple-element.122.residual, ...), custom_call_target="tpu_custom_call" | custom-call | flops 1760000000 | bytes 1048576 | tf_op jit(solution)/shard_map/finish_last/pallas_call | solution.py:284
  115.4 1.7 %last.1 = f32[64,1024]{1,0:T(8,128)} custom-call(s32[4]{0:T(128)S(1)} %get-tuple-element.87.inside, f32[64,128]{1,0:T(8,128)S(1)} %collective-permute-done.22.l0, f32[64,128]{1,0:T(8,128)S(1)} %collective-permute-done.23.l1, f32[64,128]{1,0:T(8,128)S(1)} %collective-permute-done.24.l2, f32[64,128]{1,0:T(8,128)S(1)} %collective-permute-done.25.l3, ...), custom_call_target="tpu_custom_call" | custom-call | flops 990000000 | bytes 1048576 | tf_op jit(solution)/shard_map/last/pallas_call | solution.py:284
  (72 shorter events, 11.7 us)
Async XLA Ops:
  0.7 18.3 %copy-start = (bf16[1536,1536]{1,0:T(8,128)(2,1)S(1)}, bf16[1536,1536]{1,0:T(8,128)(2,1)}, u32[]{:S(2)}) copy-start(bf16[1536,1536]{1,0:T(8,128)(2,1)} %inverse.7) | copy-start | bytes 14155780
  19.9 3.8 %collective-permute-start = (f32[8,48,128]{2,1,0:T(8,128)S(1)}, f32[8,48,128]{2,1,0:T(8,128)S(1)}, u32[]{:S(2)}, u32[]{:S(2)}) collective-permute-start(f32[8,48,128]{2,1,0:T(8,128)S(1)} %get-tuple-element.78), channel_id=1, source_target_pairs={{0,1},{1,0},{2,3},{3,2},{4,5},{5,4},{6,7},{7,6},{8,9},{9,8},{10,11... | collective-permute-start | bytes 589832 | tf_op jit(solution)/shard_map/ppermute | solution.py:375
  22.7 20.3 %copy-start.7 = (s32[1,1,8,4]{2,3,1,0:T(4,128)S(1)}, s32[1,1,8,4]{2,3,1,0:T(4,128)}, u32[]{:S(2)}) copy-start(s32[1,1,8,4]{2,3,1,0:T(4,128)} %param.14) | copy-start | bytes 388
  22.7 23.1 %copy-start.1 = (bf16[1,1,8,4,128,128]{5,4,3,2,1,0:T(8,128)(2,1)S(1)}, bf16[1,1,8,4,128,128]{5,4,3,2,1,0:T(8,128)(2,1)}, u32[]{:S(2)}) copy-start(bf16[1,1,8,4,128,128]{5,4,3,2,1,0:T(8,128)(2,1)} %param.13) | copy-start | bytes 3145732
  42.6 4.7 %copy-start.6 = (s32[1,1,4,128]{3,2,1,0:T(4,128)S(1)}, s32[1,1,4,128]{3,2,1,0:T(4,128)}, u32[]{:S(2)}) copy-start(s32[1,1,4,128]{3,2,1,0:T(4,128)} %param.17) | copy-start | bytes 6148
  43.0 5.3 %collective-permute-start.1 = (f32[64,128]{1,0:T(8,128)S(1)}, f32[64,128]{1,0:T(8,128)S(1)}, u32[]{:S(2)}, u32[]{:S(2)}) collective-permute-start(f32[64,128]{1,0:T(8,128)S(1)} %get-tuple-element.88), channel_id=1, source_target_pairs={{0,1},{1,0},{2,3},{3,2},{4,5},{5,4},{6,7},{7,6},{8,9},{9,8},{10,11... | collective-permute-start | bytes 98312 | tf_op jit(solution)/shard_map/ppermute | solution.py:352
  43.7 4.6 %collective-permute-start.2 = (f32[64,128]{1,0:T(8,128)S(1)}, f32[64,128]{1,0:T(8,128)S(1)}, u32[]{:S(2)}, u32[]{:S(2)}) collective-permute-start(f32[64,128]{1,0:T(8,128)S(1)} %get-tuple-element.89), channel_id=1, source_target_pairs={{0,16},{16,0},{32,48},{48,32},{64,80},{80,64},{96,112},{112,96},{1... | collective-permute-start | bytes 98312 | tf_op jit(solution)/shard_map/ppermute | solution.py:353
  43.7 4.6 %collective-permute-start.3 = (f32[64,128]{1,0:T(8,128)S(1)}, f32[64,128]{1,0:T(8,128)S(1)}, u32[]{:S(2)}, u32[]{:S(2)}) collective-permute-start(f32[64,128]{1,0:T(8,128)S(1)} %get-tuple-element.90), channel_id=1, source_target_pairs={{0,16},{1,2},{2,1},{3,4},{4,3},{5,6},{6,5},{7,8},{8,7},{9,10},{10,... | collective-permute-start | bytes 98312 | tf_op jit(solution)/shard_map/ppermute | solution.py:354
  44.7 3.7 %collective-permute-start.4 = (f32[64,128]{1,0:T(8,128)S(1)}, f32[64,128]{1,0:T(8,128)S(1)}, u32[]{:S(2)}, u32[]{:S(2)}) collective-permute-start(f32[64,128]{1,0:T(8,128)S(1)} %get-tuple-element.91), channel_id=1, source_target_pairs={{0,1},{1,0},{2,3},{3,2},{4,5},{5,4},{6,7},{7,6},{8,9},{9,8},{10,11... | collective-permute-start | bytes 98312 | tf_op jit(solution)/shard_map/ppermute | solution.py:355
  49.3 6.0 %collective-permute-start.5 = (f32[64,128]{1,0:T(8,128)S(1)}, f32[64,128]{1,0:T(8,128)S(1)}, u32[]{:S(2)}, u32[]{:S(2)}) collective-permute-start(f32[64,128]{1,0:T(8,128)S(1)} %get-tuple-element.101), channel_id=1, source_target_pairs={{0,1},{1,0},{2,3},{3,2},{4,5},{5,4},{6,7},{7,6},{8,9},{9,8},{10,11... | collective-permute-start | bytes 98312 | tf_op jit(solution)/shard_map/ppermute | solution.py:352
  49.4 5.9 %collective-permute-start.6 = (f32[64,128]{1,0:T(8,128)S(1)}, f32[64,128]{1,0:T(8,128)S(1)}, u32[]{:S(2)}, u32[]{:S(2)}) collective-permute-start(f32[64,128]{1,0:T(8,128)S(1)} %get-tuple-element.102), channel_id=1, source_target_pairs={{0,16},{16,0},{32,48},{48,32},{64,80},{80,64},{96,112},{112,96},{1... | collective-permute-start | bytes 98312 | tf_op jit(solution)/shard_map/ppermute | solution.py:353
  51.3 4.0 %collective-permute-start.7 = (f32[64,128]{1,0:T(8,128)S(1)}, f32[64,128]{1,0:T(8,128)S(1)}, u32[]{:S(2)}, u32[]{:S(2)}) collective-permute-start(f32[64,128]{1,0:T(8,128)S(1)} %get-tuple-element.103), channel_id=1, source_target_pairs={{0,16},{1,2},{2,1},{3,4},{4,3},{5,6},{6,5},{7,8},{8,7},{9,10},{10,... | collective-permute-start | bytes 98312 | tf_op jit(solution)/shard_map/ppermute | solution.py:354
  52.1 3.2 %collective-permute-start.8 = (f32[64,128]{1,0:T(8,128)S(1)}, f32[64,128]{1,0:T(8,128)S(1)}, u32[]{:S(2)}, u32[]{:S(2)}) collective-permute-start(f32[64,128]{1,0:T(8,128)S(1)} %get-tuple-element.104), channel_id=1, source_target_pairs={{0,1},{1,0},{2,3},{3,2},{4,5},{5,4},{6,7},{7,6},{8,9},{9,8},{10,11... | collective-permute-start | bytes 98312 | tf_op jit(solution)/shard_map/ppermute | solution.py:355
  56.2 5.8 %collective-permute-start.9 = (f32[64,128]{1,0:T(8,128)S(1)}, f32[64,128]{1,0:T(8,128)S(1)}, u32[]{:S(2)}, u32[]{:S(2)}) collective-permute-start(f32[64,128]{1,0:T(8,128)S(1)} %get-tuple-element.108), channel_id=1, source_target_pairs={{0,1},{1,0},{2,3},{3,2},{4,5},{5,4},{6,7},{7,6},{8,9},{9,8},{10,11... | collective-permute-start | bytes 98312 | tf_op jit(solution)/shard_map/ppermute | solution.py:352
  57.4 4.6 %collective-permute-start.10 = (f32[64,128]{1,0:T(8,128)S(1)}, f32[64,128]{1,0:T(8,128)S(1)}, u32[]{:S(2)}, u32[]{:S(2)}) collective-permute-start(f32[64,128]{1,0:T(8,128)S(1)} %get-tuple-element.109), channel_id=1, source_target_pairs={{0,16},{16,0},{32,48},{48,32},{64,80},{80,64},{96,112},{112,96},{1... | collective-permute-start | bytes 98312 | tf_op jit(solution)/shard_map/ppermute | solution.py:353
  58.7 3.4 %collective-permute-start.11 = (f32[64,128]{1,0:T(8,128)S(1)}, f32[64,128]{1,0:T(8,128)S(1)}, u32[]{:S(2)}, u32[]{:S(2)}) collective-permute-start(f32[64,128]{1,0:T(8,128)S(1)} %get-tuple-element.110), channel_id=1, source_target_pairs={{0,16},{1,2},{2,1},{3,4},{4,3},{5,6},{6,5},{7,8},{8,7},{9,10},{10,... | collective-permute-start | bytes 98312 | tf_op jit(solution)/shard_map/ppermute | solution.py:354
  60.4 1.7 %collective-permute-start.12 = (f32[64,128]{1,0:T(8,128)S(1)}, f32[64,128]{1,0:T(8,128)S(1)}, u32[]{:S(2)}, u32[]{:S(2)}) collective-permute-start(f32[64,128]{1,0:T(8,128)S(1)} %get-tuple-element.111), channel_id=1, source_target_pairs={{0,1},{1,0},{2,3},{3,2},{4,5},{5,4},{6,7},{7,6},{8,9},{9,8},{10,11... | collective-permute-start | bytes 98312 | tf_op jit(solution)/shard_map/ppermute | solution.py:355
  60.4 18.2 %slice-start = ((s8[4718592]{0:T(1024)(128)(4,1)}), s8[4194304]{0:T(1024)(128)(4,1)S(1)}, s32[]{:S(2)}) async-start(s8[4718592]{0:T(1024)(128)(4,1)} %bitcast.21), calls=%async_computation.4 | async-start | bytes 8388608
  60.4 18.2 %slice-start.1 = ((s8[4718592]{0:T(1024)(128)(4,1)}), s8[524288]{0:T(1024)(128)(4,1)S(1)}, s32[]{:S(2)}) async-start(s8[4718592]{0:T(1024)(128)(4,1)} %bitcast.21), calls=%async_computation.5 | async-start | bytes 1048576
  79.5 3.4 %collective-permute-start.13 = (f32[8,48,128]{2,1,0:T(8,128)S(1)}, f32[8,48,128]{2,1,0:T(8,128)S(1)}, u32[]{:S(2)}, u32[]{:S(2)}) collective-permute-start(f32[8,48,128]{2,1,0:T(8,128)S(1)} %get-tuple-element.118), channel_id=1, source_target_pairs={{0,1},{1,0},{2,3},{3,2},{4,5},{5,4},{6,7},{7,6},{8,9},{9,8},{10,11... | collective-permute-start | bytes 589832 | tf_op jit(solution)/shard_map/ppermute | solution.py:375
  95.7 5.2 %collective-permute-start.14 = (f32[64,128]{1,0:T(8,128)S(1)}, f32[64,128]{1,0:T(8,128)S(1)}, u32[]{:S(2)}, u32[]{:S(2)}) collective-permute-start(f32[64,128]{1,0:T(8,128)S(1)} %get-tuple-element.124), channel_id=1, source_target_pairs={{0,1},{1,0},{2,3},{3,2},{4,5},{5,4},{6,7},{7,6},{8,9},{9,8},{10,11... | collective-permute-start | bytes 98312 | tf_op jit(solution)/shard_map/ppermute | solution.py:352
  97.2 3.7 %collective-permute-start.15 = (f32[64,128]{1,0:T(8,128)S(1)}, f32[64,128]{1,0:T(8,128)S(1)}, u32[]{:S(2)}, u32[]{:S(2)}) collective-permute-start(f32[64,128]{1,0:T(8,128)S(1)} %get-tuple-element.125), channel_id=1, source_target_pairs={{0,16},{16,0},{32,48},{48,32},{64,80},{80,64},{96,112},{112,96},{1... | collective-permute-start | bytes 98312 | tf_op jit(solution)/shard_map/ppermute | solution.py:353
  97.2 3.7 %collective-permute-start.16 = (f32[64,128]{1,0:T(8,128)S(1)}, f32[64,128]{1,0:T(8,128)S(1)}, u32[]{:S(2)}, u32[]{:S(2)}) collective-permute-start(f32[64,128]{1,0:T(8,128)S(1)} %get-tuple-element.126), channel_id=1, source_target_pairs={{0,16},{1,2},{2,1},{3,4},{4,3},{5,6},{6,5},{7,8},{8,7},{9,10},{10,... | collective-permute-start | bytes 98312 | tf_op jit(solution)/shard_map/ppermute | solution.py:354
  98.2 2.7 %collective-permute-start.17 = (f32[64,128]{1,0:T(8,128)S(1)}, f32[64,128]{1,0:T(8,128)S(1)}, u32[]{:S(2)}, u32[]{:S(2)}) collective-permute-start(f32[64,128]{1,0:T(8,128)S(1)} %get-tuple-element.127), channel_id=1, source_target_pairs={{0,1},{1,0},{2,3},{3,2},{4,5},{5,4},{6,7},{7,6},{8,9},{9,8},{10,11... | collective-permute-start | bytes 98312 | tf_op jit(solution)/shard_map/ppermute | solution.py:355
  101.8 5.7 %collective-permute-start.18 = (f32[64,128]{1,0:T(8,128)S(1)}, f32[64,128]{1,0:T(8,128)S(1)}, u32[]{:S(2)}, u32[]{:S(2)}) collective-permute-start(f32[64,128]{1,0:T(8,128)S(1)} %get-tuple-element.131), channel_id=1, source_target_pairs={{0,1},{1,0},{2,3},{3,2},{4,5},{5,4},{6,7},{7,6},{8,9},{9,8},{10,11... | collective-permute-start | bytes 98312 | tf_op jit(solution)/shard_map/ppermute | solution.py:352
  102.9 4.7 %collective-permute-start.19 = (f32[64,128]{1,0:T(8,128)S(1)}, f32[64,128]{1,0:T(8,128)S(1)}, u32[]{:S(2)}, u32[]{:S(2)}) collective-permute-start(f32[64,128]{1,0:T(8,128)S(1)} %get-tuple-element.132), channel_id=1, source_target_pairs={{0,16},{16,0},{32,48},{48,32},{64,80},{80,64},{96,112},{112,96},{1... | collective-permute-start | bytes 98312 | tf_op jit(solution)/shard_map/ppermute | solution.py:353
  103.9 3.7 %collective-permute-start.20 = (f32[64,128]{1,0:T(8,128)S(1)}, f32[64,128]{1,0:T(8,128)S(1)}, u32[]{:S(2)}, u32[]{:S(2)}) collective-permute-start(f32[64,128]{1,0:T(8,128)S(1)} %get-tuple-element.133), channel_id=1, source_target_pairs={{0,16},{1,2},{2,1},{3,4},{4,3},{5,6},{6,5},{7,8},{8,7},{9,10},{10,... | collective-permute-start | bytes 98312 | tf_op jit(solution)/shard_map/ppermute | solution.py:354
  105.6 2.0 %collective-permute-start.21 = (f32[64,128]{1,0:T(8,128)S(1)}, f32[64,128]{1,0:T(8,128)S(1)}, u32[]{:S(2)}, u32[]{:S(2)}) collective-permute-start(f32[64,128]{1,0:T(8,128)S(1)} %get-tuple-element.134), channel_id=1, source_target_pairs={{0,1},{1,0},{2,3},{3,2},{4,5},{5,4},{6,7},{7,6},{8,9},{9,8},{10,11... | collective-permute-start | bytes 98312 | tf_op jit(solution)/shard_map/ppermute | solution.py:355
  108.5 6.9 %collective-permute-start.22 = (f32[64,128]{1,0:T(8,128)S(1)}, f32[64,128]{1,0:T(8,128)S(1)}, u32[]{:S(2)}, u32[]{:S(2)}) collective-permute-start(f32[64,128]{1,0:T(8,128)S(1)} %get-tuple-element.139), channel_id=1, source_target_pairs={{0,1},{1,0},{2,3},{3,2},{4,5},{5,4},{6,7},{7,6},{8,9},{9,8},{10,11... | collective-permute-start | bytes 98312 | tf_op jit(solution)/shard_map/ppermute | solution.py:352
  110.9 4.5 %collective-permute-start.23 = (f32[64,128]{1,0:T(8,128)S(1)}, f32[64,128]{1,0:T(8,128)S(1)}, u32[]{:S(2)}, u32[]{:S(2)}) collective-permute-start(f32[64,128]{1,0:T(8,128)S(1)} %get-tuple-element.140), channel_id=1, source_target_pairs={{0,16},{16,0},{32,48},{48,32},{64,80},{80,64},{96,112},{112,96},{1... | collective-permute-start | bytes 98312 | tf_op jit(solution)/shard_map/ppermute | solution.py:353
  111.1 4.3 %collective-permute-start.24 = (f32[64,128]{1,0:T(8,128)S(1)}, f32[64,128]{1,0:T(8,128)S(1)}, u32[]{:S(2)}, u32[]{:S(2)}) collective-permute-start(f32[64,128]{1,0:T(8,128)S(1)} %get-tuple-element.141), channel_id=1, source_target_pairs={{0,16},{1,2},{2,1},{3,4},{4,3},{5,6},{6,5},{7,8},{8,7},{9,10},{10,... | collective-permute-start | bytes 98312 | tf_op jit(solution)/shard_map/ppermute | solution.py:354
  112.7 2.7 %collective-permute-start.25 = (f32[64,128]{1,0:T(8,128)S(1)}, f32[64,128]{1,0:T(8,128)S(1)}, u32[]{:S(2)}, u32[]{:S(2)}) collective-permute-start(f32[64,128]{1,0:T(8,128)S(1)} %get-tuple-element.142), channel_id=1, source_target_pairs={{0,1},{1,0},{2,3},{3,2},{4,5},{5,4},{6,7},{7,6},{8,9},{9,8},{10,11... | collective-permute-start | bytes 98312 | tf_op jit(solution)/shard_map/ppermute | solution.py:355
  (4 other events, 17.7 us)
